TPU v7x, 32 devices: a whole 2x2x4 slice. The times are simulated.
32 devices in a mesh: ep: 8 (over z, y), tp: 4 (over x, core).
Axes of the slice: x: 2, y: 2, z: 4, core: 2. Of those that a mesh axis runs over, the one named last changes fastest.
Arguments:
- tokens: bfloat16 [16384, 1536], P(('ep', 'tp')), may hold values from -6 to 6
- norm1_gain: float32 [1536], replicated, may hold values from 0.5 to 1.5
- w_query: bfloat16 [1536, 1536], P(None, 'tp'), may hold values from -0.21875 to 0.21875
- key_weight: bfloat16 [1536, 512], P(None, 'tp'), may hold values from -0.21875 to 0.21875
- value_weight: bfloat16 [1536, 512], P(None, 'tp'), may hold values from -0.15625 to 0.15625
- w_out: bfloat16 [1536, 1536], P('tp'), may hold values from -1.25 to 1.25
- norm2_gain: float32 [1536], replicated, may hold values from 0.5 to 1.5
- w_router: bfloat16 [1536, 8], replicated, may hold values from -0.078125 to 0.078125
- w_gate: bfloat16 [8, 1536, 512], P('ep'), may hold values from -0.15625 to 0.15625
- w_up: bfloat16 [8, 1536, 512], P('ep'), may hold values from -0.15625 to 0.15625
- w_down: bfloat16 [8, 512, 1536], P('ep'), may hold values from -3 to 3
- routes: int32 [16384, 4], P(('ep', 'tp')), may hold values from 0 to 7, all different within a row; in each aligned block of 512 rows (0 to 511, 512 to 1023, ...) at most 384 rows name the same one
- piece_first_position: int32 [8, 4], P('ep'), may hold values from 0 to 1984, as said below
- piece_length: int32 [8, 4], P('ep'), may hold values from 64 to 256
- grad_out: bfloat16 [16384, 1536], P(('ep', 'tp')), may hold values from -6 to 6
Outputs:
- output: float32 [16384, 1536], P(('ep', 'tp'))
- grad_input: float32 [16384, 1536], P(('ep', 'tp'))
- grad_norm1: float32 [1536], P(('ep', 'tp'))
- grad_query: float32 [1536, 1536], P('ep', 'tp')
- grad_key: float32 [1536, 512], P('ep', 'tp')
- grad_value: float32 [1536, 512], P('ep', 'tp')
- grad_outproj: float32 [1536, 1536], P('tp', 'ep')
- grad_norm2: float32 [1536], P(('ep', 'tp'))
- grad_router: float32 [1536, 8], P(('ep', 'tp'))
- grad_gate: float32 [8, 1536, 512], P('ep', 'tp')
- grad_up: float32 [8, 1536, 512], P('ep', 'tp')
- grad_down: float32 [8, 512, 1536], P('ep', None, 'tp')
Inputs may be any that keep to these rules, and one draw needn't show every extreme that they name: `routes`: each row names 4 different experts; within the rows of one device (aligned blocks of 512 rows) no expert is named by more than 384 rows. `piece_first_position`: piece j of a sequence lies within positions j * 512 to (j + 1) * 512 - 1.
All inputs are finite; a program needn't handle non-finite values.
Results may differ from a plain program's by a relative error of at most 0.023.
Values may be sent and summed in bfloat16 or wider, within the bound.
No kernel may reach another device: no remote copies, remote signals or barrier semaphores. Data moves between devices by JAX's collectives and lax.ppermute only.
A program may use at most 256 MiB of HBM per device.

v0:
```python
import math

import jax
import jax.numpy as jnp
from jax import lax
from jax.sharding import PartitionSpec as P

HEAD_SIZE = 64
SEQUENCE_LENGTH = 2048


EPSILON = 1e-05
ROPE_BASE = 10000.0
MASK_FILL = -1e30


def rms_norm(values_in, gain_vec):
    return (
        values_in
        * lax.rsqrt(jnp.mean(values_in * values_in, axis=-1, keepdims=True) + EPSILON)
        * gain_vec
    )


def rope_tables(positions):
    half_width = HEAD_SIZE // 2
    exponent = jnp.arange(half_width, dtype=jnp.float32) * (2.0 / HEAD_SIZE)
    frequency = ROPE_BASE ** (-exponent)
    angles = positions.astype(jnp.float32)[:, None] * frequency[None, :]
    return (jnp.cos(angles)[:, None, :], jnp.sin(angles)[:, None, :])


def apply_rotary(values_in, rotary_cosine, rotary_sine):
    half_width = values_in.shape[-1] // 2
    first_half = values_in[..., :half_width]
    second_half = values_in[..., half_width:]
    return jnp.concatenate(
        [
            first_half * rotary_cosine - second_half * rotary_sine,
            second_half * rotary_cosine + first_half * rotary_sine,
        ],
        axis=-1,
    )


def rotate_back(values_in, rotary_cosine, rotary_sine):
    half_width = values_in.shape[-1] // 2
    first_half = values_in[..., :half_width]
    second_half = values_in[..., half_width:]
    return jnp.concatenate(
        [
            first_half * rotary_cosine + second_half * rotary_sine,
            second_half * rotary_cosine - first_half * rotary_sine,
        ],
        axis=-1,
    )


def piece_labels(starts_row, lengths_row, length_all):
    positions = jnp.arange(length_all, dtype=jnp.int32)
    inside = (positions[:, None] >= starts_row[None, :]) & (
        positions[:, None] < (starts_row + lengths_row)[None, :]
    )
    labels = jnp.arange(1, starts_row.shape[0] + 1, dtype=jnp.int32)
    return jnp.sum(jnp.where(inside, labels[None, :], 0), axis=1) - 1


def allowed_pairs(query_pos, query_label, key_label):
    key_pos = jnp.arange(key_label.shape[0], dtype=jnp.int32)
    causal = key_pos[None, :] <= query_pos[:, None]
    same_piece = (query_label[:, None] == key_label[None, :]) & (query_label[:, None] >= 0)
    return causal | same_piece


def body(
    tokens,
    norm1_gain,
    w_query,
    key_weight,
    value_weight,
    w_out,
    norm2_gain,
    w_router,
    w_gate,
    w_up,
    w_down,
    routes,
    piece_first_position,
    piece_length,
    grad_out,
):
    row_count = tokens.shape[0]
    feature_width = tokens.shape[1]
    inputs = tokens.astype(jnp.float32)
    normed_one, norm_one_back = jax.vjp(rms_norm, inputs, norm1_gain)
    first_low = normed_one.astype(jnp.bfloat16)
    first_all = lax.all_gather(first_low, "tp", axis=0, tiled=True)
    group_rows = first_all.shape[0]
    query_cols = w_query.shape[1]
    kv_cols = key_weight.shape[1]
    head_local = query_cols // HEAD_SIZE
    kv_local = kv_cols // HEAD_SIZE
    query_group_width = head_local // kv_local
    score_scale = 1.0 / math.sqrt(HEAD_SIZE)
    rows_per_block = min(512, SEQUENCE_LENGTH)
    block_total = group_rows // rows_per_block
    blocks_per_seq = SEQUENCE_LENGTH // rows_per_block
    query_lin = jnp.dot(first_all, w_query, preferred_element_type=jnp.float32)
    key_linear = jnp.dot(first_all, key_weight, preferred_element_type=jnp.float32)
    value_lin = jnp.dot(first_all, value_weight, preferred_element_type=jnp.float32)
    positions = jnp.arange(group_rows, dtype=jnp.int32) % SEQUENCE_LENGTH
    rotary_cosine, rotary_sine = rope_tables(positions)
    query_low = apply_rotary(
        query_lin.reshape(group_rows, head_local, HEAD_SIZE), rotary_cosine, rotary_sine
    ).astype(jnp.bfloat16)
    query_low = query_low.reshape(group_rows, kv_local, query_group_width, HEAD_SIZE)
    key_low = apply_rotary(
        key_linear.reshape(group_rows, kv_local, HEAD_SIZE), rotary_cosine, rotary_sine
    ).astype(jnp.bfloat16)
    value_low = value_lin.astype(jnp.bfloat16).reshape(group_rows, kv_local, HEAD_SIZE)

    def block_scores(block_index):
        query_start = block_index * rows_per_block
        sequence = query_start // SEQUENCE_LENGTH
        key_start = sequence * SEQUENCE_LENGTH
        query_block = lax.dynamic_slice_in_dim(query_low, query_start, rows_per_block, 0)
        starts_row = lax.dynamic_index_in_dim(piece_first_position, sequence, 0, keepdims=False)
        lengths_row = lax.dynamic_index_in_dim(piece_length, sequence, 0, keepdims=False)
        label_seq = piece_labels(starts_row, lengths_row, SEQUENCE_LENGTH)
        query_pos = query_start - key_start + jnp.arange(rows_per_block, dtype=jnp.int32)
        query_label = lax.dynamic_slice_in_dim(
            label_seq, query_start - key_start, rows_per_block, 0
        )
        allowed = allowed_pairs(query_pos, query_label, label_seq)
        scores = (
            jnp.einsum("qhgd,khd->hgqk", query_block, key_low, preferred_element_type=jnp.float32)
            * score_scale
        )
        scores = jnp.where(allowed[None, None], scores, MASK_FILL)
        return (scores, query_block, key_low, value_low)

    def forward_block(block_index):
        scores, query_block, key_block, value_block = block_scores(block_index)
        row_peak = jnp.max(scores, axis=-1, keepdims=True)
        log_total = row_peak + jnp.log(jnp.sum(jnp.exp(scores - row_peak), axis=-1, keepdims=True))
        weights = jnp.exp(scores - log_total).astype(jnp.bfloat16)
        attended = jnp.einsum(
            "hgqk,khd->qhgd", weights, value_block, preferred_element_type=jnp.float32
        )
        return (attended.reshape(rows_per_block, query_cols), log_total)

    attended_blocks, log_totals = lax.map(forward_block, jnp.arange(block_total, dtype=jnp.int32))
    attended_low = attended_blocks.reshape(group_rows, query_cols).astype(jnp.bfloat16)
    attn_out = lax.psum_scatter(
        jnp.dot(attended_low, w_out, preferred_element_type=jnp.float32),
        "tp",
        scatter_dimension=0,
        tiled=True,
    )
    middle = inputs + attn_out
    normed_two, norm_two_back = jax.vjp(rms_norm, middle, norm2_gain)
    second_low = normed_two.astype(jnp.bfloat16)
    logits = jnp.dot(second_low, w_router, preferred_element_type=jnp.float32)
    router_probs = jax.nn.softmax(logits, axis=-1)
    expert_count = w_router.shape[1]
    top_count = routes.shape[1]
    capacity = 3 * row_count * top_count // (2 * expert_count)
    chosen = routes[:, :, None] == jnp.arange(expert_count, dtype=jnp.int32)[None, None, :]
    gate_probs = jnp.sum(jnp.where(chosen, router_probs[:, None, :], 0.0), axis=-1)
    chosen_flat = chosen.reshape(row_count * top_count, expert_count).astype(jnp.int32)
    earlier = jnp.cumsum(chosen_flat, axis=0) - chosen_flat
    slot_rank = jnp.sum(earlier * chosen_flat, axis=1)
    slot_index = routes.reshape(-1) * capacity + slot_rank
    route_token = jnp.arange(row_count * top_count, dtype=jnp.int32) // top_count
    slot_token = (
        jnp.full((expert_count * capacity,), row_count, jnp.int32).at[slot_index].set(route_token)
    )
    padded_rows = jnp.concatenate([second_low, jnp.zeros((1, feature_width), jnp.bfloat16)], axis=0)
    send_rows = padded_rows[slot_token].reshape(expert_count, capacity, feature_width)
    recv_rows = lax.all_to_all(send_rows, "ep", split_axis=0, concat_axis=1, tiled=True)
    gate_pre = jnp.einsum("erd,edf->erf", recv_rows, w_gate, preferred_element_type=jnp.float32)
    up_pre = jnp.einsum("erd,edf->erf", recv_rows, w_up, preferred_element_type=jnp.float32)
    gate_sig = jax.nn.sigmoid(gate_pre)
    gate_act = gate_pre * gate_sig
    activation = (gate_act * up_pre).astype(jnp.bfloat16)
    expert_out = jnp.einsum(
        "erf,efd->erd", activation, w_down, preferred_element_type=jnp.float32
    ).astype(jnp.bfloat16)
    returned = lax.all_to_all(expert_out, "ep", split_axis=1, concat_axis=0, tiled=True)
    routed = returned.reshape(expert_count * capacity, feature_width)[slot_index]
    routed = routed.reshape(row_count, top_count, feature_width)
    mixed_out = jnp.einsum("rk,rkd->rd", gate_probs, routed, preferred_element_type=jnp.float32)
    output = middle + mixed_out
    upstream = grad_out.astype(jnp.float32)
    gate_grad = jnp.einsum("rd,rkd->rk", upstream, routed, preferred_element_type=jnp.float32)
    slot_gate = (
        jnp.zeros((expert_count * capacity,), jnp.float32)
        .at[slot_index]
        .set(gate_probs.reshape(-1))
    )
    padded_grad = jnp.concatenate([upstream, jnp.zeros((1, feature_width), jnp.float32)], axis=0)
    send_grad = (padded_grad[slot_token] * slot_gate[:, None]).astype(jnp.bfloat16)
    send_grad = send_grad.reshape(expert_count, capacity, feature_width)
    recv_grad = lax.all_to_all(send_grad, "ep", split_axis=0, concat_axis=1, tiled=True)
    down_part = jnp.einsum(
        "erf,erd->efd", activation, recv_grad, preferred_element_type=jnp.float32
    )
    act_grad = jnp.einsum("erd,efd->erf", recv_grad, w_down, preferred_element_type=jnp.float32)
    gate_pre_grad = (act_grad * up_pre * gate_sig * (1.0 + gate_pre * (1.0 - gate_sig))).astype(
        jnp.bfloat16
    )
    up_pre_grad = (act_grad * gate_act).astype(jnp.bfloat16)
    gate_part = jnp.einsum(
        "erd,erf->edf", recv_rows, gate_pre_grad, preferred_element_type=jnp.float32
    )
    up_part = jnp.einsum("erd,erf->edf", recv_rows, up_pre_grad, preferred_element_type=jnp.float32)
    rows_grad = jnp.einsum(
        "erf,edf->erd", gate_pre_grad, w_gate, preferred_element_type=jnp.float32
    ) + jnp.einsum("erf,edf->erd", up_pre_grad, w_up, preferred_element_type=jnp.float32)
    returned_grad = lax.all_to_all(
        rows_grad.astype(jnp.bfloat16), "ep", split_axis=1, concat_axis=0, tiled=True
    )
    routed_grad = returned_grad.reshape(expert_count * capacity, feature_width)[slot_index]
    routed_grad = routed_grad.reshape(row_count, top_count, feature_width)
    second_from_routes = jnp.sum(routed_grad.astype(jnp.float32), axis=1)
    probs_grad = jnp.sum(jnp.where(chosen, gate_grad[:, :, None], 0.0), axis=1)
    logits_grad = (
        router_probs * (probs_grad - jnp.sum(router_probs * probs_grad, axis=-1, keepdims=True))
    ).astype(jnp.bfloat16)
    router_part = jnp.einsum(
        "rd,re->de", second_low, logits_grad, preferred_element_type=jnp.float32
    )
    second_grad = (
        jnp.einsum("re,de->rd", logits_grad, w_router, preferred_element_type=jnp.float32)
        + second_from_routes
    )
    middle_part, gain_two_part = norm_two_back(second_grad)
    middle_grad = upstream + middle_part
    attn_grad_low = middle_grad.astype(jnp.bfloat16)
    attn_grad_all = lax.all_gather(attn_grad_low, "tp", axis=0, tiled=True)
    attended_grad = jnp.einsum(
        "td,cd->tc", attn_grad_all, w_out, preferred_element_type=jnp.float32
    ).astype(jnp.bfloat16)
    outproj_part = jnp.einsum(
        "tc,td->cd", attended_low, attn_grad_all, preferred_element_type=jnp.float32
    )
    attended_split = attended_grad.reshape(group_rows, kv_local, query_group_width, HEAD_SIZE)

    def backward_block(block_index):
        scores, query_block, key_block, value_block = block_scores(block_index)
        log_total = lax.dynamic_index_in_dim(log_totals, block_index, 0, keepdims=False)
        weights = jnp.exp(scores - log_total)
        grad_block = lax.dynamic_slice_in_dim(
            attended_split, block_index * rows_per_block, rows_per_block, 0
        )
        weights_grad = jnp.einsum(
            "qhgd,khd->hgqk", grad_block, value_block, preferred_element_type=jnp.float32
        )
        centre = jnp.sum(weights * weights_grad, axis=-1, keepdims=True)
        scores_grad = (weights * (weights_grad - centre)).astype(jnp.bfloat16)
        query_grad = (
            jnp.einsum("hgqk,khd->qhgd", scores_grad, key_block, preferred_element_type=jnp.float32)
            * score_scale
        )
        key_grad = (
            jnp.einsum(
                "hgqk,qhgd->khd", scores_grad, query_block, preferred_element_type=jnp.float32
            )
            * score_scale
        )
        value_grad = jnp.einsum(
            "hgqk,qhgd->khd",
            weights.astype(jnp.bfloat16),
            grad_block,
            preferred_element_type=jnp.float32,
        )
        return (query_grad.reshape(rows_per_block, query_cols), key_grad, value_grad)

    query_grads, key_grads, value_grads = lax.map(
        backward_block, jnp.arange(block_total, dtype=jnp.int32)
    )
    seq_count = block_total // blocks_per_seq
    query_grad_all = query_grads.reshape(group_rows, head_local, HEAD_SIZE)
    key_grad_all = jnp.sum(
        key_grads.reshape(seq_count, blocks_per_seq, SEQUENCE_LENGTH, kv_local, HEAD_SIZE), axis=1
    )
    key_grad_all = key_grad_all.reshape(group_rows, kv_local, HEAD_SIZE)
    value_grad_all = jnp.sum(
        value_grads.reshape(seq_count, blocks_per_seq, SEQUENCE_LENGTH, kv_local, HEAD_SIZE), axis=1
    )
    query_lin_grad = (
        rotate_back(query_grad_all, rotary_cosine, rotary_sine)
        .reshape(group_rows, query_cols)
        .astype(jnp.bfloat16)
    )
    key_lin_grad = (
        rotate_back(key_grad_all, rotary_cosine, rotary_sine)
        .reshape(group_rows, kv_cols)
        .astype(jnp.bfloat16)
    )
    value_lin_grad = value_grad_all.reshape(group_rows, kv_cols).astype(jnp.bfloat16)
    query_part = jnp.einsum(
        "td,tc->dc", first_all, query_lin_grad, preferred_element_type=jnp.float32
    )
    key_part = jnp.einsum("td,tc->dc", first_all, key_lin_grad, preferred_element_type=jnp.float32)
    value_part = jnp.einsum(
        "td,tc->dc", first_all, value_lin_grad, preferred_element_type=jnp.float32
    )
    first_grad = lax.psum_scatter(
        (
            jnp.einsum("tc,dc->td", query_lin_grad, w_query, preferred_element_type=jnp.float32)
            + jnp.einsum("tc,dc->td", key_lin_grad, key_weight, preferred_element_type=jnp.float32)
            + jnp.einsum(
                "tc,dc->td", value_lin_grad, value_weight, preferred_element_type=jnp.float32
            )
        ).astype(jnp.bfloat16),
        "tp",
        scatter_dimension=0,
        tiled=True,
    ).astype(jnp.float32)
    input_part, gain_one_part = norm_one_back(first_grad)
    input_grad = middle_grad + input_part
    grad_query, grad_key, grad_value, grad_outproj = (
        lax.psum_scatter(
            query_part.astype(jnp.bfloat16), "ep", scatter_dimension=0, tiled=True
        ).astype(jnp.float32),
        lax.psum_scatter(
            key_part.astype(jnp.bfloat16), "ep", scatter_dimension=0, tiled=True
        ).astype(jnp.float32),
        lax.psum_scatter(
            value_part.astype(jnp.bfloat16), "ep", scatter_dimension=0, tiled=True
        ).astype(jnp.float32),
        lax.psum_scatter(
            outproj_part.astype(jnp.bfloat16), "ep", scatter_dimension=1, tiled=True
        ).astype(jnp.float32),
    )
    grad_gate, grad_up, grad_down = (
        lax.psum_scatter(
            gate_part.astype(jnp.bfloat16), "tp", scatter_dimension=1, tiled=True
        ).astype(jnp.float32),
        lax.psum_scatter(
            up_part.astype(jnp.bfloat16), "tp", scatter_dimension=1, tiled=True
        ).astype(jnp.float32),
        lax.psum_scatter(
            down_part.astype(jnp.bfloat16), "tp", scatter_dimension=2, tiled=True
        ).astype(jnp.float32),
    )
    grad_norm1, grad_norm2, grad_router = (
        lax.psum_scatter(gain_one_part, ("ep", "tp"), scatter_dimension=0, tiled=True),
        lax.psum_scatter(gain_two_part, ("ep", "tp"), scatter_dimension=0, tiled=True),
        lax.psum_scatter(router_part, ("ep", "tp"), scatter_dimension=0, tiled=True),
    )
    return (
        output,
        input_grad,
        grad_norm1,
        grad_query,
        grad_key,
        grad_value,
        grad_outproj,
        grad_norm2,
        grad_router,
        grad_gate,
        grad_up,
        grad_down,
    )


def solution(mesh):
    return jax.shard_map(
        body,
        mesh=mesh,
        in_specs=(
            P(("ep", "tp"), None),
            P(),
            P(None, "tp"),
            P(None, "tp"),
            P(None, "tp"),
            P("tp", None),
            P(),
            P(),
            P("ep", None, None),
            P("ep", None, None),
            P("ep", None, None),
            P(("ep", "tp"), None),
            P("ep", None),
            P("ep", None),
            P(("ep", "tp"), None),
        ),
        out_specs=(
            P(("ep", "tp"), None),
            P(("ep", "tp"), None),
            P(("ep", "tp")),
            P("ep", "tp"),
            P("ep", "tp"),
            P("ep", "tp"),
            P("tp", "ep"),
            P(("ep", "tp")),
            P(("ep", "tp"), None),
            P("ep", "tp", None),
            P("ep", "tp", None),
            P("ep", None, "tp"),
        ),
        check_vma=False,
    )
```

profile of v0, /device:TPU:2, one launch (start us, length us, event | category | flops | bytes accessed | tf_op | source)
XLA Modules:
  0.0 2531.6 jit_solution(3685132081366548018)
XLA Ops:
  13.4 45.5 %all-gather.3.cloned.1.call-done = bf16[2048,1536]{1,0:T(8,128)(2,1)} async-done(((bf16[512,1536]{1,0:T(8,128)(2,1)}), bf16[2048,1536]{1,0:T(8,128)(2,1)}) %all-gather.3.cloned.1.call-update) | async-done | bytes 6291472 | tf_op jit(solution)/shard_map/all_gather | solution.py:97
  70.9 157.0 %while.32 = (s32[]{:T(128)}, bf16[4,512,384]{2,1,0:T(8,128)(2,1)}, f32[4,2,3,512,1]{3,2,1,4,0:T(4,128)}, s32[4]{0:T(128)S(1)}, s32[1,4]{1,0:T(1,128)S(1)}, /*ind...) while((s32[]{:T(128)}, bf16[4,512,384]{2,1,0:T(8,128)(2,1)}, ...), condition=%wide.region_5.6_spmd, body=%wide.region_1.5_spmd.sunk | while | flops 1684051968 | bytes 83246568 | solution.py:152
  85.8 11.9 fusion.174
  250.5 86.7 %reduce-scatter.15.cloned.1.call-done = f32[512,1536]{1,0:T(8,128)} async-done(((f32[2048,1536]{1,0:T(8,128)}), f32[512,1536]{1,0:T(8,128)}) %reduce-scatter.15.cloned.1.call-update) | async-done | bytes 3145744 | tf_op jit(solution)/shard_map/reduce_scatter | solution.py:154
  342.9 14.7 gather_fusion
  357.6 211.6 %all_to_all.16 = bf16[8,384,1536]{2,1,0:T(8,128)(2,1)S(1)} all-to-all(bf16[8,384,1536]{2,1,0:T(8,128)(2,1)} %bitcast.308), channel_id=1, replica_groups=mesh['ep'=8,'tp'=4] {'ep'}, dimensions={0} | all-to-all | bytes 18874368 | tf_op jit(solution)/shard_map/all_to_all | solution.py:180
  587.8 103.8 %copy.111 = bf16[1,3072,1536]{2,0,1:T(2,128)(2,1)} copy(bf16[1,3072,1536]{2,1,0:T(8,128)(2,1)S(1)} %fusion.50) | data formatting | bytes 18874368 | tf_op jit(solution)/shard_map/convert_element_type | solution.py:188
  692.1 61.4 %reduce.6 = bf16[3072,1536]{1,0:T(8,128)(2,1)} reduce(bf16[3072,1,1536]{2,1,0:T(2,128)(2,1)} %bitcast.306, bf16[]{:T(256)} %broadcast.496), dimensions={1}, to_apply=%bitcast.240.reduce_sub_computation | reduce | bytes 18874370
  772.8 22.7 gather_fusion.2
  796.1 179.2 %all-to-all-done.1 = bf16[8,2,294912]{2,1,0:T(2,128)(2,1)} async-done(((bf16[8,2,294912]{2,1,0:T(2,128)(2,1)}), bf16[8,2,294912]{2,1,0:T(2,128)(2,1)}, u32[]{:S(2)}, u32[]{:S(2)}) %all-to-all-start.1) | async-done | bytes 9437216 | tf_op jit(solution)/shard_map/all_to_all | solution.py:189
  975.3 14.5 reshape.601
  989.8 14.3 copy.108
  1004.1 18.2 gather_fusion.1
  1057.6 209.2 %all_to_all.17 = bf16[8,384,1536]{2,1,0:T(8,128)(2,1)S(1)} all-to-all(bf16[8,384,1536]{2,1,0:T(8,128)(2,1)S(1)} %multiply_convert_fusion), channel_id=1, replica_groups=mesh['ep'=8,'tp'=4] {'ep'}, dimensions={0} | all-to-all | bytes 18874368 | tf_op jit(solution)/shard_map/all_to_all | solution.py:204
  1266.8 14.5 multiply_convert_fusion.1
  1290.5 12.4 fusion.51
  1303.0 17.4 copy.110
  1320.3 61.4 %reduce.7 = bf16[3072,1536]{1,0:T(8,128)(2,1)} reduce(bf16[3072,1,1536]{2,1,0:T(2,128)(2,1)} %bitcast.307, bf16[]{:T(256)} %broadcast.496), dimensions={1}, to_apply=%bitcast.239.reduce_sub_computation | reduce | bytes 18874370
  1381.8 12.2 reshape.602
  1399.1 204.4 %all-to-all-done.3 = bf16[8,2,294912]{2,1,0:T(2,128)(2,1)} async-done(((bf16[8,2,294912]{2,1,0:T(2,128)(2,1)}), bf16[8,2,294912]{2,1,0:T(2,128)(2,1)}, u32[]{:S(2)}, u32[]{:S(2)}) %all-to-all-start.3) | async-done | bytes 9437216 | tf_op jit(solution)/shard_map/all_to_all | solution.py:220
  1603.6 14.5 reshape.603
  1618.1 14.3 copy.107
  1632.4 18.2 gather_fusion.3
  1650.5 12.2 reshape.529
  1662.8 12.6 reduce_sum.204
  1736.5 407.5 %while.33 = (s32[]{:T(128)}, f32[4,512,384]{1,0,2:T(4,128)}, f32[4,2048,2,64]{1,3,2,0:T(8,128)}, f32[4,2048,2,64]{1,3,2,0:T(8,128)}, s32[4]{0:T(128)S(1)}, /*ind...) while((s32[]{:T(128)}, f32[4,512,384]{1,0,2:T(4,128)}, ...), condition=%wide.region_23.24_spmd, body=%wide.region_20.23_spmd.sunk | while | flops 4125595648 | bytes 202243632 | solution.py:279
  1753.5 12.8 fusion.189
  1766.2 17.3 fusion.186
  1783.6 21.4 fusion.187
  1822.3 16.0 dynamic_update_slice.51
  1855.2 12.7 fusion.189
  1867.8 17.9 fusion.186
  1885.7 22.3 fusion.187
  1925.7 16.0 dynamic_update_slice.51
  1958.3 12.6 fusion.189
  1970.9 17.2 fusion.186
  1988.0 21.2 fusion.187
  2026.6 16.0 dynamic_update_slice.51
  2059.2 12.6 fusion.189
  2071.8 17.2 fusion.186
  2089.0 21.2 fusion.187
  2127.6 16.0 dynamic_update_slice.51
  2196.5 12.1 add_convert_fusion.1
  2227.2 51.6 %reduce-scatter.23.cloned.1.call-done = bf16[192,128]{1,0:T(8,128)(2,1)} async-done(((bf16[1536,128]{1,0:T(8,128)(2,1)}), bf16[192,128]{1,0:T(8,128)(2,1)}) %reduce-scatter.23.cloned.1.call-update) | async-done | bytes 49168 | tf_op jit(solution)/shard_map/reduce_scatter | solution.py:330
  2280.3 65.3 %reduce-scatter.25.cloned.1.call-done = bf16[384,192]{0,1:T(8,128)(2,1)} async-done(((bf16[384,1536]{0,1:T(8,128)(2,1)}), bf16[384,192]{0,1:T(8,128)(2,1)}) %reduce-scatter.25.cloned.1.call-update) | async-done | bytes 147472 | tf_op jit(solution)/shard_map/reduce_scatter | solution.py:333
  2347.2 65.8 %reduce-scatter.19.cloned.1.call-done = bf16[192,384]{1,0:T(8,128)(2,1)} async-done(((bf16[1536,384]{1,0:T(8,128)(2,1)}), bf16[192,384]{1,0:T(8,128)(2,1)}) %reduce-scatter.19.cloned.1.call-update) | async-done | bytes 147472 | tf_op jit(solution)/shard_map/reduce_scatter | solution.py:324
  2414.7 57.1 %reduce-scatter.17.cloned.1.call-done = bf16[512,1536]{1,0:T(8,128)(2,1)} async-done(((bf16[2048,1536]{1,0:T(8,128)(2,1)}), bf16[512,1536]{1,0:T(8,128)(2,1)}) %reduce-scatter.17.cloned.1.call-update) | async-done | bytes 1572880 | tf_op jit(solution)/shard_map/reduce_scatter | solution.py:309
  2474.5 41.5 %all-reduce.4 = (f32[1536]{0:T(1024)S(1)}, f32[1536]{0:T(1024)S(1)}) all-reduce(f32[1536]{0:T(1024)S(1)} %get-tuple-element.354, f32[1536]{0:T(1024)S(1)} %copy-done.47), channel_id=4, replica_groups=mesh['ep'=8,'tp'=4] {'ep','tp'}, use_global_device_ids=true, to_apply=%region_29.30.clone | all-reduce | flops 3072 | bytes 24576
  (363 shorter events, 550.0 us)
Async XLA Ops:
  7.2 575.2 %copy-start = (bf16[1,512,1536]{2,1,0:T(8,128)(2,1)S(1)}, bf16[1,512,1536]{2,1,0:T(8,128)(2,1)}, u32[]{:S(2)}) copy-start(bf16[1,512,1536]{2,1,0:T(8,128)(2,1)} %param.29) | copy-start | bytes 4718596
  7.2 51.6 %copy-start.25 = (bf16[1536,128]{1,0:T(8,128)(2,1)S(1)}, bf16[1536,128]{1,0:T(8,128)(2,1)}, u32[]{:S(2)}) copy-start(bf16[1536,128]{1,0:T(8,128)(2,1)} %param.22) | copy-start | bytes 1179652
  7.2 51.6 %all-gather.3.cloned.1.call-start = ((), (), s32[]{:S(2)}) async-start(), calls=%async_computation.14 | async-start | bytes 7864320 | tf_op jit(solution)/shard_map/all_gather | solution.py:97
  12.2 325.0 %reduce-scatter.15.cloned.1.call-start = ((), (), s32[]{:S(2)}) async-start(), calls=%async_computation.15 | async-start | bytes 15728640 | tf_op jit(solution)/shard_map/reduce_scatter | solution.py:154
  13.4 53.6 %copy-start.19 = (f32[2048,32]{0,1:T(8,128)}, f32[2048,32]{0,1:T(8,128)S(1)}, u32[]{:S(2)}) copy-start(f32[2048,32]{0,1:T(8,128)S(1)} %get-tuple-element.426) | copy-start | bytes 786436
  13.4 53.6 %copy-start.21 = (f32[2048,32]{0,1:T(8,128)}, f32[2048,32]{0,1:T(8,128)S(1)}, u32[]{:S(2)}) copy-start(f32[2048,32]{0,1:T(8,128)S(1)} %get-tuple-element.427) | copy-start | bytes 786436
  227.9 10.1 copy-start.5
  227.9 10.1 copy-start.13
  227.9 10.1 copy-start.42
  238.0 99.3 %copy-start.7 = (bf16[512,1536]{1,0:T(8,128)(2,1)S(1)}, bf16[512,1536]{1,0:T(8,128)(2,1)}, u32[]{:S(2)}) copy-start(bf16[512,1536]{1,0:T(8,128)(2,1)} %param.19) | copy-start | bytes 4718596
  250.5 90.8 %copy-start.30 = (f32[1536]{0:T(1024)S(1)}, f32[1536]{0:T(1024)}, u32[]{:S(2)}) copy-start(f32[1536]{0:T(1024)} %param.25) | copy-start | bytes 18436
  357.6 211.6 %copy-start.56 = (bf16[1,1536,512]{2,1,0:T(8,128)(2,1)S(1)}, bf16[1,1536,512]{2,1,0:T(8,128)(2,1)}, u32[]{:S(2)}) copy-start(bf16[1,1536,512]{2,1,0:T(8,128)(2,1)} %param.27) | copy-start | bytes 4718596
  765.4 209.9 %all-to-all-start.1 = ((bf16[8,2,294912]{2,1,0:T(2,128)(2,1)}), bf16[8,2,294912]{2,1,0:T(2,128)(2,1)}, u32[]{:S(2)}, u32[]{:S(2)}) async-start(bf16[8,2,294912]{2,1,0:T(2,128)(2,1)} %reshape.600), calls=%async_computation.2 | async-start | bytes 18874368 | tf_op jit(solution)/shard_map/all_to_all | solution.py:189
  772.7 22.8 copy-start.11
  772.7 22.8 copy-start.33
  1022.3 11.2 copy-start.16
  1042.1 15.5 copy-start.36
  1266.8 14.5 copy-start.18
  1266.8 14.5 copy-start.57
  1281.3 9.2 copy-start.61
  1281.3 9.2 copy-start.59
  1394.0 209.6 %all-to-all-start.3 = ((bf16[8,2,294912]{2,1,0:T(2,128)(2,1)}), bf16[8,2,294912]{2,1,0:T(2,128)(2,1)}, u32[]{:S(2)}, u32[]{:S(2)}) async-start(bf16[8,2,294912]{2,1,0:T(2,128)(2,1)} %reshape.602), calls=%async_computation.4 | async-start | bytes 18874368 | tf_op jit(solution)/shard_map/all_to_all | solution.py:220
  1399.0 329.3 %all-gather.5.cloned.1.call-start = ((), (), s32[]{:S(2)}) async-start(), calls=%async_computation.16 | async-start | bytes 7864320 | tf_op jit(solution)/shard_map/all_gather | solution.py:240
  1662.8 12.6 copy-start.31
  1662.8 12.6 copy-start.34
  1662.8 12.6 copy-start.45
  1684.0 533.4 %reduce-scatter.31.cloned.1.call-start = ((), (), s32[]{:S(2)}) async-start(), calls=%async_computation.24 | async-start | bytes 811008
  1685.6 533.3 %reduce-scatter.33.cloned.1.call-start = ((), (), s32[]{:S(2)}) async-start(), calls=%async_computation.25 | async-start | bytes 1966080
  1705.1 516.7 %reduce-scatter.29.cloned.1.call-start = ((), (), s32[]{:S(2)}) async-start(), calls=%async_computation.23 | async-start | bytes 1966080 | tf_op jit(solution)/shard_map/reduce_scatter | solution.py:341
  1715.7 508.1 %reduce-scatter.27.cloned.1.call-start = ((), (), s32[]{:S(2)}) async-start(), calls=%async_computation.22 | async-start | bytes 1966080 | tf_op jit(solution)/shard_map/reduce_scatter | solution.py:338
  1715.8 12.6 copy-start.27
  1726.4 10.1 copy-start.6
  1726.4 10.0 copy-start.14
  1726.4 10.0 copy-start.41
  1726.4 10.0 copy-start.43
  1726.4 499.3 %reduce-scatter.21.cloned.1.call-start = ((), (), s32[]{:S(2)}) async-start(), calls=%async_computation.19 | async-start | bytes 442368 | tf_op jit(solution)/shard_map/reduce_scatter | solution.py:327
  2152.2 126.6 %reduce-scatter.23.cloned.1.call-start = ((), (), s32[]{:S(2)}) async-start(), calls=%async_computation.20 | async-start | bytes 442368 | tf_op jit(solution)/shard_map/reduce_scatter | solution.py:330
  2160.3 185.3 %reduce-scatter.25.cloned.1.call-start = ((), (), s32[]{:S(2)}) async-start(), calls=%async_computation.21 | async-start | bytes 1327104 | tf_op jit(solution)/shard_map/reduce_scatter | solution.py:333
  2168.2 244.8 %reduce-scatter.19.cloned.1.call-start = ((), (), s32[]{:S(2)}) async-start(), calls=%async_computation.18 | async-start | bytes 1327104 | tf_op jit(solution)/shard_map/reduce_scatter | solution.py:324
  2183.3 288.4 %reduce-scatter.17.cloned.1.call-start = ((), (), s32[]{:S(2)}) async-start(), calls=%async_computation.17 | async-start | bytes 7864320 | tf_op jit(solution)/shard_map/reduce_scatter | solution.py:309
  2220.2 251.5 %copy-start.8 = (bf16[512,1536]{1,0:T(8,128)(2,1)S(1)}, bf16[512,1536]{1,0:T(8,128)(2,1)}, u32[]{:S(2)}) copy-start(bf16[512,1536]{1,0:T(8,128)(2,1)} %param.19) | copy-start | bytes 4718596
  2220.2 251.5 %copy-start.35 = (f32[1536]{0:T(1024)S(1)}, f32[1536]{0:T(1024)}, u32[]{:S(2)}) copy-start(f32[1536]{0:T(1024)} %param.20) | copy-start | bytes 18436
  2220.3 251.5 %copy-start.49 = (f32[512]{0:T(512)S(1)}, f32[512]{0:T(512)}, u32[]{:S(2)}) copy-start(f32[512]{0:T(512)} %copy-done.48) | copy-start | bytes 6148
  2221.8 252.7 %copy-start.51 = (f32[512]{0:T(512)S(1)}, f32[512]{0:T(512)}, u32[]{:S(2)}) copy-start(f32[512]{0:T(512)} %copy-done.50) | copy-start | bytes 6148
  2221.8 252.7 %copy-start.47 = (f32[1536]{0:T(1024)S(1)}, f32[1536]{0:T(1024)}, u32[]{:S(2)}) copy-start(f32[1536]{0:T(1024)} %get-tuple-element.352) | copy-start | bytes 18436
  2221.8 295.4 %copy-start.32 = (f32[1536]{0:T(1024)S(1)}, f32[1536]{0:T(1024)}, u32[]{:S(2)}) copy-start(f32[1536]{0:T(1024)} %param.25) | copy-start | bytes 18436
  2221.8 295.4 %copy-start.46 = (f32[512]{0:T(512)S(1)}, f32[512]{0:T(512)}, u32[]{:S(2)}) copy-start(f32[512]{0:T(512)} %copy-done.44) | copy-start | bytes 6148
  2221.8 295.4 %copy-start.55 = (f32[512]{0:T(512)S(1)}, f32[512]{0:T(512)}, u32[]{:S(2)}) copy-start(f32[512]{0:T(512)} %copy-done.54) | copy-start | bytes 6148
  (30 other events, 123.3 us)
Sparse Core Ops, SparseCore 0:
  12.3 46.4 all-gather.2
  238.2 99.0 reduce-scatter.14
  1684.1 44.2 all-gather.4
  1733.9 96.6 reduce-scatter.30
  1833.0 26.1 reduce-scatter.32
  1861.7 28.1 reduce-scatter.28
  1892.5 28.1 reduce-scatter.26
  2152.4 62.3 reduce-scatter.20
  2218.3 60.4 reduce-scatter.22
  2282.4 63.1 reduce-scatter.24
  2349.9 63.0 reduce-scatter.18
  2415.6 56.1 reduce-scatter.16
where the time goes:
time: 2540 us; the launch traced here: 2530 us
  waiting for transfers between devices  758 us (30%)
  matrix products  510 us (20%)
  blocking collectives  462 us (18%)
  local copies, waits for them, and re-layouts  425 us (17%)
  other arithmetic  336 us (13%)
    all_to_all x1, blocking collectives, body(): lax.all_to_all(send_rows, 'ep', split_axis=0, concat_axis=1, tiled=True)  212 us
    all_to_all x1, blocking collectives, body(): lax.all_to_all(send_grad, 'ep', split_axis=0, concat_axis=1, tiled=True)  209 us
    all_to_all x1, waiting for transfers between devices, body(): lax.all_to_all(rows_grad.astype(jnp.bfloat16), 'ep', split_axis=1, concat...  204 us
    all_to_all x1, waiting for transfers between devices, body(): lax.all_to_all(expert_out, 'ep', split_axis=1, concat_axis=0, tiled=True)  179 us
    unnamed x3, other arithmetic  123 us
    convert_element_type x1, local copies, waits for them, and re-layouts, body(): expert_out = jnp.einsum('erf,efd->erd', activation, w_down, preferred_ele...  104 us
    unnamed x143, local copies, waits for them, and re-layouts  102 us
    dot_general x8, matrix products, block_scores(): jnp.einsum('qhgd,khd->hgqk', query_block, key_low, preferred_element_type...  90.4 us
  transfers between devices with their start and end apart: 14, of which 9 were waited for; matrix products, arithmetic and copies ran while one was open for 23% of the time, Pallas kernels for 0%

commit v1 on v0

v1 whole, which is shorter than its diff:
```python
import functools
import math

import jax
import jax.numpy as jnp
from jax import lax
from jax.experimental import pallas as pl
from jax.experimental.pallas import tpu as pltpu
from jax.sharding import Mesh, PartitionSpec as P

HEAD_SIZE = 64
HALF = HEAD_SIZE // 2
SEQUENCE_LENGTH = 2048
EPSILON = 1e-05
ROPE_BASE = 10000.0
MASK_FILL = -1e30
LANES = 128
F32 = jnp.float32
BF16 = jnp.bfloat16
VMEM_LIMIT = 60 * 1024 * 1024


def dot(a, b, ca=1, cb=0):
    return lax.dot_general(a, b, (((ca,), (cb,)), ((), ())), preferred_element_type=F32)


def qkv_kernel(q_cols, kv_cols, h_ref, w_ref, cos_ref, sin_ref, q_ref, k_ref, kt_ref, v_ref, vt_ref):
    y = dot(w_ref[...], h_ref[...], 1, 1)
    cos, sin = cos_ref[...], sin_ref[...]

    def turned(base):
        a = y[base : base + HALF]
        b = y[base + HALF : base + HEAD_SIZE]
        return jnp.concatenate([a * cos - b * sin, b * cos + a * sin], axis=0)

    for h in range(q_cols // HEAD_SIZE):
        base = h * HEAD_SIZE
        q_ref[base : base + HEAD_SIZE, :] = (
            turned(base).astype(BF16) * jnp.asarray(1.0 / math.sqrt(HEAD_SIZE), BF16)
        )
    for g in range(kv_cols // HEAD_SIZE):
        base = g * HEAD_SIZE
        kt = turned(q_cols + base)
        kt_ref[base : base + HEAD_SIZE, :] = kt.astype(BF16)
        k_ref[g] = kt.T.astype(BF16)
        vt = y[q_cols + kv_cols + base : q_cols + kv_cols + base + HEAD_SIZE]
        vt_ref[base : base + HEAD_SIZE, :] = vt.astype(BF16)
        v_ref[g] = vt.T.astype(BF16)


def project_qkv(h_all, w_all, cos, sin, rows, q_cols, kv_cols):
    total, width = h_all.shape
    groups = kv_cols // HEAD_SIZE
    cols = q_cols + 2 * kv_cols
    return pl.pallas_call(
        functools.partial(qkv_kernel, q_cols, kv_cols),
        grid=(total // rows,),
        in_specs=[
            pl.BlockSpec((rows, width), lambda i: (i, 0)),
            pl.BlockSpec((cols, width), lambda i: (0, 0)),
            pl.BlockSpec((HALF, rows), lambda i: (0, i)),
            pl.BlockSpec((HALF, rows), lambda i: (0, i)),
        ],
        out_specs=[
            pl.BlockSpec((q_cols, rows), lambda i: (0, i)),
            pl.BlockSpec((groups, rows, HEAD_SIZE), lambda i: (0, i, 0)),
            pl.BlockSpec((kv_cols, rows), lambda i: (0, i)),
            pl.BlockSpec((groups, rows, HEAD_SIZE), lambda i: (0, i, 0)),
            pl.BlockSpec((kv_cols, rows), lambda i: (0, i)),
        ],
        out_shape=[
            jax.ShapeDtypeStruct((q_cols, total), BF16),
            jax.ShapeDtypeStruct((groups, total, HEAD_SIZE), BF16),
            jax.ShapeDtypeStruct((kv_cols, total), BF16),
            jax.ShapeDtypeStruct((groups, total, HEAD_SIZE), BF16),
            jax.ShapeDtypeStruct((kv_cols, total), BF16),
        ],
        compiler_params=pltpu.CompilerParams(vmem_limit_bytes=VMEM_LIMIT),
        name="qkv",
    )(h_all, w_all, cos, sin)


def last_key(s_ref, zone, own, rows):
    zone_index = own * rows // zone
    zones = SEQUENCE_LENGTH // zone
    start = s_ref[1 + zone_index]
    stop = start + s_ref[1 + zones + zone_index]
    position = own * rows + lax.broadcasted_iota(jnp.int32, (1, rows), 1)
    return jnp.where((position >= start) & (position < stop), stop - 1, position)


def block_walk(me, own, rows, zone, pair):
    per_zone = zone // rows
    pair(own, True, True)
    for other in range(1, per_zone):
        pair(own ^ other, True, False)
    first = (own // per_zone) * per_zone

    def step(key_block, carry):
        pair(key_block, False, False)
        return carry

    lax.fori_loop(0, first, step, 0)


def attend_kernel(rows, zone, heads, groups, s_ref, q_ref, k_ref, vt_ref, o_ref, lse_ref, acc, top, total):
    me = s_ref[0]
    own = me ^ pl.program_id(0)
    limit = last_key(s_ref, zone, own, rows)

    def pair(key_block, masked, first):
        offset = pl.multiple_of((me ^ key_block) * rows, rows)
        if masked:
            key_pos = key_block * rows + lax.broadcasted_iota(jnp.int32, (rows, rows), 0)
            allowed = key_pos <= limit
        for h in range(heads):
            g = h // (heads // groups)
            r = slice(h * HEAD_SIZE, (h + 1) * HEAD_SIZE)
            s = dot(k_ref[g, pl.ds(offset, rows), :], q_ref[r, :])
            if masked:
                s = jnp.where(allowed, s, MASK_FILL)
            peak = jnp.max(s, axis=0, keepdims=True)
            vt = vt_ref[g * HEAD_SIZE : (g + 1) * HEAD_SIZE, pl.ds(offset, rows)]
            if first:
                p = jnp.exp(s - peak)
                top[h : h + 1, :] = peak
                total[h : h + 1, :] = jnp.sum(p, axis=0, keepdims=True)
                acc[r, :] = dot(vt, p.astype(BF16))
            else:
                old = top[h : h + 1, :]
                new = jnp.maximum(old, peak)
                fade = jnp.exp(old - new)
                p = jnp.exp(s - new)
                top[h : h + 1, :] = new
                total[h : h + 1, :] = total[h : h + 1, :] * fade + jnp.sum(p, axis=0, keepdims=True)
                acc[r, :] = acc[r, :] * fade + dot(vt, p.astype(BF16))

    block_walk(me, own, rows, zone, pair)
    for h in range(heads):
        r = slice(h * HEAD_SIZE, (h + 1) * HEAD_SIZE)
        o_ref[r, :] = (acc[r, :] / total[h : h + 1, :]).astype(BF16)
        lse_ref[h : h + 1, :] = top[h : h + 1, :] + jnp.log(total[h : h + 1, :])


def attend(scalars, q, k, vt, rows, zone):
    q_cols, total = q.shape
    groups = k.shape[0]
    heads = q_cols // HEAD_SIZE
    return pl.pallas_call(
        functools.partial(attend_kernel, rows, zone, heads, groups),
        grid_spec=pltpu.PrefetchScalarGridSpec(
            num_scalar_prefetch=1,
            grid=(total // rows,),
            in_specs=[
                pl.BlockSpec((q_cols, rows), lambda i, s: (0, i)),
                pl.BlockSpec(k.shape, lambda i, s: (0, 0, 0)),
                pl.BlockSpec(vt.shape, lambda i, s: (0, 0)),
            ],
            out_specs=[
                pl.BlockSpec((q_cols, rows), lambda i, s: (0, i)),
                pl.BlockSpec((heads, rows), lambda i, s: (0, i)),
            ],
            scratch_shapes=[
                pltpu.VMEM((q_cols, rows), F32),
                pltpu.VMEM((8, rows), F32),
                pltpu.VMEM((8, rows), F32),
            ],
        ),
        out_shape=[
            jax.ShapeDtypeStruct((q_cols, total), BF16),
            jax.ShapeDtypeStruct((heads, total), F32),
        ],
        compiler_params=pltpu.CompilerParams(vmem_limit_bytes=VMEM_LIMIT),
        name="attend",
    )(scalars, q, k, vt)


def attend_back_kernel(
    rows,
    zone,
    heads,
    groups,
    s_ref,
    q_ref,
    o_ref,
    do_ref,
    lse_ref,
    k_ref,
    kt_ref,
    v_ref,
    cos_ref,
    sin_ref,
    dq_ref,
    dkv_ref,
    dq,
    dk,
    dv,
    delta,
):
    me = s_ref[0]
    step = pl.program_id(0)
    own = me ^ step
    limit = last_key(s_ref, zone, own, rows)
    here = pl.multiple_of(step * rows, rows)

    @pl.when(step == 0)
    def _():
        dk[...] = jnp.zeros_like(dk)
        dv[...] = jnp.zeros_like(dv)

    for h in range(heads):
        r = slice(h * HEAD_SIZE, (h + 1) * HEAD_SIZE)
        delta[h : h + 1, :] = jnp.sum(
            do_ref[r, :].astype(F32) * o_ref[r, :].astype(F32), axis=0, keepdims=True
        )

    def pair(key_block, masked, first):
        offset = pl.multiple_of((me ^ key_block) * rows, rows)
        keys = pl.ds(offset, rows)
        if masked:
            key_pos = key_block * rows + lax.broadcasted_iota(jnp.int32, (rows, rows), 0)
            allowed = key_pos <= limit
        for g in range(groups):
            kb = k_ref[g, keys, :]
            vb = v_ref[g, keys, :]
            kt = kt_ref[g * HEAD_SIZE : (g + 1) * HEAD_SIZE, keys]
            dk_sum = dk[g, keys, :]
            dv_sum = dv[g, keys, :]
            for h in range(g * (heads // groups), (g + 1) * (heads // groups)):
                r = slice(h * HEAD_SIZE, (h + 1) * HEAD_SIZE)
                s = dot(kb, q_ref[r, :])
                if masked:
                    s = jnp.where(allowed, s, MASK_FILL)
                p = jnp.exp(s - lse_ref[h : h + 1, :])
                dp = dot(vb, do_ref[r, :])
                ds = (p * (dp - delta[h : h + 1, :])).astype(BF16)
                dv_sum = dv_sum + dot(p.astype(BF16), do_ref[r, :], 1, 1)
                dk_sum = dk_sum + dot(ds, q_ref[r, :], 1, 1)
                part = dot(kt, ds)
                dq[r, :] = part if first else dq[r, :] + part
            dk[g, keys, :] = dk_sum
            dv[g, keys, :] = dv_sum

    block_walk(me, own, rows, zone, pair)
    cos, sin = cos_ref[:, pl.ds(here, rows)], sin_ref[:, pl.ds(here, rows)]
    scale = 1.0 / math.sqrt(HEAD_SIZE)
    for h in range(heads):
        base = h * HEAD_SIZE
        a = dq[base : base + HALF, :] * scale
        b = dq[base + HALF : base + HEAD_SIZE, :] * scale
        dq_ref[base : base + HALF, :] = (a * cos + b * sin).astype(BF16)
        dq_ref[base + HALF : base + HEAD_SIZE, :] = (b * cos - a * sin).astype(BF16)

    @pl.when(step == pl.num_programs(0) - 1)
    def _():
        every_cos, every_sin = cos_ref[...], sin_ref[...]
        for g in range(groups):
            base = g * HEAD_SIZE
            turned = dk[g].T
            a, b = turned[:HALF], turned[HALF:]
            dkv_ref[base : base + HALF, :] = (a * every_cos + b * every_sin).astype(BF16)
            dkv_ref[base + HALF : base + HEAD_SIZE, :] = (b * every_cos - a * every_sin).astype(BF16)
            base = (groups + g) * HEAD_SIZE
            dkv_ref[base : base + HEAD_SIZE, :] = dv[g].T.astype(BF16)


def attend_back(scalars, q, o, do, lse, k, kt, v, cos, sin, rows, zone):
    q_cols, total = q.shape
    groups = k.shape[0]
    heads = q_cols // HEAD_SIZE
    whole2 = lambda i, s: (0, 0)
    whole3 = lambda i, s: (0, 0, 0)
    block = lambda i, s: (0, i)
    return pl.pallas_call(
        functools.partial(attend_back_kernel, rows, zone, heads, groups),
        grid_spec=pltpu.PrefetchScalarGridSpec(
            num_scalar_prefetch=1,
            grid=(total // rows,),
            in_specs=[
                pl.BlockSpec((q_cols, rows), block),
                pl.BlockSpec((q_cols, rows), block),
                pl.BlockSpec((q_cols, rows), block),
                pl.BlockSpec((heads, rows), block),
                pl.BlockSpec(k.shape, whole3),
                pl.BlockSpec(kt.shape, whole2),
                pl.BlockSpec(v.shape, whole3),
                pl.BlockSpec(cos.shape, whole2),
                pl.BlockSpec(sin.shape, whole2),
            ],
            out_specs=[
                pl.BlockSpec((q_cols, rows), block),
                pl.BlockSpec((2 * groups * HEAD_SIZE, total), whole2),
            ],
            scratch_shapes=[
                pltpu.VMEM((q_cols, rows), F32),
                pltpu.VMEM((groups, total, HEAD_SIZE), F32),
                pltpu.VMEM((groups, total, HEAD_SIZE), F32),
                pltpu.VMEM((8, rows), F32),
            ],
        ),
        out_shape=[
            jax.ShapeDtypeStruct((q_cols, total), BF16),
            jax.ShapeDtypeStruct((2 * groups * HEAD_SIZE, total), BF16),
        ],
        compiler_params=pltpu.CompilerParams(vmem_limit_bytes=VMEM_LIMIT),
        name="attend_back",
    )(scalars, q, o, do, lse, k, kt, v, cos, sin)


def expert_kernel(
    experts,
    s_ref,
    h_ref,
    dy_ref,
    routes_ref,
    router_ref,
    wg_ref,
    wu_ref,
    wd_ref,
    mix_ref,
    dh_ref,
    dgate_ref,
    gates_ref,
    act_ref,
    dgu_ref,
    mix,
    dh,
):
    e = pl.program_id(1)
    rows = h_ref.shape[0]
    hidden = wg_ref.shape[2]
    lane = lax.broadcasted_iota(jnp.int32, (rows, LANES), 1)
    expert = s_ref[e]

    @pl.when(e == 0)
    def _():
        logits = dot(h_ref[...], router_ref[...])
        logits = jnp.where(lane < experts, logits, MASK_FILL)
        weights = jnp.exp(logits - jnp.max(logits, axis=1, keepdims=True))
        weights = weights / jnp.sum(weights, axis=1, keepdims=True)
        chosen = jnp.zeros((rows, LANES), jnp.bool_)
        for j in range(routes_ref.shape[1]):
            chosen = chosen | (routes_ref[:, j : j + 1] == lane)
        gates_ref[...] = jnp.where(chosen, weights, 0.0)
        dgate_ref[...] = jnp.zeros_like(dgate_ref)
        mix[...] = jnp.zeros_like(mix)
        dh[...] = jnp.zeros_like(dh)

    gate = jnp.sum(jnp.where(lane == expert, gates_ref[...], 0.0), axis=1, keepdims=True)
    chosen = jnp.max(jnp.where(routes_ref[...] == expert, 1.0, 0.0), axis=1, keepdims=True)
    gp = dot(h_ref[...], wg_ref[0])
    up = dot(h_ref[...], wu_ref[0])
    sg = jax.nn.sigmoid(gp)
    silu = gp * sg
    act = (silu * up).astype(BF16)
    act_ref[0] = act
    eo = dot(act, wd_ref[0]).astype(BF16).astype(F32)
    dy = dy_ref[...].astype(F32)
    dgate = chosen * jnp.sum(dy * eo, axis=1, keepdims=True)
    dgate_ref[...] += jnp.where(lane == expert, dgate, 0.0)
    mix[...] += gate * eo
    dact = dot((gate * dy).astype(BF16), wd_ref[0], 1, 1)
    dgp = (dact * up * sg * (1.0 + gp * (1.0 - sg))).astype(BF16)
    dup = (dact * silu).astype(BF16)
    dgu_ref[0, :, :hidden] = dgp
    dgu_ref[0, :, hidden:] = dup
    part = dot(dgp, wg_ref[0], 1, 1) + dot(dup, wu_ref[0], 1, 1)
    dh[...] += part.astype(BF16).astype(F32)

    @pl.when(e == pl.num_programs(1) - 1)
    def _():
        mix_ref[...] = mix[...].astype(BF16)
        dh_ref[...] = dh[...].astype(BF16)


def run_experts(ids, h, dy, routes, router, wg, wu, wd, experts, rows):
    total, width = h.shape
    mine, _, hidden = wg.shape
    token = lambda i, e, s: (i, 0)
    matrix = lambda i, e, s: (e, 0, 0)
    return pl.pallas_call(
        functools.partial(expert_kernel, experts),
        grid_spec=pltpu.PrefetchScalarGridSpec(
            num_scalar_prefetch=1,
            grid=(total // rows, mine),
            in_specs=[
                pl.BlockSpec((rows, width), token),
                pl.BlockSpec((rows, width), token),
                pl.BlockSpec((rows, routes.shape[1]), token),
                pl.BlockSpec((width, LANES), lambda i, e, s: (0, 0)),
                pl.BlockSpec((1, width, hidden), matrix),
                pl.BlockSpec((1, width, hidden), matrix),
                pl.BlockSpec((1, hidden, width), matrix),
            ],
            out_specs=[
                pl.BlockSpec((rows, width), token),
                pl.BlockSpec((rows, width), token),
                pl.BlockSpec((rows, LANES), token),
                pl.BlockSpec((rows, LANES), token),
                pl.BlockSpec((1, rows, hidden), lambda i, e, s: (e, i, 0)),
                pl.BlockSpec((1, rows, 2 * hidden), lambda i, e, s: (e, i, 0)),
            ],
            scratch_shapes=[pltpu.VMEM((rows, width), F32), pltpu.VMEM((rows, width), F32)],
        ),
        out_shape=[
            jax.ShapeDtypeStruct((total, width), BF16),
            jax.ShapeDtypeStruct((total, width), BF16),
            jax.ShapeDtypeStruct((total, LANES), F32),
            jax.ShapeDtypeStruct((total, LANES), F32),
            jax.ShapeDtypeStruct((mine, total, hidden), BF16),
            jax.ShapeDtypeStruct((mine, total, 2 * hidden), BF16),
        ],
        compiler_params=pltpu.CompilerParams(vmem_limit_bytes=VMEM_LIMIT),
        name="experts",
    )(ids, h, dy, routes, router, wg, wu, wd)


def expert_grad_kernel(s_ref, h_ref, dy_ref, gates_ref, act_ref, dgu_ref, out_ref, gate_up, down):
    rows = h_ref.shape[0]
    hidden = act_ref.shape[2]
    step = pl.program_id(1)
    lane = lax.broadcasted_iota(jnp.int32, (rows, LANES), 1)
    expert = s_ref[pl.program_id(0)]
    gate = jnp.sum(jnp.where(lane == expert, gates_ref[...], 0.0), axis=1, keepdims=True)
    deo = (gate * dy_ref[...].astype(F32)).astype(BF16)
    new_gate_up = dot(h_ref[...], dgu_ref[0], 0, 0)
    new_down = dot(deo, act_ref[0], 0, 0)

    @pl.when(step == 0)
    def _():
        gate_up[...] = new_gate_up
        down[...] = new_down

    @pl.when(step > 0)
    def _():
        gate_up[...] += new_gate_up
        down[...] += new_down

    @pl.when(step == pl.num_programs(1) - 1)
    def _():
        out_ref[0, :, : 2 * hidden] = gate_up[...].astype(BF16)
        out_ref[0, :, 2 * hidden :] = down[...].astype(BF16)


def expert_grads(ids, h, dy, gates, act, dgu, rows):
    total, width = h.shape
    mine, _, hidden = act.shape
    token = lambda e, i, s: (i, 0)
    return pl.pallas_call(
        expert_grad_kernel,
        grid_spec=pltpu.PrefetchScalarGridSpec(
            num_scalar_prefetch=1,
            grid=(mine, total // rows),
            in_specs=[
                pl.BlockSpec((rows, width), token),
                pl.BlockSpec((rows, width), token),
                pl.BlockSpec((rows, LANES), token),
                pl.BlockSpec((1, rows, hidden), lambda e, i, s: (e, i, 0)),
                pl.BlockSpec((1, rows, 2 * hidden), lambda e, i, s: (e, i, 0)),
            ],
            out_specs=pl.BlockSpec((1, width, 3 * hidden), lambda e, i, s: (e, 0, 0)),
            scratch_shapes=[pltpu.VMEM((width, 2 * hidden), F32), pltpu.VMEM((width, hidden), F32)],
        ),
        out_shape=jax.ShapeDtypeStruct((mine, width, 3 * hidden), BF16),
        compiler_params=pltpu.CompilerParams(vmem_limit_bytes=VMEM_LIMIT),
        name="expert_grads",
    )(ids, h, dy, gates, act, dgu)


def body(
    sizes,
    tokens,
    norm1_gain,
    w_query,
    key_weight,
    value_weight,
    w_out,
    norm2_gain,
    w_router,
    w_gate,
    w_up,
    w_down,
    routes,
    piece_first_position,
    piece_length,
    grad_out,
):
    nz, nx = sizes
    rows, width = tokens.shape
    blocks = 2 * nx
    q_cols, kv_cols = w_query.shape[1], key_weight.shape[1]
    experts = w_router.shape[1]
    hidden = w_gate.shape[2]
    zone = SEQUENCE_LENGTH // piece_length.shape[1]
    iz, iy, ix, ic = (lax.axis_index(a) for a in "zyxc")
    me = ix * 2 + ic

    def tp_swap(value, bit):
        if bit == 0:
            return lax.ppermute(value, "c", [(0, 1), (1, 0)])
        return lax.ppermute(value, "x", [(i, i ^ (1 << (bit - 1))) for i in range(nx)])

    def y_swap(value):
        return lax.ppermute(value, "y", [(0, 1), (1, 0)])

    bits = blocks.bit_length() - 1

    def tp_gather(value):
        held = {0: value}
        for bit in reversed(range(bits)):
            for i in list(held):
                held[i | (1 << bit)] = tp_swap(held[i], bit)
        return jnp.concatenate([held[i] for i in range(blocks)], axis=0)

    def tp_scatter(parts):
        parts = dict(enumerate(parts))
        for bit in range(bits):
            for i in sorted(parts):
                if i & (1 << bit):
                    parts[i] = tp_swap(parts[i], bit)
            for i in sorted(parts):
                if i & (1 << bit):
                    other = parts.pop(i)
                    base = parts[i ^ (1 << bit)].astype(F32) + other.astype(F32)
                    parts[i ^ (1 << bit)] = base if i == 1 << bit else base.astype(BF16)
        return parts[0]

    def group_gather(value):
        across = y_swap(value)
        return [value, tp_swap(value, 0), across, tp_swap(across, 0)]

    mine = nz // 2
    ids = (ic * mine + jnp.arange(mine, dtype=jnp.int32)) * 2 + iy
    if nz == 4:
        up0 = [(0, 1), (1, 2)]
        pairs = {
            "a": [((i, 0), (j, 0)) for i, j in up0] + [((3 - i, 1), (3 - j, 1)) for i, j in up0],
            "b": [((1, 0), (0, 0)), ((2, 1), (3, 1))],
            "c": [((i, 0), (j, 0)) for i, j in [(1, 2), (2, 3)]]
            + [((3 - i, 1), (3 - j, 1)) for i, j in [(1, 2), (2, 3)]],
            "d": [((2, 0), (3, 0)), ((1, 1), (0, 1))],
        }
        perms = {
            k: [(s[0] * 2 + s[1], d[0] * 2 + d[1]) for s, d in v] for k, v in pairs.items()
        }
        along = jnp.where(ic == 0, iz, 3 - iz)

        def spread(weight):
            a = lax.ppermute(weight, ("z", "c"), perms["a"])
            b = lax.ppermute(weight, ("z", "c"), perms["b"])
            c = lax.ppermute(a, ("z", "c"), perms["c"])
            d = lax.ppermute(c, ("z", "c"), perms["d"])
            outer = jnp.where(along == 0, weight, jnp.where(along == 1, a, jnp.where(along == 2, c, d)))
            inner = jnp.where(along == 0, b, jnp.where(along == 1, weight, jnp.where(along == 2, a, c)))
            low = jnp.where(ic == 0, outer, inner)
            high = jnp.where(ic == 0, inner, outer)
            return jnp.concatenate([low, high], axis=0)

    else:

        def spread(weight):
            every = lax.all_gather(weight, "z", axis=0, tiled=True)
            return lax.dynamic_slice_in_dim(every, ic * mine, mine, 0)

    wg, wu, wd = spread(w_gate), spread(w_up), spread(w_down)
    dy_group = jnp.concatenate(group_gather(grad_out), axis=0)
    routes_group = jnp.concatenate(group_gather(routes), axis=0)

    x = tokens.astype(F32)
    r1 = lax.rsqrt(jnp.mean(x * x, axis=-1, keepdims=True) + EPSILON)
    h1 = (x * r1 * norm1_gain).astype(BF16)
    h_all = tp_gather(h1)
    w_all = jnp.concatenate([w_query, key_weight, value_weight], axis=1)
    w_all_t = w_all.T
    total = rows * blocks
    order = me ^ jnp.arange(blocks, dtype=jnp.int32)
    position = (order[:, None] * rows + jnp.arange(rows, dtype=jnp.int32)[None, :]).reshape(total)
    frequency = ROPE_BASE ** (-(jnp.arange(HALF, dtype=F32) * (2.0 / HEAD_SIZE)))
    angles = frequency[:, None] * position.astype(F32)[None, :]
    cos, sin = jnp.cos(angles), jnp.sin(angles)
    scalars = jnp.concatenate(
        [me.astype(jnp.int32)[None], piece_first_position[0], piece_length[0]]
    )
    q, k, kt, v, vt = project_qkv(h_all, w_all_t, cos, sin, rows, q_cols, kv_cols)
    o, lse = attend(scalars, q, k, vt, rows, zone)
    out_parts = [
        dot(o[:, i * rows : (i + 1) * rows], w_out, 0, 0).astype(BF16) for i in range(blocks)
    ]
    x1 = x + tp_scatter(out_parts)
    r2 = lax.rsqrt(jnp.mean(x1 * x1, axis=-1, keepdims=True) + EPSILON)
    n2 = x1 * r2
    h2 = (n2 * norm2_gain).astype(BF16)

    router_wide = jnp.pad(w_router, ((0, 0), (0, LANES - experts)))
    h2_group = group_gather(h2)
    mixes, dhs, dgates, gates, acts, dgus = [], [], [], [], [], []
    for first in (0, 2):
        part = slice(first * rows, (first + 2) * rows)
        results = run_experts(
            ids,
            jnp.concatenate(h2_group[first : first + 2], axis=0),
            dy_group[part],
            routes_group[part],
            router_wide,
            wg,
            wu,
            wd,
            experts,
            rows,
        )
        for store, value in zip((mixes, dhs, dgates, gates, acts, dgus), results):
            store.append(value)

    def group_scatter(near, far, kind):
        own, core = near[:rows], near[rows:]
        side, cross = far[:rows], far[rows:]
        side = (side.astype(F32) + tp_swap(cross, 0).astype(F32)).astype(kind)
        side = y_swap(side)
        return own.astype(F32) + tp_swap(core, 0).astype(F32) + side.astype(F32)

    dh2_routes = group_scatter(dhs[0], dhs[1], BF16)
    dprobs = group_scatter(dgates[0], dgates[1], F32)[:, :experts]
    output = x1 + group_scatter(mixes[0], mixes[1], BF16)

    logits = dot(h2, w_router)
    probs = jax.nn.softmax(logits, axis=-1)
    dlogits = (
        probs * (dprobs - jnp.sum(probs * dprobs, axis=-1, keepdims=True))
    ).astype(BF16)
    router_part = dot(h2, dlogits, 0, 0)
    dh2 = dot(dlogits, w_router, 1, 1) + dh2_routes
    gain2_part = jnp.sum(dh2 * n2, axis=0)
    scaled = dh2 * norm2_gain
    dx1 = grad_out.astype(F32) + r2 * (
        scaled - n2 * jnp.mean(scaled * n2, axis=-1, keepdims=True)
    )

    da_all = tp_gather(dx1.astype(BF16))
    do = dot(w_out, da_all, 1, 1).astype(BF16)
    dq, dkv = attend_back(scalars, q, o, do, lse, k, kt, v, cos, sin, rows, zone)
    dqkv = jnp.concatenate([dq, dkv], axis=0)
    dh1_parts = [
        dot(dqkv[:, i * rows : (i + 1) * rows], w_all_t, 0, 0).astype(BF16) for i in range(blocks)
    ]
    dh1 = tp_scatter(dh1_parts)
    n1 = x * r1
    scaled = dh1 * norm1_gain
    grad_input = dx1 + r1 * (scaled - n1 * jnp.mean(scaled * n1, axis=-1, keepdims=True))

    grad_all = lax.dot_general(h_all, dqkv, (((0,), (1,)), ((), ())), preferred_element_type=F32)
    gain1_part = jnp.sum(grad_all * w_all.astype(F32), axis=1) / norm1_gain
    grad_qkv = lax.psum_scatter(
        grad_all.astype(BF16), ("z", "y"), scatter_dimension=0, tiled=True
    ).astype(F32)
    out_grad = lax.dot_general(da_all, o, (((0,), (1,)), ((), ())), preferred_element_type=F32)
    grad_outproj = lax.psum_scatter(
        out_grad.astype(BF16), ("z", "y"), scatter_dimension=0, tiled=True
    ).astype(F32).T

    stacked = expert_grads(
        ids,
        jnp.concatenate(h2_group, axis=0),
        dy_group,
        jnp.concatenate(gates, axis=0),
        jnp.concatenate(acts, axis=1),
        jnp.concatenate(dgus, axis=1),
        rows,
    )
    if nz == 4:
        part = lax.psum_scatter(
            stacked.reshape(mine * width, 3 * hidden), "z", scatter_dimension=0, tiled=True
        )
        part = lax.psum_scatter(part, "x", scatter_dimension=0, tiled=True)
        perm = []
        for z in range(4):
            for xx in range(2):
                for cc in range(2):
                    perm.append((z * 4 + xx * 2 + cc, (2 * cc + z // 2) * 4 + (z % 2) * 2 + xx))
        part = lax.ppermute(part, ("z", "x", "c"), perm)
    else:
        every = jnp.zeros((nz, width, 3 * hidden), BF16)
        every = lax.dynamic_update_slice_in_dim(every, stacked, ic * mine, 0)
        part = lax.psum_scatter(
            every.reshape(nz * width, 3 * hidden), "z", scatter_dimension=0, tiled=True
        )
        part = lax.psum_scatter(part, ("x", "c"), scatter_dimension=0, tiled=True)
    part = part.astype(F32)
    grad_gate = part[None, :, :hidden]
    grad_up = part[None, :, hidden : 2 * hidden]
    grad_down = part[:, 2 * hidden :].T[None]

    every_axis = ("z", "y", "x", "c")
    small = jnp.concatenate([router_part, gain2_part[:, None]], axis=1)
    small = lax.psum_scatter(small, every_axis, scatter_dimension=0, tiled=True)
    grad_norm1 = lax.psum_scatter(gain1_part, every_axis, scatter_dimension=0, tiled=True)
    return (
        output,
        grad_input,
        grad_norm1,
        grad_qkv[:, :q_cols],
        grad_qkv[:, q_cols : q_cols + kv_cols],
        grad_qkv[:, q_cols + kv_cols :],
        grad_outproj,
        small[:, experts],
        small[:, :experts],
        grad_gate,
        grad_up,
        grad_down,
    )


def solution(mesh):
    ep, tp = mesh.shape["ep"], mesh.shape["tp"]
    nz, nx = ep // 2, tp // 2
    grid = Mesh(mesh.devices.reshape(nz, 2, nx, 2), ("z", "y", "x", "c"))
    e, t = ("z", "y"), ("x", "c")
    every = ("z", "y", "x", "c")
    return jax.shard_map(
        functools.partial(body, (nz, nx)),
        mesh=grid,
        in_specs=(
            P(every, None),
            P(),
            P(None, t),
            P(None, t),
            P(None, t),
            P(t, None),
            P(),
            P(),
            P(e, None, None),
            P(e, None, None),
            P(e, None, None),
            P(every, None),
            P(e, None),
            P(e, None),
            P(every, None),
        ),
        out_specs=(
            P(every, None),
            P(every, None),
            P(every),
            P(e, t),
            P(e, t),
            P(e, t),
            P(t, e),
            P(every),
            P(every, None),
            P(e, t, None),
            P(e, t, None),
            P(e, None, t),
        ),
        check_vma=False,
    )
```

time: 2540 us -> 918 us (0.36)
  matrix products: 510 us -> 49 us
  blocking collectives: 462 us -> 48.8 us
  local copies, waits for them, and re-layouts: 425 us -> 35.5 us
  waiting for transfers between devices: 758 us -> 397 us
  other arithmetic: 336 us -> 97 us
  Pallas kernels: 0 us -> 191 us
  starting transfers between devices: 10.8 us -> 74 us
    dot_general x53 -> x14, matrix products: 508 us -> 49 us  [the longest x12 35.9 us: dot(): lax.dot_general(a, b, (((ca,), (cb,)), ((), ())), preferred_element_type=...]
    all_to_all x2 -> x0, blocking collectives: 421 us -> none  [the longest x1 212 us: body(): lax.all_to_all(send_rows, 'ep', split_axis=0, concat_axis=1, tiled=True)]
    all_to_all x2 -> x0, waiting for transfers between devices: 384 us -> none  [the longest x1 204 us: body(): lax.all_to_all(rows_grad.astype(jnp.bfloat16), 'ep', split_axis=1, concat...]
    reduce_scatter x8 -> x3, waiting for transfers between devices: 327 us -> 92.2 us  [the longest x1 53.8 us: body(): lax.psum_scatter(stacked.reshape(mine * width, 3 * hidden), 'z', scatter_...]
    ppermute x0 -> x43, waiting for transfers between devices: none -> 221 us  [the longest x4 87.4 us: tp_swap(): return lax.ppermute(value, 'x', [(i, i ^ 1 << bit - 1) for i in range(nx)])]
    pallas_call x0 -> x6, Pallas kernels: none -> 191 us  [the longest x2 65.8 us: run_experts(): pl.pallas_call(functools.partial(expert_kernel, experts), grid_spec=pltpu...]
    convert_element_type x3 -> x0, local copies, waits for them, and re-layouts: 133 us -> none  [the longest x1 104 us: body(): expert_out = jnp.einsum('erf,efd->erd', activation, w_down, preferred_ele...]
    unnamed x3 -> x2, other arithmetic: 123 us -> 0.07 us
  transfers between devices with their start and end apart: 14 -> 48, of which waited for: 9 -> 17; matrix products, arithmetic and copies ran while one was open for 23% -> 16% of each run, Pallas kernels for 0% -> 14%
where the time goes in v1:
time: 918 us; the launch traced here: 907 us
  waiting for transfers between devices  397 us (43%)
  Pallas kernels  191 us (21%)
  other arithmetic  97 us (11%)
  starting transfers between devices  74 us (8%)
  matrix products  49 us (5%)
  blocking collectives  48.8 us (5%)
  local copies, waits for them, and re-layouts  35.5 us (4%)
  between operations  14.7 us (2%)
    ppermute x4, waiting for transfers between devices, tp_swap(): return lax.ppermute(value, 'x', [(i, i ^ 1 << bit - 1) for i in range(nx)])  87.4 us
    unnamed x7, waiting for transfers between devices  83.8 us
    pallas_call x2, Pallas kernels, run_experts(): pl.pallas_call(functools.partial(expert_kernel, experts), grid_spec=pltpu...  65.8 us
    ppermute x6, waiting for transfers between devices, y_swap(): return lax.ppermute(value, 'y', [(0, 1), (1, 0)])  63.8 us
    ppermute x3, waiting for transfers between devices, spread(): b = lax.ppermute(weight, ('z', 'c'), perms['b'])  61.4 us
    reduce_scatter x1, waiting for transfers between devices, body(): lax.psum_scatter(stacked.reshape(mine * width, 3 * hidden), 'z', scatter_...  53.8 us
    unnamed x1, blocking collectives  48.8 us
    pallas_call x1, Pallas kernels, attend_back(): pl.pallas_call(functools.partial(attend_back_kernel, rows, zone, heads, g...  45.8 us
  transfers between devices with their start and end apart: 48, of which 17 were waited for; matrix products, arithmetic and copies ran while one was open for 16% of the time, Pallas kernels for 14%

profile of v1, /device:TPU:2, one launch (start us, length us, event | category | flops | bytes accessed | tf_op | source)
XLA Modules:
  0.0 906.5 jit_solution(8090282249998492027)
XLA Ops:
  11.5 36.4 %collective-permute-done.1 = bf16[512,1536]{1,0:T(8,128)(2,1)} collective-permute-done((bf16[512,1536]{1,0:T(8,128)(2,1)}, bf16[512,1536]{1,0:T(8,128)(2,1)}, u32[]{:S(2)}, u32[]{:S(2)}) %collective-permute-start.1) | collective-permute-done | bytes 1572896 | tf_op jit(solution)/shard_map/ppermute | solution.py:501
  57.1 28.1 %collective-permute-done.26 = s32[512,4]{0,1:T(4,128)S(1)} collective-permute-done((s32[512,4]{0,1:T(4,128)S(1)}, s32[512,4]{0,1:T(4,128)S(1)}, u32[]{:S(2)}, u32[]{:S(2)}) %collective-permute-start.26) | collective-permute-done | bytes 8224 | tf_op jit(solution)/shard_map/ppermute | solution.py:504
  85.2 4.6 collective-permute-start.13
  89.8 3.5 collective-permute-start.9
  95.7 6.3 pad_maximum_fusion.1.h_ref
  102.0 9.1 qkv.1
  111.1 34.8 %attend.1 = (bf16[384,2048]{1,0:T(8,128)(2,1)}, f32[6,2048]{1,0:T(8,128)}) custom-call(s32[9]{0:T(128)} %pad_add_fusion.2.s_ref, bf16[384,2048]{1,0:T(8,128)(2,1)} %get-tuple-element.33.q_ref, bf16[2,2048,64]{2,1,0:T(8,128)(2,1)} %get-tuple-element.34.k_ref, bf16[128,2048]{1,0:T(8,128)(2,1)} %get-tuple-element.35.vt_ref), custom_call_target="tpu_custom_call" | custom-call | tf_op jit(solution)/shard_map/attend/pallas_call | solution.py:149
  146.5 3.1 convolution_convert_fusion.4
  160.0 3.9 pad_maximum_fusion.7.dy_ref
  164.9 4.2 collective-permute-done.17
  175.1 3.7 pad_maximum_fusion.12.dy_ref
  178.8 6.4 pad_maximum_fusion.4.dy_ref
  187.7 20.9 %collective-permute-done.16 = bf16[1,1536,512]{2,1,0:T(8,128)(2,1)S(1)} collective-permute-done((bf16[1,1536,512]{2,1,0:T(8,128)(2,1)}, bf16[1,1536,512]{2,1,0:T(8,128)(2,1)S(1)}, u32[]{:S(2)}, u32[]{:S(2)}) %collective-permute-start.16) | collective-permute-done | bytes 1572896 | tf_op jit(solution)/shard_map/ppermute | solution.py:550
  209.8 32.4 %collective-permute-done.12 = bf16[1,1536,512]{2,1,0:T(8,128)(2,1)S(1)} collective-permute-done((bf16[1,1536,512]{2,1,0:T(8,128)(2,1)}, bf16[1,1536,512]{2,1,0:T(8,128)(2,1)S(1)}, u32[]{:S(2)}, u32[]{:S(2)}) %collective-permute-start.12) | collective-permute-done | bytes 1572896 | tf_op jit(solution)/shard_map/ppermute | solution.py:550
  244.7 4.2 broadcast_select_fusion.3
  249.1 15.5 %collective-permute-done.5 = bf16[512,1536]{1,0:T(8,128)(2,1)S(1)} collective-permute-done((bf16[512,1536]{1,0:T(8,128)(2,1)S(1)}, bf16[512,1536]{1,0:T(8,128)(2,1)S(1)}, u32[]{:S(2)}, u32[]{:S(2)}) %collective-permute-start.5) | collective-permute-done | bytes 1572896 | tf_op jit(solution)/shard_map/ppermute | solution.py:501
  267.9 8.1 collective-permute-done.20
  276.0 3.0 broadcast_select_fusion.1
  278.9 33.0 %collective-permute-start.6 = (bf16[512,1536]{1,0:T(8,128)(2,1)S(1)}, bf16[512,1536]{1,0:T(8,128)(2,1)S(1)}, u32[]{:S(2)}, u32[]{:S(2)}) collective-permute-start(bf16[512,1536]{1,0:T(8,128)(2,1)S(1)} %multiply_convert_fusion), channel_id=1, source_target_pairs={{0,1},{1,0},{2,3},{3,2},{4,5},{5,4},{6,7},{7,6},{8,9},{9,8},{10,11... | collective-permute-start | bytes 4718600 | tf_op jit(solution)/shard_map/ppermute | solution.py:500
  313.8 3.6 collective-permute-start.23
  324.4 32.7 %experts.2 = (bf16[1024,1536]{1,0:T(8,128)(2,1)}, bf16[1024,1536]{1,0:T(8,128)(2,1)}, f32[1024,128]{1,0:T(8,128)}, f32[1024,128]{1,0:T(8,128)}, bf16[2,1024,512]...) custom-call(s32[2]{0:T(128)} %multiply_add_fusion.1.s_ref, bf16[1024,1536]{1,0:T(8,128)(2,1)} %pad_maximum_fusion.6.h_ref, ...), custom_call_target="tpu_custom_call" | custom-call | tf_op jit(solution)/shard_map/experts/pallas_call | solution.py:381
  357.2 3.7 pad_maximum_fusion.11.h_ref
  360.9 33.1 %experts.3 = (bf16[1024,1536]{1,0:T(8,128)(2,1)}, bf16[1024,1536]{1,0:T(8,128)(2,1)}, f32[1024,128]{1,0:T(8,128)}, f32[1024,128]{1,0:T(8,128)}, bf16[2,1024,512]...) custom-call(s32[2]{0:T(128)} %multiply_add_fusion.1.s_ref, bf16[1024,1536]{1,0:T(8,128)(2,1)} %pad_maximum_fusion.11.h_ref, ...), custom_call_target="tpu_custom_call" | custom-call | tf_op jit(solution)/shard_map/experts/pallas_call | solution.py:381
  396.2 3.8 pad_maximum_fusion.5.act_ref
  400.0 7.8 pad_maximum_fusion.dgu_ref
  407.8 5.6 pad_maximum_fusion.3.h_ref
  413.5 35.2 %expert_grads.1 = bf16[2,1536,1536]{2,1,0:T(8,128)(2,1)} custom-call(s32[2]{0:T(128)} %multiply_add_fusion.1.s_ref, bf16[2048,1536]{1,0:T(8,128)(2,1)} %pad_maximum_fusion.3.h_ref, bf16[2048,1536]{1,0:T(8,128)(2,1)} %pad_maximum_fusion.4.dy_ref, f32[2048,128]{1,0:T(8,128)} %pad_maximum_fusion.16.gates_ref, bf16[2,2048,512]{2,1,0:T(8,128)(2,1)} %pad_maximum_fusion.5.act_ref, ...), custom_call_target="tpu_custom_call" | custom-call | tf_op jit(solution)/shard_map/expert_grads/pallas_call | solution.py:449
  462.3 35.8 %collective-permute-done.32 = f32[512,128]{1,0:T(8,128)} collective-permute-done((f32[512,128]{1,0:T(8,128)}, f32[512,128]{1,0:T(8,128)}, u32[]{:S(2)}, u32[]{:S(2)}) %collective-permute-start.32) | collective-permute-done | bytes 262176 | tf_op jit(solution)/shard_map/ppermute | solution.py:504
  500.6 4.9 multiply_reduce_fusion.1
  505.5 4.7 fusion.22
  510.7 35.5 %collective-permute-done.37 = bf16[512,1536]{1,0:T(8,128)(2,1)} collective-permute-done((bf16[512,1536]{1,0:T(8,128)(2,1)}, bf16[512,1536]{1,0:T(8,128)(2,1)}, u32[]{:S(2)}, u32[]{:S(2)}) %collective-permute-start.37) | collective-permute-done | bytes 1572896 | tf_op jit(solution)/shard_map/ppermute | solution.py:501
  549.9 6.9 convolution_convert_fusion.8
  556.9 53.8 %reduce-scatter.12.cloned.1.call-done = bf16[768,1536]{1,0:T(8,128)(2,1)} async-done(((bf16[3072,1536]{1,0:T(8,128)(2,1)}), bf16[768,1536]{1,0:T(8,128)(2,1)}) %reduce-scatter.12.cloned.1.call-update) | async-done | bytes 2359312 | tf_op jit(solution)/shard_map/reduce_scatter | solution.py:670
  611.2 6.5 fusion.9.do_ref
  617.7 45.8 %attend_back.1 = (bf16[384,2048]{1,0:T(8,128)(2,1)}, bf16[256,2048]{1,0:T(8,128)(2,1)}) custom-call(s32[9]{0:T(128)} %pad_add_fusion.2.s_ref, bf16[384,2048]{1,0:T(8,128)(2,1)} %get-tuple-element.33.q_ref, bf16[384,2048]{1,0:T(8,128)(2,1)} %get-tuple-element.36.o_ref, bf16[384,2048]{1,0:T(8,128)(2,1)} %fusion.9.do_ref, f32[6,2048]{1,0:T(8,128)} %get-tuple-element.43.lse_ref, ...), custom_call_target="tpu_custom_call" | custom-call | tf_op jit(solution)/shard_map/attend_back/pallas_call | solution.py:274
  670.2 2.7 convolution_convert_fusion.2
  672.9 6.3 fusion.24
  679.2 4.0 copy.79
  683.2 4.3 add_convert_fusion
  690.0 2.9 add_convert_fusion.2
  694.4 18.4 %reduce-scatter.18.cloned.1.call-done = f32[48,9]{1,0:T(8,128)} async-done(((f32[1536,9]{1,0:T(8,128)}), f32[48,9]{1,0:T(8,128)}) %reduce-scatter.18.cloned.1.call-update) | async-done | bytes 1744
  718.3 48.8 %all-reduce.1 = f32[1536]{0:T(1024)} all-reduce(f32[1536]{0:T(1024)} %div.29), channel_id=2, replica_groups=mesh['z'=4,'y'=2,'x'=2,'c'=2] {'z','y','x','c'}, use_global_device_ids=true, to_apply=%region_8.9.clone | all-reduce | flops 1536 | bytes 12288
  768.4 11.2 %reduce-scatter.10.cloned.1.call-done = bf16[192,384]{1,0:T(8,128)(2,1)} async-done(((bf16[1536,384]{1,0:T(8,128)(2,1)}), bf16[192,384]{1,0:T(8,128)(2,1)}) %reduce-scatter.10.cloned.1.call-update) | async-done | bytes 147472 | tf_op jit(solution)/shard_map/reduce_scatter | solution.py:656
  781.2 5.8 fusion.4
  787.0 27.2 %reduce-scatter.14.cloned.1.call-done = bf16[384,1536]{1,0:T(8,128)(2,1)} async-done(((bf16[768,1536]{1,0:T(8,128)(2,1)}), bf16[384,1536]{1,0:T(8,128)(2,1)}) %reduce-scatter.14.cloned.1.call-update) | async-done | bytes 1179664 | tf_op jit(solution)/shard_map/reduce_scatter | solution.py:673
  814.2 3.0 collective-permute-start.42
  817.3 9.6 %fusion.7 = (f32[512,1536]{1,0:T(8,128)}, f32[512,1536]{1,0:T(8,128)}) fusion(bf16[512,1536]{1,0:T(8,128)(2,1)S(1)} %copy-done.5, bf16[512,1536]{1,0:T(8,128)(2,1)} %collective-permute-done.41, bf16[512,1536]{1,0:T(8,128)(2,1)} %collective-permute-done.39, bf16[512,1536]{1,0:T(8,128)(2,1)} %get-tuple-element.132, f32[512]{0:T(512)S(1)} %broadcast_multiply_fusion, ...), kind=kLoop, calls=%fused_computation.17 | loop fusion | flops 19660800 | bytes 25186304 | tf_op jit(solution)/shard_map/add | solution.py:648
  826.9 65.3 %reduce-scatter.16.cloned.1.call-done = bf16[192,640]{1,0:T(8,128)(2,1)} async-done(((bf16[1536,640]{1,0:T(8,128)(2,1)}), bf16[192,640]{1,0:T(8,128)(2,1)}) %reduce-scatter.16.cloned.1.call-update) | async-done | bytes 245776
  (228 shorter events, 101.6 us)
Async XLA Ops:
  7.2 603.5 %reduce-scatter.12.cloned.1.call-start = ((), (), s32[]{:S(2)}) async-start(), calls=%async_computation.6 | async-start | bytes 11796480 | tf_op jit(solution)/shard_map/reduce_scatter | solution.py:670
  11.5 36.5 %collective-permute-start.1 = (bf16[512,1536]{1,0:T(8,128)(2,1)}, bf16[512,1536]{1,0:T(8,128)(2,1)}, u32[]{:S(2)}, u32[]{:S(2)}) collective-permute-start(bf16[512,1536]{1,0:T(8,128)(2,1)} %fusion.3), channel_id=1, source_target_pairs={{0,2},{2,0},{1,3},{3,1},{4,6},{6,4},{5,7},{7,5},{8,10},{10,8},{9,1... | collective-permute-start | bytes 4718600 | tf_op jit(solution)/shard_map/ppermute | solution.py:501
  11.5 78.3 %collective-permute-start = (bf16[512,1536]{1,0:T(8,128)(2,1)}, bf16[512,1536]{1,0:T(8,128)(2,1)}, u32[]{:S(2)}, u32[]{:S(2)}) collective-permute-start(bf16[512,1536]{1,0:T(8,128)(2,1)} %fusion.3), channel_id=1, source_target_pairs={{0,1},{1,0},{2,3},{3,2},{4,5},{5,4},{6,7},{7,6},{8,9},{9,8},{10,11... | collective-permute-start | bytes 4718600 | tf_op jit(solution)/shard_map/ppermute | solution.py:500
  48.0 47.7 %collective-permute-start.2 = (bf16[512,1536]{1,0:T(8,128)(2,1)}, bf16[512,1536]{1,0:T(8,128)(2,1)}, u32[]{:S(2)}, u32[]{:S(2)}) collective-permute-start(bf16[512,1536]{1,0:T(8,128)(2,1)} %collective-permute-done.1), channel_id=1, source_target_pairs={{0,1},{1,0},{2,3},{3,2},{4,5},{5,4},{6,7},{7,6},{8,9},{9,8},{10,11... | collective-permute-start | bytes 4718600 | tf_op jit(solution)/shard_map/ppermute | solution.py:500
  48.0 104.1 %collective-permute-start.24 = (bf16[512,1536]{1,0:T(8,128)(2,1)}, bf16[512,1536]{1,0:T(8,128)(2,1)}, u32[]{:S(2)}, u32[]{:S(2)}) collective-permute-start(bf16[512,1536]{1,0:T(8,128)(2,1)} %param.29), channel_id=1, source_target_pairs={{0,4},{4,0},{1,5},{5,1},{2,6},{6,2},{3,7},{7,3},{8,12},{12,8},{9,1... | collective-permute-start | bytes 4718600 | tf_op jit(solution)/shard_map/ppermute | solution.py:504
  49.5 106.7 %collective-permute-start.7 = (bf16[512,1536]{1,0:T(8,128)(2,1)}, bf16[512,1536]{1,0:T(8,128)(2,1)}, u32[]{:S(2)}, u32[]{:S(2)}) collective-permute-start(bf16[512,1536]{1,0:T(8,128)(2,1)} %param.29), channel_id=1, source_target_pairs={{0,1},{1,0},{2,3},{3,2},{4,5},{5,4},{6,7},{7,6},{8,9},{9,8},{10,11... | collective-permute-start | bytes 4718600 | tf_op jit(solution)/shard_map/ppermute | solution.py:500
  49.7 35.5 %collective-permute-start.26 = (s32[512,4]{0,1:T(4,128)S(1)}, s32[512,4]{0,1:T(4,128)S(1)}, u32[]{:S(2)}, u32[]{:S(2)}) collective-permute-start(s32[512,4]{0,1:T(4,128)S(1)} %copy-done.32), channel_id=1, source_target_pairs={{0,4},{4,0},{1,5},{5,1},{2,6},{6,2},{3,7},{7,3},{8,12},{12,8},{9,1... | collective-permute-start | bytes 24584 | tf_op jit(solution)/shard_map/ppermute | solution.py:504
  85.2 66.9 %collective-permute-start.13 = (bf16[1,1536,512]{2,1,0:T(8,128)(2,1)}, bf16[1,1536,512]{2,1,0:T(8,128)(2,1)}, u32[]{:S(2)}, u32[]{:S(2)}) collective-permute-start(bf16[1,1536,512]{2,1,0:T(8,128)(2,1)} %param.24), channel_id=1, source_target_pairs={{0,8},{8,16},{25,17},{17,9},{2,10},{10,18},{27,19},{19,11},{4,12},... | collective-permute-start | bytes 4718600 | tf_op jit(solution)/shard_map/ppermute | solution.py:549
  89.8 64.1 %collective-permute-start.9 = (bf16[1,1536,512]{2,1,0:T(8,128)(2,1)}, bf16[1,1536,512]{2,1,0:T(8,128)(2,1)}, u32[]{:S(2)}, u32[]{:S(2)}) collective-permute-start(bf16[1,1536,512]{2,1,0:T(8,128)(2,1)} %param.23), channel_id=1, source_target_pairs={{0,8},{8,16},{25,17},{17,9},{2,10},{10,18},{27,19},{19,11},{4,12},... | collective-permute-start | bytes 4718600 | tf_op jit(solution)/shard_map/ppermute | solution.py:549
  95.7 50.2 %collective-permute-start.8 = (s32[512,4]{0,1:T(4,128)S(1)}, s32[512,4]{0,1:T(4,128)S(1)}, u32[]{:S(2)}, u32[]{:S(2)}) collective-permute-start(s32[512,4]{0,1:T(4,128)S(1)} %copy-done.32), channel_id=1, source_target_pairs={{0,1},{1,0},{2,3},{3,2},{4,5},{5,4},{6,7},{7,6},{8,9},{9,8},{10,11... | collective-permute-start | bytes 24584 | tf_op jit(solution)/shard_map/ppermute | solution.py:500
  145.9 3.7 collective-permute-start.27
  149.6 19.5 %collective-permute-start.17 = (bf16[1,512,1536]{2,1,0:T(8,128)(2,1)}, bf16[1,512,1536]{2,1,0:T(8,128)(2,1)}, u32[]{:S(2)}, u32[]{:S(2)}) collective-permute-start(bf16[1,512,1536]{2,1,0:T(8,128)(2,1)} %param.25), channel_id=1, source_target_pairs={{0,8},{8,16},{25,17},{17,9},{2,10},{10,18},{27,19},{19,11},{4,12},... | collective-permute-start | bytes 4718600 | tf_op jit(solution)/shard_map/ppermute | solution.py:549
  152.1 18.3 %collective-permute-start.25 = (bf16[512,1536]{1,0:T(8,128)(2,1)}, bf16[512,1536]{1,0:T(8,128)(2,1)}, u32[]{:S(2)}, u32[]{:S(2)}) collective-permute-start(bf16[512,1536]{1,0:T(8,128)(2,1)} %collective-permute-done.24), channel_id=1, source_target_pairs={{0,1},{1,0},{2,3},{3,2},{4,5},{5,4},{6,7},{7,6},{8,9},{9,8},{10,11... | collective-permute-start | bytes 4718600 | tf_op jit(solution)/shard_map/ppermute | solution.py:500
  152.1 19.6 %collective-permute-start.14 = (bf16[1,1536,512]{2,1,0:T(8,128)(2,1)}, bf16[1,1536,512]{2,1,0:T(8,128)(2,1)}, u32[]{:S(2)}, u32[]{:S(2)}) collective-permute-start(bf16[1,1536,512]{2,1,0:T(8,128)(2,1)} %collective-permute-done.13), channel_id=1, source_target_pairs={{8,16},{16,24},{17,9},{9,1},{10,18},{18,26},{19,11},{11,3},{12,20}... | collective-permute-start | bytes 4718600 | tf_op jit(solution)/shard_map/ppermute | solution.py:551
  153.9 18.6 %collective-permute-start.10 = (bf16[1,1536,512]{2,1,0:T(8,128)(2,1)}, bf16[1,1536,512]{2,1,0:T(8,128)(2,1)}, u32[]{:S(2)}, u32[]{:S(2)}) collective-permute-start(bf16[1,1536,512]{2,1,0:T(8,128)(2,1)} %collective-permute-done.9), channel_id=1, source_target_pairs={{8,16},{16,24},{17,9},{9,1},{10,18},{18,26},{19,11},{11,3},{12,20}... | collective-permute-start | bytes 4718600 | tf_op jit(solution)/shard_map/ppermute | solution.py:551
  156.2 17.1 %collective-permute-start.4 = (bf16[512,1536]{1,0:T(8,128)(2,1)}, bf16[512,1536]{1,0:T(8,128)(2,1)}, u32[]{:S(2)}, u32[]{:S(2)}) collective-permute-start(bf16[512,1536]{1,0:T(8,128)(2,1)} %convolution_convert_fusion.4), channel_id=1, source_target_pairs={{0,1},{1,0},{2,3},{3,2},{4,5},{5,4},{6,7},{7,6},{8,9},{9,8},{10,11... | collective-permute-start | bytes 4718600 | tf_op jit(solution)/shard_map/ppermute | solution.py:500
  169.1 39.4 %collective-permute-start.16 = (bf16[1,1536,512]{2,1,0:T(8,128)(2,1)}, bf16[1,1536,512]{2,1,0:T(8,128)(2,1)S(1)}, u32[]{:S(2)}, u32[]{:S(2)}) collective-permute-start(bf16[1,1536,512]{2,1,0:T(8,128)(2,1)} %param.24), channel_id=1, source_target_pairs={{8,0},{17,25},{10,2},{19,27},{12,4},{21,29},{14,6},{23,31}} | collective-permute-start | bytes 4718600 | tf_op jit(solution)/shard_map/ppermute | solution.py:550
  170.4 71.8 %collective-permute-start.12 = (bf16[1,1536,512]{2,1,0:T(8,128)(2,1)}, bf16[1,1536,512]{2,1,0:T(8,128)(2,1)S(1)}, u32[]{:S(2)}, u32[]{:S(2)}) collective-permute-start(bf16[1,1536,512]{2,1,0:T(8,128)(2,1)} %param.23), channel_id=1, source_target_pairs={{8,0},{17,25},{10,2},{19,27},{12,4},{21,29},{14,6},{23,31}} | collective-permute-start | bytes 4718600 | tf_op jit(solution)/shard_map/ppermute | solution.py:550
  171.7 70.5 %collective-permute-start.18 = (bf16[1,512,1536]{2,1,0:T(8,128)(2,1)}, bf16[1,512,1536]{2,1,0:T(8,128)(2,1)S(1)}, u32[]{:S(2)}, u32[]{:S(2)}) collective-permute-start(bf16[1,512,1536]{2,1,0:T(8,128)(2,1)} %collective-permute-done.17), channel_id=1, source_target_pairs={{8,16},{16,24},{17,9},{9,1},{10,18},{18,26},{19,11},{11,3},{12,20}... | collective-permute-start | bytes 4718600 | tf_op jit(solution)/shard_map/ppermute | solution.py:551
  172.5 71.6 %collective-permute-start.15 = (bf16[1,1536,512]{2,1,0:T(8,128)(2,1)}, bf16[1,1536,512]{2,1,0:T(8,128)(2,1)S(1)}, u32[]{:S(2)}, u32[]{:S(2)}) collective-permute-start(bf16[1,1536,512]{2,1,0:T(8,128)(2,1)} %collective-permute-done.14), channel_id=1, source_target_pairs={{16,24},{9,1},{18,26},{11,3},{20,28},{13,5},{22,30},{15,7}} | collective-permute-start | bytes 4718600 | tf_op jit(solution)/shard_map/ppermute | solution.py:552
  173.3 71.4 %collective-permute-start.11 = (bf16[1,1536,512]{2,1,0:T(8,128)(2,1)}, bf16[1,1536,512]{2,1,0:T(8,128)(2,1)S(1)}, u32[]{:S(2)}, u32[]{:S(2)}) collective-permute-start(bf16[1,1536,512]{2,1,0:T(8,128)(2,1)} %collective-permute-done.10), channel_id=1, source_target_pairs={{16,24},{9,1},{18,26},{11,3},{20,28},{13,5},{22,30},{15,7}} | collective-permute-start | bytes 4718600 | tf_op jit(solution)/shard_map/ppermute | solution.py:552
  208.6 67.4 %collective-permute-start.20 = (bf16[1,512,1536]{2,1,0:T(8,128)(2,1)}, bf16[1,512,1536]{2,1,0:T(8,128)(2,1)S(1)}, u32[]{:S(2)}, u32[]{:S(2)}) collective-permute-start(bf16[1,512,1536]{2,1,0:T(8,128)(2,1)} %param.25), channel_id=1, source_target_pairs={{8,0},{17,25},{10,2},{19,27},{12,4},{21,29},{14,6},{23,31}} | collective-permute-start | bytes 4718600 | tf_op jit(solution)/shard_map/ppermute | solution.py:550
  242.3 6.8 collective-permute-start.3
  242.3 33.7 %collective-permute-start.19 = (bf16[1,512,1536]{2,1,0:T(8,128)(2,1)S(1)}, bf16[1,512,1536]{2,1,0:T(8,128)(2,1)}, u32[]{:S(2)}, u32[]{:S(2)}) collective-permute-start(bf16[1,512,1536]{2,1,0:T(8,128)(2,1)S(1)} %collective-permute-done.18), channel_id=1, source_target_pairs={{16,24},{9,1},{18,26},{11,3},{20,28},{13,5},{22,30},{15,7}} | collective-permute-start | bytes 4718600 | tf_op jit(solution)/shard_map/ppermute | solution.py:552
  244.1 20.4 %collective-permute-start.5 = (bf16[512,1536]{1,0:T(8,128)(2,1)S(1)}, bf16[512,1536]{1,0:T(8,128)(2,1)S(1)}, u32[]{:S(2)}, u32[]{:S(2)}) collective-permute-start(bf16[512,1536]{1,0:T(8,128)(2,1)S(1)} %add_convert_fusion.3), channel_id=1, source_target_pairs={{0,2},{2,0},{1,3},{3,1},{4,6},{6,4},{5,7},{7,5},{8,10},{10,8},{9,1... | collective-permute-start | bytes 4718600 | tf_op jit(solution)/shard_map/ppermute | solution.py:501
  266.1 47.7 %collective-permute-start.22 = (bf16[512,1536]{1,0:T(8,128)(2,1)S(1)}, bf16[512,1536]{1,0:T(8,128)(2,1)}, u32[]{:S(2)}, u32[]{:S(2)}) collective-permute-start(bf16[512,1536]{1,0:T(8,128)(2,1)S(1)} %multiply_convert_fusion), channel_id=1, source_target_pairs={{0,4},{4,0},{1,5},{5,1},{2,6},{6,2},{3,7},{7,3},{8,12},{12,8},{9,1... | collective-permute-start | bytes 4718600 | tf_op jit(solution)/shard_map/ppermute | solution.py:504
  278.9 42.5 %collective-permute-start.6 = (bf16[512,1536]{1,0:T(8,128)(2,1)S(1)}, bf16[512,1536]{1,0:T(8,128)(2,1)S(1)}, u32[]{:S(2)}, u32[]{:S(2)}) collective-permute-start(bf16[512,1536]{1,0:T(8,128)(2,1)S(1)} %multiply_convert_fusion), channel_id=1, source_target_pairs={{0,1},{1,0},{2,3},{3,2},{4,5},{5,4},{6,7},{7,6},{8,9},{9,8},{10,11... | collective-permute-start | bytes 4718600 | tf_op jit(solution)/shard_map/ppermute | solution.py:500
  313.8 43.3 %collective-permute-start.23 = (bf16[512,1536]{1,0:T(8,128)(2,1)}, bf16[512,1536]{1,0:T(8,128)(2,1)}, u32[]{:S(2)}, u32[]{:S(2)}) collective-permute-start(bf16[512,1536]{1,0:T(8,128)(2,1)} %collective-permute-done.22), channel_id=1, source_target_pairs={{0,1},{1,0},{2,3},{3,2},{4,5},{5,4},{6,7},{7,6},{8,9},{9,8},{10,11... | collective-permute-start | bytes 4718600 | tf_op jit(solution)/shard_map/ppermute | solution.py:500
  448.7 264.1 %reduce-scatter.18.cloned.1.call-start = ((), (), s32[]{:S(2)}) async-start(), calls=%async_computation.9 | async-start | bytes 811008
  450.7 3.5 collective-permute-start.34
  452.6 47.9 %collective-permute-start.33 = (bf16[512,1536]{1,0:T(8,128)(2,1)}, bf16[512,1536]{1,0:T(8,128)(2,1)}, u32[]{:S(2)}, u32[]{:S(2)}) collective-permute-start(bf16[512,1536]{1,0:T(8,128)(2,1)} %slice.109), channel_id=1, source_target_pairs={{0,1},{1,0},{2,3},{3,2},{4,5},{5,4},{6,7},{7,6},{8,9},{9,8},{10,11... | collective-permute-start | bytes 4718600 | tf_op jit(solution)/shard_map/ppermute | solution.py:500
  455.7 44.9 %collective-permute-start.35 = (bf16[512,1536]{1,0:T(8,128)(2,1)}, bf16[512,1536]{1,0:T(8,128)(2,1)}, u32[]{:S(2)}, u32[]{:S(2)}) collective-permute-start(bf16[512,1536]{1,0:T(8,128)(2,1)} %add_convert_fusion.1), channel_id=1, source_target_pairs={{0,4},{4,0},{1,5},{5,1},{2,6},{6,2},{3,7},{7,3},{8,12},{12,8},{9,1... | collective-permute-start | bytes 4718600 | tf_op jit(solution)/shard_map/ppermute | solution.py:504
  457.2 1.6 collective-permute-start.31
  458.1 4.2 collective-permute-start.30
  459.6 38.5 %collective-permute-start.32 = (f32[512,128]{1,0:T(8,128)}, f32[512,128]{1,0:T(8,128)}, u32[]{:S(2)}, u32[]{:S(2)}) collective-permute-start(f32[512,128]{1,0:T(8,128)} %slice_add_fusion.2), channel_id=1, source_target_pairs={{0,4},{4,0},{1,5},{5,1},{2,6},{6,2},{3,7},{7,3},{8,12},{12,8},{9,1... | collective-permute-start | bytes 786440 | tf_op jit(solution)/shard_map/ppermute | solution.py:504
  510.2 36.0 %collective-permute-start.37 = (bf16[512,1536]{1,0:T(8,128)(2,1)}, bf16[512,1536]{1,0:T(8,128)(2,1)}, u32[]{:S(2)}, u32[]{:S(2)}) collective-permute-start(bf16[512,1536]{1,0:T(8,128)(2,1)} %fusion.22), channel_id=1, source_target_pairs={{0,2},{2,0},{1,3},{3,1},{4,6},{6,4},{5,7},{7,5},{8,10},{10,8},{9,1... | collective-permute-start | bytes 4718600 | tf_op jit(solution)/shard_map/ppermute | solution.py:501
  510.7 37.1 %collective-permute-start.36 = (bf16[512,1536]{1,0:T(8,128)(2,1)}, bf16[512,1536]{1,0:T(8,128)(2,1)}, u32[]{:S(2)}, u32[]{:S(2)}) collective-permute-start(bf16[512,1536]{1,0:T(8,128)(2,1)} %fusion.22), channel_id=1, source_target_pairs={{0,1},{1,0},{2,3},{3,2},{4,5},{5,4},{6,7},{7,6},{8,9},{9,8},{10,11... | collective-permute-start | bytes 4718600 | tf_op jit(solution)/shard_map/ppermute | solution.py:500
  546.2 3.8 collective-permute-start.38
  547.7 231.8 %reduce-scatter.10.cloned.1.call-start = ((), (), s32[]{:S(2)}) async-start(), calls=%async_computation.5 | async-start | bytes 1327104 | tf_op jit(solution)/shard_map/reduce_scatter | solution.py:656
  556.8 257.4 %reduce-scatter.14.cloned.1.call-start = ((), (), s32[]{:S(2)}) async-start(), calls=%async_computation.7 | async-start | bytes 3538944 | tf_op jit(solution)/shard_map/reduce_scatter | solution.py:673
  610.7 281.5 %reduce-scatter.16.cloned.1.call-start = ((), (), s32[]{:S(2)}) async-start(), calls=%async_computation.8 | async-start | bytes 2211840
  668.4 14.8 %collective-permute-start.40 = (bf16[512,1536]{1,0:T(8,128)(2,1)}, bf16[512,1536]{1,0:T(8,128)(2,1)}, u32[]{:S(2)}, u32[]{:S(2)}) collective-permute-start(bf16[512,1536]{1,0:T(8,128)(2,1)} %convolution_convert_fusion), channel_id=1, source_target_pairs={{0,1},{1,0},{2,3},{3,2},{4,5},{5,4},{6,7},{7,6},{8,9},{9,8},{10,11... | collective-permute-start | bytes 4718600 | tf_op jit(solution)/shard_map/ppermute | solution.py:500
  669.7 19.9 %collective-permute-start.28 = (bf16[512,1536]{1,0:T(8,128)(2,1)}, bf16[512,1536]{1,0:T(8,128)(2,1)}, u32[]{:S(2)}, u32[]{:S(2)}) collective-permute-start(bf16[512,1536]{1,0:T(8,128)(2,1)} %slice.102), channel_id=1, source_target_pairs={{0,1},{1,0},{2,3},{3,2},{4,5},{5,4},{6,7},{7,6},{8,9},{9,8},{10,11... | collective-permute-start | bytes 4718600 | tf_op jit(solution)/shard_map/ppermute | solution.py:500
  672.9 108.3 %collective-permute-start.39 = (bf16[512,1536]{1,0:T(8,128)(2,1)}, bf16[512,1536]{1,0:T(8,128)(2,1)}, u32[]{:S(2)}, u32[]{:S(2)}) collective-permute-start(bf16[512,1536]{1,0:T(8,128)(2,1)} %convolution_convert_fusion.2), channel_id=1, source_target_pairs={{0,1},{1,0},{2,3},{3,2},{4,5},{5,4},{6,7},{7,6},{8,9},{9,8},{10,11... | collective-permute-start | bytes 4718600 | tf_op jit(solution)/shard_map/ppermute | solution.py:500
  687.6 93.6 %collective-permute-start.41 = (bf16[512,1536]{1,0:T(8,128)(2,1)}, bf16[512,1536]{1,0:T(8,128)(2,1)}, u32[]{:S(2)}, u32[]{:S(2)}) collective-permute-start(bf16[512,1536]{1,0:T(8,128)(2,1)} %add_convert_fusion), channel_id=1, source_target_pairs={{0,2},{2,0},{1,3},{3,1},{4,6},{6,4},{5,7},{7,5},{8,10},{10,8},{9,1... | collective-permute-start | bytes 4718600 | tf_op jit(solution)/shard_map/ppermute | solution.py:501
  689.4 127.8 %collective-permute-start.21 = (bf16[512,1536]{1,0:T(8,128)(2,1)}, bf16[512,1536]{1,0:T(8,128)(2,1)}, u32[]{:S(2)}, u32[]{:S(2)}) collective-permute-start(bf16[512,1536]{1,0:T(8,128)(2,1)} %slice.100), channel_id=1, source_target_pairs={{0,1},{1,0},{2,3},{3,2},{4,5},{5,4},{6,7},{7,6},{8,9},{9,8},{10,11... | collective-permute-start | bytes 4718600 | tf_op jit(solution)/shard_map/ppermute | solution.py:500
  693.0 124.3 %collective-permute-start.29 = (bf16[512,1536]{1,0:T(8,128)(2,1)}, bf16[512,1536]{1,0:T(8,128)(2,1)}, u32[]{:S(2)}, u32[]{:S(2)}) collective-permute-start(bf16[512,1536]{1,0:T(8,128)(2,1)} %add_convert_fusion.2), channel_id=1, source_target_pairs={{0,4},{4,0},{1,5},{5,1},{2,6},{6,2},{3,7},{7,3},{8,12},{12,8},{9,1... | collective-permute-start | bytes 4718600 | tf_op jit(solution)/shard_map/ppermute | solution.py:504
  814.2 81.6 %collective-permute-start.42 = (bf16[384,1536]{1,0:T(8,128)(2,1)}, bf16[384,1536]{1,0:T(8,128)(2,1)}, u32[]{:S(2)}, u32[]{:S(2)}) collective-permute-start(bf16[384,1536]{1,0:T(8,128)(2,1)} %reduce-scatter.14.cloned.1.call-done), channel_id=1, source_target_pairs={{0,0},{1,16},{2,1},{3,17},{8,2},{9,18},{10,3},{11,19},{16,8},{17,2... | collective-permute-start | bytes 3538952 | tf_op jit(solution)/shard_map/ppermute | solution.py:679
  (37 other events, 897.6 us)
Sparse Core Ops, SparseCore 0:
  448.9 161.8 reduce-scatter.11
  616.4 96.4 reduce-scatter.17
  716.3 63.2 reduce-scatter.9
  781.6 32.5 reduce-scatter.13
  817.9 74.2 reduce-scatter.15

commit v2 on v1

v2 whole, which is shorter than its diff:
```python
import functools
import math

import jax
import jax.numpy as jnp
from jax import lax
from jax.experimental import pallas as pl
from jax.experimental.pallas import tpu as pltpu
from jax.sharding import Mesh, PartitionSpec as P

HEAD_SIZE = 64
HALF = HEAD_SIZE // 2
SEQUENCE_LENGTH = 2048
EPSILON = 1e-05
ROPE_BASE = 10000.0
MASK_FILL = -1e30
LANES = 128
F32 = jnp.float32
BF16 = jnp.bfloat16
VMEM_LIMIT = 60 * 1024 * 1024


def dot(a, b, ca=1, cb=0):
    return lax.dot_general(a, b, (((ca,), (cb,)), ((), ())), preferred_element_type=F32)


def after(value, *deps):
    return lax.optimization_barrier((value, *deps))[0]


def cost(micros):
    return pl.CostEstimate(
        flops=int(micros * 1e9), transcendentals=0, bytes_accessed=int(micros * 3e6)
    )


def params():
    return pltpu.CompilerParams(vmem_limit_bytes=VMEM_LIMIT)


def once(shape):
    return pl.BlockSpec(shape, lambda *_: (0,) * len(shape), pipeline_mode=pl.Buffered(1))


def qkv_kernel(q_cols, kv_cols, parts, *refs):
    h_refs, (w_ref, cos_ref, sin_ref) = refs[:parts], refs[parts : parts + 3]
    q_ref, k_ref, kt_ref, v_ref, vt_ref = refs[-5:]
    rows = h_refs[0].shape[0]
    scale = jnp.asarray(1.0 / math.sqrt(HEAD_SIZE), BF16)
    for b in range(parts):
        here = slice(b * rows, (b + 1) * rows)
        y = dot(w_ref[...], h_refs[b][...], 1, 1)
        cos, sin = cos_ref[:, here], sin_ref[:, here]

        def turned(base):
            a = y[base : base + HALF]
            b = y[base + HALF : base + HEAD_SIZE]
            return jnp.concatenate([a * cos - b * sin, b * cos + a * sin], axis=0)

        for h in range(q_cols // HEAD_SIZE):
            base = h * HEAD_SIZE
            q_ref[base : base + HEAD_SIZE, here] = turned(base).astype(BF16) * scale
        for g in range(kv_cols // HEAD_SIZE):
            base = g * HEAD_SIZE
            kt = turned(q_cols + base)
            kt_ref[base : base + HEAD_SIZE, here] = kt.astype(BF16)
            k_ref[g, here, :] = kt.T.astype(BF16)
            vt = y[q_cols + kv_cols + base : q_cols + kv_cols + base + HEAD_SIZE]
            vt_ref[base : base + HEAD_SIZE, here] = vt.astype(BF16)
            v_ref[g, here, :] = vt.T.astype(BF16)


def project_qkv(h_parts, w_all, cos, sin, q_cols, kv_cols, half, previous):
    parts = len(h_parts)
    rows, width = h_parts[0].shape
    size = parts * rows
    groups = kv_cols // HEAD_SIZE
    cols = q_cols + 2 * kv_cols
    lane_block = lambda *_: (0, half)
    row_block = lambda *_: (0, half, 0)
    kv_shapes = [
        jax.ShapeDtypeStruct((groups, 2 * size, HEAD_SIZE), BF16),
        jax.ShapeDtypeStruct((kv_cols, 2 * size), BF16),
    ] * 2
    kv_specs = [
        pl.BlockSpec((groups, size, HEAD_SIZE), row_block),
        pl.BlockSpec((kv_cols, size), lane_block),
    ] * 2
    previous = list(previous or ())
    return pl.pallas_call(
        functools.partial(qkv_kernel, q_cols, kv_cols, parts),
        grid=(1,),
        in_specs=[once((rows, width))] * parts
        + [
            once((cols, width)),
            pl.BlockSpec((HALF, size), lane_block),
            pl.BlockSpec((HALF, size), lane_block),
        ]
        + [pl.BlockSpec(memory_space=pl.ANY)] * len(previous),
        out_specs=[once((q_cols, size))] + kv_specs,
        out_shape=[jax.ShapeDtypeStruct((q_cols, size), BF16)] + kv_shapes,
        input_output_aliases={parts + 3 + i: 1 + i for i in range(len(previous))},
        compiler_params=params(),
        cost_estimate=cost(6),
        name="qkv",
    )(*h_parts, w_all, cos, sin, *previous)


def last_key(s_ref, zone, own, rows):
    zone_index = own * rows // zone
    zones = SEQUENCE_LENGTH // zone
    start = s_ref[1 + zone_index]
    stop = start + s_ref[1 + zones + zone_index]
    position = own * rows + lax.broadcasted_iota(jnp.int32, (1, rows), 1)
    return jnp.where((position >= start) & (position < stop), stop - 1, position)


def block_walk(me, own, rows, zone, pair):
    per_zone = zone // rows
    pair(own, True, True)
    for other in range(1, per_zone):
        pair(own ^ other, True, False)
    first = (own // per_zone) * per_zone

    def step(key_block, carry):
        pair(key_block, False, False)
        return carry

    lax.fori_loop(0, first, step, 0)


def attend_kernel(
    rows, zone, heads, groups, base, s_ref, q_ref, k_ref, vt_ref, w_ref, o_ref, lse_ref, *refs
):
    out_refs, (acc, top, total) = refs[:-3], refs[-3:]
    me = s_ref[0]
    own = me ^ (pl.program_id(0) + base)
    limit = last_key(s_ref, zone, own, rows)

    def pair(key_block, masked, first):
        offset = pl.multiple_of((me ^ key_block) * rows, rows)
        if masked:
            key_pos = key_block * rows + lax.broadcasted_iota(jnp.int32, (rows, rows), 0)
            allowed = key_pos <= limit
        for h in range(heads):
            g = h // (heads // groups)
            r = slice(h * HEAD_SIZE, (h + 1) * HEAD_SIZE)
            s = dot(k_ref[g, pl.ds(offset, rows), :], q_ref[r, :])
            if masked:
                s = jnp.where(allowed, s, MASK_FILL)
            peak = jnp.max(s, axis=0, keepdims=True)
            vt = vt_ref[g * HEAD_SIZE : (g + 1) * HEAD_SIZE, pl.ds(offset, rows)]
            if first:
                p = jnp.exp(s - peak)
                top[h : h + 1, :] = peak
                total[h : h + 1, :] = jnp.sum(p, axis=0, keepdims=True)
                acc[r, :] = dot(vt, p.astype(BF16))
            else:
                old = top[h : h + 1, :]
                new = jnp.maximum(old, peak)
                fade = jnp.exp(old - new)
                p = jnp.exp(s - new)
                top[h : h + 1, :] = new
                total[h : h + 1, :] = total[h : h + 1, :] * fade + jnp.sum(p, axis=0, keepdims=True)
                acc[r, :] = acc[r, :] * fade + dot(vt, p.astype(BF16))

    block_walk(me, own, rows, zone, pair)
    for h in range(heads):
        r = slice(h * HEAD_SIZE, (h + 1) * HEAD_SIZE)
        o_ref[r, :] = (acc[r, :] / total[h : h + 1, :]).astype(BF16)
        lse_ref[h : h + 1, :] = top[h : h + 1, :] + jnp.log(total[h : h + 1, :])
    for b, out_ref in enumerate(out_refs):

        @pl.when(pl.program_id(0) == b)
        def _():
            out_ref[...] = dot(o_ref[...], w_ref[...], 0, 0).astype(BF16)


def attend(scalars, q, at, count, k, vt, w_out, rows, zone, base):
    q_cols = q.shape[0]
    size = count * rows
    groups = k.shape[0]
    width = w_out.shape[1]
    heads = q_cols // HEAD_SIZE
    block = lambda i, s: (0, i)
    return pl.pallas_call(
        functools.partial(attend_kernel, rows, zone, heads, groups, base),
        grid_spec=pltpu.PrefetchScalarGridSpec(
            num_scalar_prefetch=1,
            grid=(count,),
            in_specs=[
                pl.BlockSpec((q_cols, rows), lambda i, s: (0, i + at)),
                once(k.shape),
                once(vt.shape),
                once(w_out.shape),
            ],
            out_specs=[
                pl.BlockSpec((q_cols, rows), block),
                pl.BlockSpec((heads, rows), block),
            ]
            + [once((rows, width))] * count,
            scratch_shapes=[
                pltpu.VMEM((q_cols, rows), F32),
                pltpu.VMEM((8, rows), F32),
                pltpu.VMEM((8, rows), F32),
            ],
        ),
        out_shape=[
            jax.ShapeDtypeStruct((q_cols, size), BF16),
            jax.ShapeDtypeStruct((heads, size), F32),
        ]
        + [jax.ShapeDtypeStruct((rows, width), BF16)] * count,
        compiler_params=params(),
        cost_estimate=cost(9 * count),
        name="attend",
    )(scalars, q, k, vt, w_out)


def attend_back_kernel(rows, zone, heads, groups, base, parts, *refs):
    s_ref, q_ref, o_ref, lse_ref, k_ref, kt_ref, v_ref, cos_ref, sin_ref, w_ref = refs[:10]
    da_refs = refs[10 : 10 + parts]
    rest = refs[10 + parts :]
    if base:
        old_dk, old_dv, dq_ref, dkv_ref, dq, dk, dv, delta, do_ref = rest
    else:
        dq_ref, dk, dv, dq, delta, do_ref = rest
    me = s_ref[0]
    step = pl.program_id(0)
    own = me ^ (step + base)
    limit = last_key(s_ref, zone, own, rows)
    here = pl.multiple_of((step + base) * rows, rows)

    @pl.when(step == 0)
    def _():
        for b in range(parts):
            do_ref[b] = dot(w_ref[...], da_refs[b][...], 1, 1).astype(BF16)
        if base:
            dk[...] = old_dk[...]
            dv[...] = old_dv[...]
        else:
            dk[...] = jnp.zeros_like(dk)
            dv[...] = jnp.zeros_like(dv)

    for h in range(heads):
        r = slice(h * HEAD_SIZE, (h + 1) * HEAD_SIZE)
        delta[h : h + 1, :] = jnp.sum(
            do_ref[step, r, :].astype(F32) * o_ref[r, :].astype(F32), axis=0, keepdims=True
        )

    def pair(key_block, masked, first):
        offset = pl.multiple_of((me ^ key_block) * rows, rows)
        keys = pl.ds(offset, rows)
        if masked:
            key_pos = key_block * rows + lax.broadcasted_iota(jnp.int32, (rows, rows), 0)
            allowed = key_pos <= limit
        for g in range(groups):
            kb = k_ref[g, keys, :]
            vb = v_ref[g, keys, :]
            kt = kt_ref[g * HEAD_SIZE : (g + 1) * HEAD_SIZE, keys]
            dk_sum = dk[g, keys, :]
            dv_sum = dv[g, keys, :]
            for h in range(g * (heads // groups), (g + 1) * (heads // groups)):
                r = slice(h * HEAD_SIZE, (h + 1) * HEAD_SIZE)
                do = do_ref[step, r, :]
                s = dot(kb, q_ref[r, :])
                if masked:
                    s = jnp.where(allowed, s, MASK_FILL)
                p = jnp.exp(s - lse_ref[h : h + 1, :])
                dp = dot(vb, do)
                ds = (p * (dp - delta[h : h + 1, :])).astype(BF16)
                dv_sum = dv_sum + dot(p.astype(BF16), do, 1, 1)
                dk_sum = dk_sum + dot(ds, q_ref[r, :], 1, 1)
                part = dot(kt, ds)
                dq[r, :] = part if first else dq[r, :] + part
            dk[g, keys, :] = dk_sum
            dv[g, keys, :] = dv_sum

    block_walk(me, own, rows, zone, pair)
    cos, sin = cos_ref[:, pl.ds(here, rows)], sin_ref[:, pl.ds(here, rows)]
    scale = 1.0 / math.sqrt(HEAD_SIZE)
    for h in range(heads):
        at = h * HEAD_SIZE
        a = dq[at : at + HALF, :] * scale
        b = dq[at + HALF : at + HEAD_SIZE, :] * scale
        dq_ref[at : at + HALF, :] = (a * cos + b * sin).astype(BF16)
        dq_ref[at + HALF : at + HEAD_SIZE, :] = (b * cos - a * sin).astype(BF16)

    if base:

        @pl.when(step == pl.num_programs(0) - 1)
        def _():
            every_cos, every_sin = cos_ref[...], sin_ref[...]
            for g in range(groups):
                at = g * HEAD_SIZE
                turned = dk[g].T
                a, b = turned[:HALF], turned[HALF:]
                dkv_ref[at : at + HALF, :] = (a * every_cos + b * every_sin).astype(BF16)
                dkv_ref[at + HALF : at + HEAD_SIZE, :] = (b * every_cos - a * every_sin).astype(BF16)
                at = (groups + g) * HEAD_SIZE
                dkv_ref[at : at + HEAD_SIZE, :] = dv[g].T.astype(BF16)


def attend_back(scalars, q, o, lse, k, kt, v, cos, sin, w_out, da_parts, rows, zone, base, sums):
    q_cols, size = q.shape
    groups, total, _ = k.shape
    heads = q_cols // HEAD_SIZE
    parts = len(da_parts)
    block = lambda i, s: (0, i)
    sum_shape = (groups, total, HEAD_SIZE)
    inputs = [q, o, lse, k, kt, v, cos, sin, w_out, *da_parts]
    in_specs = [
        pl.BlockSpec((q_cols, rows), block),
        pl.BlockSpec((q_cols, rows), block),
        pl.BlockSpec((heads, rows), block),
    ] + [once(a.shape) for a in inputs[3:]]
    out_specs = [pl.BlockSpec((q_cols, rows), block)]
    out_shape = [jax.ShapeDtypeStruct((q_cols, size), BF16)]
    scratch = [pltpu.VMEM((q_cols, rows), F32)]
    if base:
        inputs += list(sums)
        in_specs += [once(sum_shape)] * 2
        out_specs += [once((2 * groups * HEAD_SIZE, total))]
        out_shape += [jax.ShapeDtypeStruct((2 * groups * HEAD_SIZE, total), BF16)]
        scratch += [pltpu.VMEM(sum_shape, F32)] * 2
    else:
        out_specs += [once(sum_shape)] * 2
        out_shape += [jax.ShapeDtypeStruct(sum_shape, F32)] * 2
    scratch += [pltpu.VMEM((8, rows), F32), pltpu.VMEM((parts, q_cols, rows), BF16)]
    return pl.pallas_call(
        functools.partial(attend_back_kernel, rows, zone, heads, groups, base, parts),
        grid_spec=pltpu.PrefetchScalarGridSpec(
            num_scalar_prefetch=1,
            grid=(size // rows,),
            in_specs=in_specs,
            out_specs=out_specs,
            scratch_shapes=scratch,
        ),
        out_shape=out_shape,
        compiler_params=params(),
        cost_estimate=cost(30),
        name="attend_back",
    )(scalars, *inputs)


def input_grad_kernel(dq_ref, dkv_ref, w_ref, *out_refs):
    q_cols = dq_ref.shape[0]
    rows = out_refs[0].shape[0]
    for b, out_ref in enumerate(out_refs):
        here = slice(b * rows, (b + 1) * rows)
        out = dot(dq_ref[:, here], w_ref[:q_cols, :], 0, 0)
        out = out + dot(dkv_ref[:, here], w_ref[q_cols:, :], 0, 0)
        out_ref[...] = out.astype(BF16)


def input_grads(dq, dkv, w_all_t, rows, half):
    q_cols, size = dq.shape
    cols, width = w_all_t.shape
    count = size // rows
    return pl.pallas_call(
        input_grad_kernel,
        grid=(1,),
        in_specs=[
            once((q_cols, size)),
            pl.BlockSpec((cols - q_cols, size), lambda i: (0, half)),
            once((cols, width)),
        ],
        out_specs=[once((rows, width))] * count,
        out_shape=[jax.ShapeDtypeStruct((rows, width), BF16)] * count,
        compiler_params=params(),
        cost_estimate=cost(5),
        name="input_grads",
    )(dq, dkv, w_all_t)


def qkv_grad_kernel(parts, *refs):
    h_refs = refs[: 2 * parts]
    near_ref, far_ref, dkv_ref, w_ref, gain_ref, grad_ref, gain_grad_ref = refs[2 * parts :]
    rows = h_refs[0].shape[0]
    sums = [0.0, 0.0]
    for b in range(2 * parts):
        dq_ref, at = (near_ref, b) if b < parts else (far_ref, b - parts)
        h = h_refs[b][...]
        sums[0] = sums[0] + dot(dq_ref[:, at * rows : (at + 1) * rows], h)
        sums[1] = sums[1] + dot(dkv_ref[:, b * rows : (b + 1) * rows], h)
    q_cols = near_ref.shape[0]
    grad_ref[:, :q_cols] = sums[0].T.astype(BF16)
    grad_ref[:, q_cols:] = sums[1].T.astype(BF16)
    gain = jnp.sum(sums[0] * w_ref[:q_cols, :].astype(F32), axis=0, keepdims=True)
    gain = gain + jnp.sum(sums[1] * w_ref[q_cols:, :].astype(F32), axis=0, keepdims=True)
    gain_grad_ref[...] = gain / gain_ref[...]


def qkv_grads(h_parts, dq_near, dq_far, dkv, w_all_t, gain):
    cols, width = w_all_t.shape
    inputs = [*h_parts, dq_near, dq_far, dkv, w_all_t, gain[None, :]]
    return pl.pallas_call(
        functools.partial(qkv_grad_kernel, len(h_parts) // 2),
        grid=(1,),
        in_specs=[once(a.shape) for a in inputs],
        out_specs=[once((width, cols)), once((1, width))],
        out_shape=[
            jax.ShapeDtypeStruct((width, cols), BF16),
            jax.ShapeDtypeStruct((1, width), F32),
        ],
        compiler_params=params(),
        cost_estimate=cost(10),
        name="qkv_grads",
    )(*inputs)


def out_grad_kernel(parts, finish, *refs):
    da_refs, o_ref, grad_ref = refs[:parts], refs[parts], refs[-1]
    rows = da_refs[0].shape[0]
    total = refs[parts + 1][...] if finish else 0.0
    for b in range(parts):
        total = total + dot(o_ref[:, b * rows : (b + 1) * rows], da_refs[b][...])
    grad_ref[...] = total.T.astype(BF16) if finish else total


def out_grads(da_parts, o, previous):
    q_cols, width = o.shape[0], da_parts[0].shape[1]
    inputs = [*da_parts, o] + ([] if previous is None else [previous])
    finish = previous is not None
    shape = (width, q_cols) if finish else (q_cols, width)
    return pl.pallas_call(
        functools.partial(out_grad_kernel, len(da_parts), finish),
        grid=(1,),
        in_specs=[once(a.shape) for a in inputs],
        out_specs=once(shape),
        out_shape=jax.ShapeDtypeStruct(shape, BF16 if finish else F32),
        compiler_params=params(),
        cost_estimate=cost(4),
        name="out_grads",
    )(*inputs)


def expert_kernel(experts, adds, choices, *refs):
    s_ref, h0, h1, dy0, dy1, router_ref = refs[:6]
    w_choices = refs[6 : 6 + choices]
    old = refs[6 + choices : 6 + choices + (4 if adds else 0)]
    outs = refs[len(refs) - 19 :]
    mix0, mix1, dh0, dh1, act_out, dgu_out = outs[:6]
    h_s, dy_s, w_s, mix_s, dh_s, gates, dgate, mix_o, dh_o, act_o, dgu_o, in_sem, out_sem = outs[6:]
    e = pl.program_id(0)
    last = pl.num_programs(0) - 1
    rows, width = h0.shape
    hidden = w_s.shape[2] // 3
    lane = lax.broadcasted_iota(jnp.int32, (rows, LANES), 1)
    slot = lax.rem(e, 2)

    def fetch_weights(index, into):
        for n in range(choices):

            @pl.when(s_ref[0] == n)
            def _():
                pltpu.make_async_copy(
                    w_choices[n].at[index], w_s.at[into], in_sem.at[4 + into]
                ).start()

    tokens_in = [
        pltpu.make_async_copy(src, dst, in_sem.at[n])
        for n, (src, dst) in enumerate(
            ((h0, h_s.at[0]), (dy0, dy_s.at[0]), (h1, h_s.at[1]), (dy1, dy_s.at[1]))
        )
    ]
    old_in = [
        pltpu.make_async_copy(src, dst, in_sem.at[6 + n])
        for n, (src, dst) in enumerate(zip(old, (mix_o.at[0], mix_o.at[1], dh_o.at[0], dh_o.at[1])))
    ]

    @pl.when(e == 0)
    def _():
        tokens_in[0].start()
        fetch_weights(0, 0)
        for copy in tokens_in[1:] + old_in:
            copy.start()

    @pl.when(e < last)
    def _():
        fetch_weights(e + 1, 1 - slot)

    for i in range(2):

        @pl.when(e == 0)
        def _():
            tokens_in[2 * i].wait()
            logits = dot(h_s[i], router_ref[...])
            logits = jnp.where(lane < experts, logits, MASK_FILL)
            weights = jnp.exp(logits - jnp.max(logits, axis=1, keepdims=True))
            weights = weights / jnp.sum(weights, axis=1, keepdims=True)
            tokens_in[2 * i + 1].wait()
            gates[i] = weights * dy_s[i, :, width:].astype(F32)

        if i == 0:
            pltpu.make_async_copy(w_choices[0].at[0], w_s.at[slot], in_sem.at[4 + slot]).wait()
        mine = lane == s_ref[1 + e]
        gate = jnp.sum(jnp.where(mine, gates[i], 0.0), axis=1, keepdims=True)
        both = dot(h_s[i], w_s[slot, :, : 2 * hidden])
        gp, up = both[:, :hidden], both[:, hidden:]
        sg = jax.nn.sigmoid(gp)
        silu = gp * sg
        act = (silu * up).astype(BF16).astype(F32)
        dact = dot(dy_s[i, :, :width], w_s[slot, :, 2 * hidden :])
        chosen = dy_s[i, :, width:].astype(F32)
        own_dgate = jnp.where(mine, chosen * jnp.sum(act * dact, axis=1, keepdims=True), 0.0)
        scaled = (gate * act).astype(BF16)
        dact = gate * dact
        dgp = (dact * up * sg * (1.0 + gp * (1.0 - sg))).astype(BF16)
        dup = (dact * silu).astype(BF16)

        @pl.when(e > 0)
        def _():
            pltpu.make_async_copy(
                act_o.at[i], act_out.at[0, pl.ds(0, rows), :], out_sem.at[i]
            ).wait()
            pltpu.make_async_copy(
                dgu_o.at[i], dgu_out.at[0, pl.ds(0, rows), :], out_sem.at[2 + i]
            ).wait()

        act_o[i] = scaled
        dgu_o[i, :, :hidden] = dgp
        dgu_o[i, :, hidden:] = dup
        here = pl.ds(i * rows, rows)
        pltpu.make_async_copy(act_o.at[i], act_out.at[e, here, :], out_sem.at[i]).start()
        pltpu.make_async_copy(dgu_o.at[i], dgu_out.at[e, here, :], out_sem.at[2 + i]).start()
        mix = dot(scaled, w_s[slot, :, 2 * hidden :], 1, 1)
        dh = dot(dgu_o[i], w_s[slot, :, : 2 * hidden], 1, 1)

        @pl.when(e == 0)
        def _():
            if adds:
                old_in[i].wait()
                old_in[2 + i].wait()
                mix_s[i] = mix + mix_o[i].astype(F32)
                dh_s[i] = dh + dh_o[i, :, :width].astype(F32)
                kept = dh_o[i, :, width:].astype(F32)
                kept = kept + pltpu.roll(kept, LANES // 2, 1)
                dgate[i] = own_dgate + jnp.where(lane < LANES // 2, kept, 0.0)
            else:
                mix_s[i] = mix
                dh_s[i] = dh
                dgate[i] = own_dgate

        @pl.when(e > 0)
        def _():
            mix_s[i] += mix
            dh_s[i] += dh
            dgate[i] += own_dgate

        @pl.when(e == last)
        def _():
            mix_o[i] = mix_s[i].astype(BF16)
            dh_o[i, :, :width] = dh_s[i].astype(BF16)
            high = dgate[i].astype(BF16).astype(F32)
            low = dgate[i] - high
            dh_o[i, :, width:] = (high + pltpu.roll(low, LANES // 2, 1)).astype(BF16)
            pltpu.make_async_copy(mix_o.at[i], (mix0, mix1)[i], out_sem.at[4 + i]).start()
            pltpu.make_async_copy(dh_o.at[i], (dh0, dh1)[i], out_sem.at[6 + i]).start()

    @pl.when(e == last)
    def _():
        for i in range(2):
            here = pl.ds(i * rows, rows)
            pltpu.make_async_copy(act_o.at[i], act_out.at[e, here, :], out_sem.at[i]).wait()
            pltpu.make_async_copy(dgu_o.at[i], dgu_out.at[e, here, :], out_sem.at[2 + i]).wait()
            pltpu.make_async_copy(mix_o.at[i], (mix0, mix1)[i], out_sem.at[4 + i]).wait()
            pltpu.make_async_copy(dh_o.at[i], (dh0, dh1)[i], out_sem.at[6 + i]).wait()


def run_experts(scalars, h_parts, dy_parts, router, choices, experts, micros, old=()):
    rows, width = h_parts[0].shape
    wide = width + LANES
    mine, _, cols = choices[0].shape
    hidden = cols // 3
    anywhere = pl.BlockSpec(memory_space=pl.ANY)
    return pl.pallas_call(
        functools.partial(expert_kernel, experts, bool(old), len(choices)),
        grid_spec=pltpu.PrefetchScalarGridSpec(
            num_scalar_prefetch=1,
            grid=(mine,),
            in_specs=[anywhere] * 4 + [once((width, LANES))] + [anywhere] * (len(choices) + len(old)),
            out_specs=[anywhere] * 6,
            scratch_shapes=[
                pltpu.VMEM((2, rows, width), BF16),
                pltpu.VMEM((2, rows, wide), BF16),
                pltpu.VMEM((2, width, cols), BF16),
                pltpu.VMEM((2, rows, width), F32),
                pltpu.VMEM((2, rows, width), F32),
                pltpu.VMEM((2, rows, LANES), F32),
                pltpu.VMEM((2, rows, LANES), F32),
                pltpu.VMEM((2, rows, width), BF16),
                pltpu.VMEM((2, rows, wide), BF16),
                pltpu.VMEM((2, rows, hidden), BF16),
                pltpu.VMEM((2, rows, 2 * hidden), BF16),
                pltpu.SemaphoreType.DMA((10,)),
                pltpu.SemaphoreType.DMA((8,)),
            ],
        ),
        out_shape=[jax.ShapeDtypeStruct((rows, width), BF16)] * 2
        + [jax.ShapeDtypeStruct((rows, wide), BF16)] * 2
        + [
            jax.ShapeDtypeStruct((mine, 2 * rows, hidden), BF16),
            jax.ShapeDtypeStruct((mine, 2 * rows, 2 * hidden), BF16),
        ],
        compiler_params=params(),
        cost_estimate=cost(micros),
        name="experts",
    )(scalars, *h_parts, *dy_parts, router, *choices, *old)


def expert_grad_kernel(*refs):
    h_refs, dy_refs, acts, dgus = refs[:4], refs[4:8], refs[8:10], refs[10:12]
    out_ref, h_s, dy_s, act_s, dgu_s, sem = refs[12:]
    e = pl.program_id(0)
    rows, width = h_refs[0].shape
    hidden = act_s.shape[1]
    first, second = [], []
    for b in range(4):
        here = pl.ds(b * rows, rows)
        first.append(pltpu.make_async_copy(h_refs[b], h_s.at[here, :], sem.at[b]))
        second.append(
            pltpu.make_async_copy(dy_refs[b].at[:, pl.ds(0, width)], dy_s.at[here, :], sem.at[4 + b])
        )
    per_expert = []
    for b in range(2):
        here = pl.ds(2 * b * rows, 2 * rows)
        per_expert.append(pltpu.make_async_copy(dgus[b].at[e], dgu_s.at[here, :], sem.at[8 + b]))
    for b in range(2):
        here = pl.ds(2 * b * rows, 2 * rows)
        per_expert.append(pltpu.make_async_copy(acts[b].at[e], act_s.at[here, :], sem.at[10 + b]))
    for copy in per_expert[:2]:
        copy.start()

    @pl.when(e == 0)
    def _():
        for copy in first:
            copy.start()

    for copy in per_expert[2:]:
        copy.start()

    @pl.when(e == 0)
    def _():
        for copy in second:
            copy.start()
        for copy in first:
            copy.wait()

    for copy in per_expert[:2]:
        copy.wait()
    out_ref[0, :, : 2 * hidden] = dot(h_s[...], dgu_s[...], 0, 0).astype(BF16)

    @pl.when(e == 0)
    def _():
        for copy in second:
            copy.wait()

    for copy in per_expert[2:]:
        copy.wait()
    out_ref[0, :, 2 * hidden :] = dot(dy_s[...], act_s[...], 0, 0).astype(BF16)


def expert_grads(h_parts, dy_parts, acts, dgus):
    rows, width = h_parts[0].shape
    mine, _, hidden = acts[0].shape
    anywhere = pl.BlockSpec(memory_space=pl.ANY)
    return pl.pallas_call(
        expert_grad_kernel,
        grid=(mine,),
        in_specs=[anywhere] * 12,
        out_specs=pl.BlockSpec((1, width, 3 * hidden), lambda e: (e, 0, 0)),
        out_shape=jax.ShapeDtypeStruct((mine, width, 3 * hidden), BF16),
        scratch_shapes=[
            pltpu.VMEM((4 * rows, width), BF16),
            pltpu.VMEM((4 * rows, width), BF16),
            pltpu.VMEM((4 * rows, hidden), BF16),
            pltpu.VMEM((4 * rows, 2 * hidden), BF16),
            pltpu.SemaphoreType.DMA((12,)),
        ],
        compiler_params=params(),
        cost_estimate=cost(15),
        name="expert_grads",
    )(*h_parts, *dy_parts, *acts, *dgus)


def body(
    sizes,
    tokens,
    norm1_gain,
    w_query,
    key_weight,
    value_weight,
    w_out,
    norm2_gain,
    w_router,
    w_gate,
    w_up,
    w_down,
    routes,
    piece_first_position,
    piece_length,
    grad_out,
):
    nz, nx = sizes
    rows, width = tokens.shape
    blocks = 2 * nx
    half = blocks // 2
    q_cols, kv_cols = w_query.shape[1], key_weight.shape[1]
    experts = w_router.shape[1]
    hidden = w_gate.shape[2]
    zone = SEQUENCE_LENGTH // piece_length.shape[1]
    iz, iy, ix, ic = (lax.axis_index(a) for a in "zyxc")
    me = ix * 2 + ic

    def tp_swap(value, bit):
        if bit == 0:
            return lax.ppermute(value, "c", [(0, 1), (1, 0)])
        return lax.ppermute(value, "x", [(i, i ^ (1 << (bit - 1))) for i in range(nx)])

    def y_swap(value):
        return lax.ppermute(value, "y", [(0, 1), (1, 0)])

    bits = blocks.bit_length() - 1

    def tp_gather(value):
        held = {0: value}
        for bit in reversed(range(bits)):
            for i in list(held):
                held[i | (1 << bit)] = tp_swap(held[i], bit)
        return [held[i] for i in range(blocks)]

    def tp_scatter(parts):
        parts = dict(enumerate(parts))
        for bit in range(bits):
            for i in sorted(parts, reverse=True):
                if i & (1 << bit):
                    parts[i] = tp_swap(parts[i], bit)
            for i in sorted(parts, reverse=True):
                if i & (1 << bit):
                    other = parts.pop(i)
                    base = parts[i ^ (1 << bit)].astype(F32) + other.astype(F32)
                    last = i == 1 << bit and bit == bits - 1
                    parts[i ^ (1 << bit)] = base if last else base.astype(BF16)
            if bit == bits - 2:
                side, own = parts[1 << (bits - 1)], parts[0]
        return parts[0], side, own

    def sum_all(value):
        for bit in range(bits):
            value = value + tp_swap(value, bit)
        value = value + y_swap(value)
        step = 1
        while step < nz:
            value = value + lax.ppermute(value, "z", [(i, i ^ step) for i in range(nz)])
            step *= 2
        return value

    def own_columns(value):
        each = width // (nz * 4 * nx)
        index = (iz * 2 + iy) * blocks + me
        return lax.dynamic_slice_in_dim(value, index * each, each, 1)

    x = tokens.astype(F32)
    r1 = lax.rsqrt(jnp.mean(x * x, axis=-1, keepdims=True) + EPSILON)
    h1 = (x * r1 * norm1_gain).astype(BF16)
    h_parts = tp_gather(h1)

    w_all_t = jnp.concatenate([w_query, key_weight, value_weight], axis=1).T
    order = me ^ jnp.arange(blocks, dtype=jnp.int32)
    position = (order[:, None] * rows + jnp.arange(rows, dtype=jnp.int32)[None, :]).reshape(-1)
    frequency = ROPE_BASE ** (-(jnp.arange(HALF, dtype=F32) * (2.0 / HEAD_SIZE)))
    angles = frequency[:, None] * position.astype(F32)[None, :]
    cos, sin = jnp.cos(angles), jnp.sin(angles)
    scalars = jnp.concatenate(
        [me.astype(jnp.int32)[None], piece_first_position[0], piece_length[0]]
    )
    q_near, *kv = project_qkv(h_parts[:half], w_all_t, cos, sin, q_cols, kv_cols, 0, None)

    mask = jnp.zeros((rows, LANES), jnp.bool_)
    for j in range(routes.shape[1]):
        mask = mask | (routes[:, j : j + 1] == jnp.arange(LANES, dtype=jnp.int32)[None, :])
    dy_own = after(jnp.concatenate([grad_out, mask.astype(BF16)], axis=1), q_near)
    dy_side = y_swap(dy_own)

    mine = nz // 2
    cut = mine // 2
    weight = after(jnp.concatenate([w_gate[0], w_up[0], w_down[0].T], axis=1), q_near)[None]
    if nz == 4:
        ids = jnp.where(ic == 0, jnp.arange(2), 3 - jnp.arange(2)) * 2 + iy
        along = jnp.where(ic == 0, iz, 3 - iz)

        def shift(value, moves):
            perm = [(s * 2, d * 2) for s, d in moves]
            perm += [((3 - s) * 2 + 1, (3 - d) * 2 + 1) for s, d in moves]
            return lax.ppermute(value, ("z", "c"), perm)

        from_outer = shift(weight, [(0, 1), (1, 2)])
        from_inner = shift(weight, [(1, 0)])
    else:
        ids = (ic * mine + jnp.arange(mine)) * 2 + iy
        along = ic * 0

    q_far, k, kt, v, vt = project_qkv(h_parts[half:], w_all_t, cos, sin, q_cols, kv_cols, 1, kv)
    quarter = half // 2
    run = lambda q, at, count, base: attend(
        scalars, q, at, count, k, vt, w_out, rows, zone, base
    )
    o_3, lse_3, *out_3 = run(q_far, quarter, quarter, half + quarter)
    if nz == 4:
        second = shift(after(from_outer, out_3[0]), [(1, 2), (2, 3)])
    o_2, lse_2, *out_2 = run(after(q_far, out_3[0]), 0, quarter, half)
    o_near, lse_near, *out_near = run(after(q_near, out_2[0]), 0, half, 0)
    o_far = jnp.concatenate([o_2, o_3], axis=1)
    lse_far = jnp.concatenate([lse_2, lse_3], axis=1)
    dy_parts = [dy_own, tp_swap(after(dy_own, out_3[0]), 0), dy_side]
    dy_parts.append(tp_swap(after(dy_side, out_2[0]), 0))
    attended, _, near_sum = tp_scatter([*out_near, *out_2, *out_3])
    if nz == 4:
        third = shift(after(second, near_sum), [(2, 3)])
        outer = (weight, from_outer, second, third)
        inner = (from_inner, weight, from_outer, second)
    else:
        every = lax.all_gather(weight, "z", axis=0, tiled=True)
        every = lax.dynamic_slice_in_dim(every, ic * mine, mine, 0)
        outer, inner = (every[:cut],), (every[cut:],)
    x1 = x + attended
    r2 = lax.rsqrt(jnp.mean(x1 * x1, axis=-1, keepdims=True) + EPSILON)
    n2 = x1 * r2
    h2 = (n2 * norm2_gain).astype(BF16)

    router_wide = jnp.pad(w_router, ((0, 0), (0, LANES - experts)))
    h2_side = y_swap(h2)
    h2_parts = [h2, tp_swap(h2, 0), h2_side, tp_swap(h2_side, 0)]
    head = along.astype(jnp.int32)[None]
    outer_ids = jnp.concatenate([head, ids[:cut].astype(jnp.int32)])
    inner_ids = jnp.concatenate([head, ids[cut:].astype(jnp.int32)])
    through = lambda s, at, w, old=(): run_experts(
        s, h2_parts[at : at + 2], dy_parts[at : at + 2], router_wide, w, experts, 18 * cut, old
    )
    first = through(inner_ids, 0, inner)
    near = through(outer_ids, 0, outer, first[:4])
    third_pass = through(inner_ids, 2, inner)
    far = through(outer_ids, 2, outer, third_pass[:4])

    join = lambda a, b: (a.astype(F32) + tp_swap(b, 0).astype(F32)).astype(BF16)
    dh_side = join(far[2], far[3])
    dh_own = near[2].astype(F32) + tp_swap(near[3], 0).astype(F32)
    dh_sum = dh_own + y_swap(dh_side).astype(F32)
    grads_outer = expert_grads(
        [after(h2_parts[0], dh_side), *h2_parts[1:]], dy_parts, (near[4], far[4]), (near[5], far[5])
    )
    grads_inner = expert_grads(
        [after(h2_parts[0], grads_outer), *h2_parts[1:]],
        dy_parts,
        (first[4], third_pass[4]),
        (first[5], third_pass[5]),
    )

    probs = jax.nn.softmax(dot(h2, w_router), axis=-1)
    dprobs = dh_sum[:, width : width + experts]
    dprobs = dprobs + dh_sum[:, width + LANES // 2 : width + LANES // 2 + experts]
    dlogits = (
        probs * (dprobs - jnp.sum(probs * dprobs, axis=-1, keepdims=True))
    ).astype(BF16)
    dh2 = dot(dlogits, w_router, 1, 1) + dh_sum[:, :width]
    scaled = dh2 * norm2_gain
    dx1 = grad_out.astype(F32) + r2 * (
        scaled - n2 * jnp.mean(scaled * n2, axis=-1, keepdims=True)
    )
    router_part = dot(dlogits, h2, 0, 0)
    gain2 = jnp.sum(dh2 * n2, axis=0, keepdims=True)

    da_parts = tp_gather(dx1.astype(BF16))
    back = lambda q, o, lse, da, base, sums: attend_back(
        scalars, q, o, lse, k, kt, v, cos, sin, w_out, da, rows, zone, base, sums
    )
    dq_near, *sums = back(q_near, o_near, lse_near, da_parts[:half], 0, None)
    out_part = out_grads([after(da_parts[0], dq_near), *da_parts[1:half]], o_near, None)
    out_part = out_grads(da_parts[half:], o_far, out_part)
    mixed_side = join(after(far[0], dq_near), after(far[1], dq_near))
    mixed_own = near[0].astype(F32) + tp_swap(after(near[1], dq_near), 0).astype(F32)
    dq_far, dkv = back(after(q_far, out_part, mixed_side), o_far, lse_far, da_parts[half:], half, sums)
    mixed_side = y_swap(mixed_side)
    output = x1 + mixed_own + mixed_side.astype(F32)
    dh1_far = input_grads(after(dq_far, mixed_side), dkv, w_all_t, rows, 1)
    dh1_near = input_grads(dq_near, after(dkv, dh1_far[0]), w_all_t, rows, 0)
    dh1, dh1_side, _ = tp_scatter([*dh1_near, *dh1_far])
    n1 = x * r1
    scaled = dh1 * norm1_gain
    grad_input = dx1 + r1 * (scaled - n1 * jnp.mean(scaled * n1, axis=-1, keepdims=True))

    grad_outproj = lax.psum_scatter(
        out_part, ("z", "y"), scatter_dimension=0, tiled=True
    ).astype(F32).T
    qkv_grad, gain1 = qkv_grads(
        [after(h_parts[0], dh1_side), *h_parts[1:]], dq_near, dq_far, dkv, w_all_t, norm1_gain
    )
    each = width // (2 * nz)
    qkv_grad = qkv_grad.reshape(nz, 2, each, qkv_grad.shape[1])
    pick = lambda at: lax.dynamic_index_in_dim(qkv_grad, at, 1, keepdims=False)
    summed = pick(iy).astype(F32) + y_swap(pick(1 - iy)).astype(F32)
    grad_qkv = lax.psum_scatter(
        summed.astype(BF16).reshape(nz * each, -1), "z", scatter_dimension=0, tiled=True
    ).astype(F32)
    small = own_columns(sum_all(jnp.concatenate([router_part, gain2, gain1], axis=0)))

    if nz == 4:
        outer, inner = grads_outer[0], grads_inner[0]
        add = lambda a, b: (a.astype(F32) + b.astype(F32)).astype(BF16)
        o1 = shift(outer, [(3, 2)])
        i1 = shift(after(inner, o1), [(3, 2)])
        o2 = shift(add(outer, o1), [(2, 1)])
        i2 = shift(add(inner, i1), [(2, 1)])
        o3 = shift(add(outer, o2), [(1, 0)])
        i0 = shift(after(inner, i1), [(0, 1)])
        whole = jnp.where(
            along == 0,
            outer.astype(F32) + o3.astype(F32),
            inner.astype(F32) + i2.astype(F32) + i0.astype(F32),
        ).astype(BF16)
        side = width // 2
        pairs = [(z, c) for z in range(4) for c in (z // 2,)]
        other = lax.dynamic_slice_in_dim(whole, (1 - ix) * side, side, 0)
        other = lax.ppermute(
            other,
            ("z", "x", "c"),
            [((z * 2 + i) * 2 + c, (z * 2 + 1 - i) * 2 + c) for z, c in pairs for i in range(2)],
        )
        kept = lax.dynamic_slice_in_dim(whole, ix * side, side, 0)
        kept = kept.astype(F32) + other.astype(F32)
        own = lax.dynamic_slice_in_dim(kept, ic * (side // 2), side // 2, 0)
        give = lax.dynamic_slice_in_dim(kept, (1 - ic) * (side // 2), side // 2, 0).astype(BF16)
        part = jnp.where(ic == iz // 2, own, tp_swap(give, 0).astype(F32))
    else:
        stacked = jnp.concatenate([grads_outer, grads_inner], axis=0)
        every = jnp.zeros((nz, width, 3 * hidden), BF16)
        every = lax.dynamic_update_slice_in_dim(every, stacked, ic * mine, 0)
        part = lax.psum_scatter(
            every.reshape(nz * width, 3 * hidden), "z", scatter_dimension=0, tiled=True
        )
        part = lax.psum_scatter(part, ("x", "c"), scatter_dimension=0, tiled=True).astype(F32)
    grad_gate = part[None, :, :hidden]
    grad_up = part[None, :, hidden : 2 * hidden]
    grad_down = part[:, 2 * hidden :].T[None]
    return (
        output,
        grad_input,
        small[experts + 1],
        grad_qkv[:, :q_cols],
        grad_qkv[:, q_cols : q_cols + kv_cols],
        grad_qkv[:, q_cols + kv_cols :],
        grad_outproj,
        small[experts],
        small[:experts].T,
        grad_gate,
        grad_up,
        grad_down,
    )


def solution(mesh):
    ep, tp = mesh.shape["ep"], mesh.shape["tp"]
    nz, nx = ep // 2, tp // 2
    grid = Mesh(mesh.devices.reshape(nz, 2, nx, 2), ("z", "y", "x", "c"))
    e, t = ("z", "y"), ("x", "c")
    every = ("z", "y", "x", "c")
    return jax.shard_map(
        functools.partial(body, (nz, nx)),
        mesh=grid,
        in_specs=(
            P(every, None),
            P(),
            P(None, t),
            P(None, t),
            P(None, t),
            P(t, None),
            P(),
            P(),
            P(e, None, None),
            P(e, None, None),
            P(e, None, None),
            P(every, None),
            P(e, None),
            P(e, None),
            P(every, None),
        ),
        out_specs=(
            P(every, None),
            P(every, None),
            P(every),
            P(e, t),
            P(e, t),
            P(e, t),
            P(t, e),
            P(every),
            P(every, None),
            P(e, t, None),
            P(e, t, None),
            P(e, None, t),
        ),
        check_vma=False,
    )
```

time: 918 us -> 665 us (0.72)
  waiting for transfers between devices: 397 us -> 161 us
  Pallas kernels: 191 us -> 264 us
  blocking collectives: 48.8 us -> 0 us
  matrix products: 49 us -> 3.42 us
  starting transfers between devices: 74 us -> 94.9 us
  local copies, waits for them, and re-layouts: 35.5 us -> 22.5 us
    unnamed x7 -> x2, waiting for transfers between devices: 83.8 us -> 0.03 us
    reduce_scatter x3 -> x2, waiting for transfers between devices: 92.2 us -> 21.3 us  [the longest x1 13.7 us: body(): lax.psum_scatter(summed.astype(BF16).reshape(nz * each, -1), 'z', scatter...]
    unnamed x1 -> x0, blocking collectives: 48.8 us -> none
    pallas_call x4 -> x13, Pallas kernels: 110 us -> 159 us  [the longest x4 81.4 us: run_experts(): pl.pallas_call(functools.partial(expert_kernel, experts, bool(old), len(c...]
    concatenate x16 -> x6, other arithmetic: 51.2 us -> 7.56 us  [the longest x1 3.65 us: body(): jnp.concatenate([w_gate[0], w_up[0], w_down[0].T], axis=1)]
    ppermute x4 -> x5, waiting for transfers between devices: 87.4 us -> 47.2 us  [tp_swap(): return lax.ppermute(value, 'x', [(i, i ^ 1 << bit - 1) for i in range(nx)])]
    convert_element_type x4 -> x11, other arithmetic: 10.7 us -> 49.4 us  [the longest x3 21.6 us: body(): add = lambda a, b: (a.astype(F32) + b.astype(F32)).astype(BF16)]
    ppermute x13, waiting for transfers between devices: 65.6 us -> 30.4 us  [the longest x10 28.4 us: shift(): return lax.ppermute(value, ('z', 'c'), perm)]
  transfers between devices with their start and end apart: 48 -> 44, of which waited for: 17 -> 14; matrix products, arithmetic and copies ran while one was open for 16% -> 16% of each run, Pallas kernels for 14% -> 40%
where the time goes in v2:
time: 665 us; the launch traced here: 654 us
  Pallas kernels  264 us (40%)
  waiting for transfers between devices  161 us (24%)
  starting transfers between devices  94.9 us (14%)
  other arithmetic  91.6 us (14%)
  local copies, waits for them, and re-layouts  22.5 us (3%)
  between operations  16.4 us (2%)
    pallas_call x4, Pallas kernels, run_experts(): pl.pallas_call(functools.partial(expert_kernel, experts, bool(old), len(c...  81.4 us
    pallas_call x2, Pallas kernels, attend_back(): pl.pallas_call(functools.partial(attend_back_kernel, rows, zone, heads, g...  58 us
    ppermute x6, waiting for transfers between devices, y_swap(): return lax.ppermute(value, 'y', [(0, 1), (1, 0)])  57.2 us
    pallas_call x3, Pallas kernels, attend(): pl.pallas_call(functools.partial(attend_kernel, rows, zone, heads, groups...  47.6 us
    ppermute x5, waiting for transfers between devices, tp_swap(): return lax.ppermute(value, 'x', [(i, i ^ 1 << bit - 1) for i in range(nx)])  47.2 us
    ppermute x10, starting transfers between devices, shift(): return lax.ppermute(value, ('z', 'c'), perm)  34.1 us
    pallas_call x2, Pallas kernels, expert_grads(): pl.pallas_call(expert_grad_kernel, grid=(mine,), in_specs=[anywhere] * 12...  33.2 us
    ppermute x5, starting transfers between devices, tp_swap(): return lax.ppermute(value, 'x', [(i, i ^ 1 << bit - 1) for i in range(nx)])  30.4 us
  transfers between devices with their start and end apart: 44, of which 14 were waited for; matrix products, arithmetic and copies ran while one was open for 16% of the time, Pallas kernels for 40%

profile of v2, /device:TPU:2, one launch (start us, length us, event | category | flops | bytes accessed | tf_op | source)
XLA Modules:
  0.0 654.2 jit_solution(5310466373396014600)
XLA Ops:
  18.7 3.6 pad_maximum_fusion
  23.8 6.2 qkv.2
  30.0 6.2 collective-permute-start.8
  36.1 14.0 %collective-permute-done.1.refs_0_.refs_2_ = bf16[512,1536]{1,0:T(8,128)(2,1)} collective-permute-done((bf16[512,1536]{1,0:T(8,128)(2,1)}, bf16[512,1536]{1,0:T(8,128)(2,1)}, u32[]{:S(2)}, u32[]{:S(2)}) %collective-permute-start.1) | collective-permute-done | bytes 1572896 | tf_op jit(solution)/shard_map/ppermute | solution.py:718
  55.0 6.2 qkv.3
  61.2 11.3 %attend.3 = (bf16[384,512]{1,0:T(8,128)(2,1)}, f32[6,512]{1,0:T(8,128)}, bf16[512,1536]{1,0:T(8,128)(2,1)}) custom-call(s32[9]{0:T(128)} %pad_add_fusion.s_ref.refs_0_, bf16[384,1024]{1,0:T(8,128)(2,1)} %get-tuple-element.134.q_ref.refs_1_, bf16[2,2048,64]{2,1,0:T(8,128)(2,1)} %get-tuple-element.93.k_ref.refs_4_, ...), custom_call_target="tpu_custom_call" | custom-call | flops 8999999488 | bytes 27000000 | tf_op jit(solution)/shard_map/attend/pallas_call | solution.py:186
  72.5 7.9 %attend.4 = (bf16[384,512]{1,0:T(8,128)(2,1)}, f32[6,512]{1,0:T(8,128)}, bf16[512,1536]{1,0:T(8,128)(2,1)}) custom-call(s32[9]{0:T(128)} %pad_add_fusion.s_ref.refs_0_, bf16[384,1024]{1,0:T(8,128)(2,1)} %get-tuple-element.134.q_ref.refs_1_, bf16[2,2048,64]{2,1,0:T(8,128)(2,1)} %get-tuple-element.93.k_ref.refs_4_, ...), custom_call_target="tpu_custom_call" | custom-call | flops 8999999488 | bytes 27000000 | tf_op jit(solution)/shard_map/attend/pallas_call | solution.py:186
  80.4 5.5 collective-permute-done.8.refs_8_.refs_7_
  85.9 3.3 collective-permute-start.9
  89.2 28.4 %attend.5 = (bf16[384,1024]{1,0:T(8,128)(2,1)}, f32[6,1024]{1,0:T(8,128)}, bf16[512,1536]{1,0:T(8,128)(2,1)}, bf16[512,1536]{1,0:T(8,128)(2,1)}) custom-call(s32[9]{0:T(128)} %pad_add_fusion.s_ref.refs_0_, bf16[384,1024]{1,0:T(8,128)(2,1)} %get-tuple-element.98.q_ref.refs_1_, bf16[2,2048,64]{2,1,0:T(8,128)(2,1)} %get-tuple-element.93.k_ref.refs_4_, ...), custom_call_target="tpu_custom_call" | custom-call | flops 17999998976 | bytes 54000000 | tf_op jit(solution)/shard_map/attend/pallas_call | solution.py:186
  123.6 33.2 %collective-permute-done.5 = bf16[512,1536]{1,0:T(8,128)(2,1)S(1)} collective-permute-done((bf16[512,1536]{1,0:T(8,128)(2,1)S(1)}, bf16[512,1536]{1,0:T(8,128)(2,1)S(1)}, u32[]{:S(2)}, u32[]{:S(2)}) %collective-permute-start.5) | collective-permute-done | bytes 1572896 | tf_op jit(solution)/shard_map/ppermute | solution.py:718
  164.2 31.8 %collective-permute-done.13.refs_1_.refs_2_ = bf16[512,1536]{1,0:T(8,128)(2,1)} collective-permute-done((bf16[512,1536]{1,0:T(8,128)(2,1)S(1)}, bf16[512,1536]{1,0:T(8,128)(2,1)}, u32[]{:S(2)}, u32[]{:S(2)}) %collective-permute-start.13) | collective-permute-done | bytes 1572896 | tf_op jit(solution)/shard_map/ppermute | solution.py:721
  201.4 14.2 %collective-permute-done.11.refs_6_ = bf16[1,1536,1536]{2,1,0:T(8,128)(2,1)} collective-permute-done((bf16[1,1536,1536]{2,1,0:T(8,128)(2,1)}, bf16[1,1536,1536]{2,1,0:T(8,128)(2,1)}, u32[]{:S(2)}, u32[]{:S(2)}) %collective-permute-start.11) | collective-permute-done | bytes 4718624 | tf_op jit(solution)/shard_map/ppermute | solution.py:795
  215.6 18.7 %experts.6 = (bf16[512,1536]{1,0:T(8,128)(2,1)}, bf16[512,1536]{1,0:T(8,128)(2,1)}, bf16[512,1664]{1,0:T(8,128)(2,1)}, bf16[512,1664]{1,0:T(8,128)(2,1)}, bf16[1...) custom-call(s32[2]{0:T(128)} %pad_add_fusion.2.refs_0_, ...), custom_call_target="tpu_custom_call" | custom-call | flops 17999998976 | bytes 54000000 | tf_op jit(solution)/shard_map/experts/pallas_call | solution.py:576
  234.3 21.8 %experts.7 = (bf16[512,1536]{1,0:T(8,128)(2,1)}, bf16[512,1536]{1,0:T(8,128)(2,1)}, bf16[512,1664]{1,0:T(8,128)(2,1)}, bf16[512,1664]{1,0:T(8,128)(2,1)}, bf16[1...) custom-call(s32[2]{0:T(128)} %pad_add_fusion.1.refs_0_, ...), custom_call_target="tpu_custom_call" | custom-call | flops 17999998976 | bytes 54000000 | tf_op jit(solution)/shard_map/experts/pallas_call | solution.py:576
  256.2 8.1 %collective-permute-start.17 = (bf16[512,1664]{1,0:T(8,128)(2,1)}, bf16[512,1664]{1,0:T(8,128)(2,1)}, u32[]{:S(2)}, u32[]{:S(2)}) collective-permute-start(bf16[512,1664]{1,0:T(8,128)(2,1)} %get-tuple-element.124), channel_id=1, source_target_pairs={{0,1},{1,0},{2,3},{3,2},{4,5},{5,4},{6,7},{7,6},{8,9},{9,8},{10,11... | collective-permute-start | bytes 5111816 | tf_op jit(solution)/shard_map/ppermute | solution.py:717
  264.3 19.1 %experts.4 = (bf16[512,1536]{1,0:T(8,128)(2,1)}, bf16[512,1536]{1,0:T(8,128)(2,1)}, bf16[512,1664]{1,0:T(8,128)(2,1)}, bf16[512,1664]{1,0:T(8,128)(2,1)}, bf16[1...) custom-call(s32[2]{0:T(128)} %pad_add_fusion.2.refs_0_, bf16[512,1536]{1,0:T(8,128)(2,1)} %copy-done.4, ...), custom_call_target="tpu_custom_call" | custom-call | flops 17999998976 | bytes 54000000 | tf_op jit(solution)/shard_map/experts/pallas_call | solution.py:576
  283.4 21.8 %experts.5 = (bf16[512,1536]{1,0:T(8,128)(2,1)}, bf16[512,1536]{1,0:T(8,128)(2,1)}, bf16[512,1664]{1,0:T(8,128)(2,1)}, bf16[512,1664]{1,0:T(8,128)(2,1)}, bf16[1...) custom-call(s32[2]{0:T(128)} %pad_add_fusion.1.refs_0_, bf16[512,1536]{1,0:T(8,128)(2,1)} %copy-done.4, ...), custom_call_target="tpu_custom_call" | custom-call | flops 17999998976 | bytes 54000000 | tf_op jit(solution)/shard_map/experts/pallas_call | solution.py:576
  305.3 3.7 add_convert_fusion
  311.4 16.7 %expert_grads.2 = bf16[1,1536,1536]{2,1,0:T(8,128)(2,1)} custom-call(bf16[512,1536]{1,0:T(8,128)(2,1)} %copy-done.4, bf16[512,1536]{1,0:T(8,128)(2,1)} %collective-permute-done.6.refs_2_.refs_1_, bf16[512,1536]{1,0:T(8,128)(2,1)} %collective-permute-done.13.refs_1_.refs_2_, bf16[512,1536]{1,0:T(8,128)(2,1)} %collective-permute-done.14.refs_2_.refs_3_, ...), custom_call_target="tpu_custom_call" | custom-call | flops 15000000512 | bytes 45000000 | tf_op jit(solution)/shard_map/expert_grads/pallas_call | solution.py:667
  331.0 17.8 %collective-permute-done.18 = bf16[512,1664]{1,0:T(8,128)(2,1)} collective-permute-done((bf16[512,1664]{1,0:T(8,128)(2,1)}, bf16[512,1664]{1,0:T(8,128)(2,1)}, u32[]{:S(2)}, u32[]{:S(2)}) %collective-permute-start.18) | collective-permute-done | bytes 1703968 | tf_op jit(solution)/shard_map/ppermute | solution.py:721
  348.8 3.0 convert_add_fusion.7
  354.0 3.2 fusion.25
  358.0 10.6 %collective-permute-start.23 = (bf16[512,1536]{1,0:T(8,128)(2,1)}, bf16[512,1536]{1,0:T(8,128)(2,1)}, u32[]{:S(2)}, u32[]{:S(2)}) collective-permute-start(bf16[512,1536]{1,0:T(8,128)(2,1)} %get-tuple-element.133.refs_10_.refs_0_), channel_id=1, source_target_pairs={{0,2},{2,0},{1,3},{3,1},{4,6},{6,4},{5,7},{7,5},{8,10},{10,8},{9,1... | collective-permute-start | bytes 4718600 | tf_op jit(solution)/shard_map/ppermute | solution.py:718
  368.6 36.3 %attend_back.2 = (bf16[384,1024]{1,0:T(8,128)(2,1)}, f32[2,2048,64]{2,1,0:T(8,128)}, f32[2,2048,64]{2,1,0:T(8,128)}) custom-call(s32[9]{0:T(128)} %pad_add_fusion.s_ref.refs_0_, bf16[384,1024]{1,0:T(8,128)(2,1)} %get-tuple-element.98.q_ref.refs_1_, bf16[384,1024]{1,0:T(8,128)(2,1)} %get-tuple-element.112.refs_2_, f32[6,1024]{1,0:T(8,128)} %get-tuple-element.113.refs_3_, ...), custom_call_target="tpu_custom_call" | custom-call | flops 30000001024 | bytes 90000000 | tf_op jit(solution)/shard_map/attend_back/pallas_call | solution.py:329
  405.5 7.2 %fusion.4 = bf16[1536,1536]{1,0:T(8,128)(2,1)} fusion(bf16[1536,1536]{1,0:T(8,128)(2,1)} %collective-permute-done.34, bf16[1,1536,1536]{2,1,0:T(8,128)(2,1)} %expert_grads.2), kind=kLoop, calls=%fused_computation.9 | loop fusion | flops 9437184 | bytes 14155776 | tf_op jit(solution)/shard_map/convert_element_type | solution.py:909
  415.6 16.5 %expert_grads.3 = bf16[1,1536,1536]{2,1,0:T(8,128)(2,1)} custom-call(bf16[512,1536]{1,0:T(8,128)(2,1)} %copy-done.4, bf16[512,1536]{1,0:T(8,128)(2,1)} %collective-permute-done.6.refs_2_.refs_1_, bf16[512,1536]{1,0:T(8,128)(2,1)} %collective-permute-done.13.refs_1_.refs_2_, bf16[512,1536]{1,0:T(8,128)(2,1)} %collective-permute-done.14.refs_2_.refs_3_, ...), custom_call_target="tpu_custom_call" | custom-call | flops 15000000512 | bytes 45000000 | tf_op jit(solution)/shard_map/expert_grads/pallas_call | solution.py:667
  432.1 4.9 out_grads.2.refs_3_
  439.9 3.4 add_convert_fusion.3
  445.0 5.4 out_grads.3
  450.4 21.7 %attend_back.3 = (bf16[384,1024]{1,0:T(8,128)(2,1)}, bf16[256,2048]{1,0:T(8,128)(2,1)}) custom-call(s32[9]{0:T(128)} %pad_add_fusion.s_ref.refs_0_, bf16[384,1024]{1,0:T(8,128)(2,1)} %get-tuple-element.134.q_ref.refs_1_, bf16[384,1024]{1,0:T(8,128)(2,1)} %copy-done.20, f32[6,1024]{1,0:T(8,128)} %pad_maximum_fusion.3.refs_3_, ...), custom_call_target="tpu_custom_call" | custom-call | flops 30000001024 | bytes 90000000 | tf_op jit(solution)/shard_map/attend_back/pallas_call | solution.py:329
  472.1 7.6 %collective-permute-done.22 = bf16[512,1536]{1,0:T(8,128)(2,1)} collective-permute-done((bf16[512,1536]{1,0:T(8,128)(2,1)}, bf16[512,1536]{1,0:T(8,128)(2,1)}, u32[]{:S(2)}, u32[]{:S(2)}) %collective-permute-start.22) | collective-permute-done | bytes 1572896 | tf_op jit(solution)/shard_map/ppermute | solution.py:721
  479.7 7.2 %fusion.5 = bf16[1536,1536]{1,0:T(8,128)(2,1)} fusion(bf16[1536,1536]{1,0:T(8,128)(2,1)} %collective-permute-done.35, bf16[1,1536,1536]{2,1,0:T(8,128)(2,1)} %expert_grads.2), kind=kLoop, calls=%fused_computation.10 | loop fusion | flops 9437184 | bytes 14155776 | tf_op jit(solution)/shard_map/convert_element_type | solution.py:909
  488.6 7.2 %fusion = bf16[1536,1536]{1,0:T(8,128)(2,1)} fusion(bf16[1536,1536]{1,0:T(8,128)(2,1)} %collective-permute-done.37, bf16[1,1536,1536]{2,1,0:T(8,128)(2,1)} %expert_grads.3), kind=kLoop, calls=%fused_computation.5 | loop fusion | flops 9437184 | bytes 14155776 | tf_op jit(solution)/shard_map/convert_element_type | solution.py:909
  498.6 7.2 %collective-permute-start.39 = (bf16[1536,1536]{1,0:T(8,128)(2,1)}, bf16[1536,1536]{1,0:T(8,128)(2,1)}, u32[]{:S(2)}, u32[]{:S(2)}) collective-permute-start(bf16[1536,1536]{1,0:T(8,128)(2,1)} %bitcast.23), channel_id=1, source_target_pairs={{0,8},{25,17},{2,10},{27,19},{4,12},{29,21},{6,14},{31,23}} | collective-permute-start | bytes 14155784 | tf_op jit(solution)/shard_map/ppermute | solution.py:795
  505.8 5.8 input_grads.2
  518.2 9.8 %qkv_grads.1 = (bf16[1536,640]{1,0:T(8,128)(2,1)}, f32[1,1536]{1,0:T(1,128)}) custom-call(bf16[512,1536]{1,0:T(8,128)(2,1)} %fusion.9.refs_0_, bf16[512,1536]{1,0:T(8,128)(2,1)} %collective-permute-done.refs_1_, bf16[512,1536]{1,0:T(8,128)(2,1)} %collective-permute-done.1.refs_0_.refs_2_, bf16[512,1536]{1,0:T(8,128)(2,1)} %copy-done.30, ...), custom_call_target="tpu_custom_call" | custom-call | flops 10000000000 | bytes 30000000 | tf_op jit(solution)/shard_map/qkv_grads/pallas_call | solution.py:396
  530.8 8.1 %collective-permute-start.29 = (f32[10,1536]{1,0:T(8,128)S(1)}, f32[10,1536]{1,0:T(8,128)S(1)}, u32[]{:S(2)}, u32[]{:S(2)}) collective-permute-start(f32[10,1536]{1,0:T(8,128)S(1)} %fusion.24), channel_id=1, source_target_pairs={{0,2},{2,0},{1,3},{3,1},{4,6},{6,4},{5,7},{7,5},{8,10},{10,8},{9,1... | collective-permute-start | bytes 184328 | tf_op jit(solution)/shard_map/ppermute | solution.py:718
  538.9 5.8 input_grads.3
  544.7 11.6 %collective-permute-start.27 = (bf16[512,1536]{1,0:T(8,128)(2,1)}, bf16[512,1536]{1,0:T(8,128)(2,1)}, u32[]{:S(2)}, u32[]{:S(2)}) collective-permute-start(bf16[512,1536]{1,0:T(8,128)(2,1)} %add_convert_fusion.1), channel_id=1, source_target_pairs={{0,2},{2,0},{1,3},{3,1},{4,6},{6,4},{5,7},{7,5},{8,10},{10,8},{9,1... | collective-permute-start | bytes 4718600 | tf_op jit(solution)/shard_map/ppermute | solution.py:718
  556.3 8.6 %collective-permute-done.39 = bf16[1536,1536]{1,0:T(8,128)(2,1)} collective-permute-done((bf16[1536,1536]{1,0:T(8,128)(2,1)}, bf16[1536,1536]{1,0:T(8,128)(2,1)}, u32[]{:S(2)}, u32[]{:S(2)}) %collective-permute-start.39) | collective-permute-done | bytes 4718624 | tf_op jit(solution)/shard_map/ppermute | solution.py:795
  565.0 9.1 %fusion.3 = bf16[1536,1536]{1,0:T(8,128)(2,1)S(1)} fusion(bf16[1536,1536]{1,0:T(8,128)(2,1)} %collective-permute-done.39, bf16[1536,1536]{1,0:T(8,128)(2,1)} %collective-permute-done.38, bf16[1536,1536]{1,0:T(8,128)(2,1)} %collective-permute-done.36, pred[]{:T(512)S(6)} %eq.88, bf16[1,1536,1536]{2,1,0:T(8,128)(2,1)} %expert_grads.3, ...), kind=kLoop, calls=%fused_computation.8 | loop fusion | flops 23592960 | bytes 28311552 | tf_op jit(solution)/shard_map/convert_element_type | solution.py:920
  575.7 10.6 %collective-permute-start.40 = (bf16[768,1536]{1,0:T(8,128)(2,1)}, bf16[768,1536]{1,0:T(8,128)(2,1)}, u32[]{:S(2)}, u32[]{:S(2)}) collective-permute-start(bf16[768,1536]{1,0:T(8,128)(2,1)} %constant_dynamic-slice_fusion), channel_id=1, source_target_pairs={{0,2},{2,0},{8,10},{10,8},{17,19},{19,17},{25,27},{27,25},{4,6},{6... | collective-permute-start | bytes 7077896 | tf_op jit(solution)/shard_map/ppermute | solution.py:924
  590.6 4.4 convert_add_fusion.8
  595.1 7.6 %reduce-scatter.5.cloned.1.call-done = bf16[192,384]{1,0:T(8,128)(2,1)} async-done(((bf16[1536,384]{1,0:T(8,128)(2,1)}), bf16[192,384]{1,0:T(8,128)(2,1)}) %reduce-scatter.5.cloned.1.call-update) | async-done | bytes 147472 | tf_op jit(solution)/shard_map/reduce_scatter | solution.py:892
  613.4 3.2 convert_add_fusion.6
  620.0 4.8 fusion.13
  624.8 13.7 %reduce-scatter.3.cloned.1.call-done = bf16[192,640]{1,0:T(8,128)(2,1)} async-done(((bf16[768,640]{1,0:T(8,128)(2,1)}), bf16[192,640]{1,0:T(8,128)(2,1)}) %reduce-scatter.3.cloned.1.call-update) | async-done | bytes 245776 | tf_op jit(solution)/shard_map/reduce_scatter | solution.py:902
  (195 shorter events, 93.8 us)
Async XLA Ops:
  8.0 594.7 %reduce-scatter.5.cloned.1.call-start = ((), (), s32[]{:S(2)}) async-start(), calls=%async_computation.3 | async-start | bytes 1327104 | tf_op jit(solution)/shard_map/reduce_scatter | solution.py:892
  13.0 10.8 %collective-permute-start = (bf16[512,1536]{1,0:T(8,128)(2,1)}, bf16[512,1536]{1,0:T(8,128)(2,1)}, u32[]{:S(2)}, u32[]{:S(2)}) collective-permute-start(bf16[512,1536]{1,0:T(8,128)(2,1)} %fusion.9.refs_0_), channel_id=1, source_target_pairs={{0,1},{1,0},{2,3},{3,2},{4,5},{5,4},{6,7},{7,6},{8,9},{9,8},{10,11... | collective-permute-start | bytes 4718600 | tf_op jit(solution)/shard_map/ppermute | solution.py:717
  13.0 37.1 %collective-permute-start.1 = (bf16[512,1536]{1,0:T(8,128)(2,1)}, bf16[512,1536]{1,0:T(8,128)(2,1)}, u32[]{:S(2)}, u32[]{:S(2)}) collective-permute-start(bf16[512,1536]{1,0:T(8,128)(2,1)} %fusion.9.refs_0_), channel_id=1, source_target_pairs={{0,2},{2,0},{1,3},{3,1},{4,6},{6,4},{5,7},{7,5},{8,10},{10,8},{9,1... | collective-permute-start | bytes 4718600 | tf_op jit(solution)/shard_map/ppermute | solution.py:718
  30.0 55.9 %collective-permute-start.8 = (bf16[1,1536,1536]{2,1,0:T(8,128)(2,1)}, bf16[1,1536,1536]{2,1,0:T(8,128)(2,1)}, u32[]{:S(2)}, u32[]{:S(2)}) collective-permute-start(bf16[1,1536,1536]{2,1,0:T(8,128)(2,1)} %bitcast.57), channel_id=1, source_target_pairs={{0,8},{8,16},{25,17},{17,9},{2,10},{10,18},{27,19},{19,11},{4,12},... | collective-permute-start | bytes 14155784 | tf_op jit(solution)/shard_map/ppermute | solution.py:795
  50.1 3.6 collective-permute-start.2
  72.5 45.2 %collective-permute-start.4 = (bf16[512,1536]{1,0:T(8,128)(2,1)}, bf16[512,1536]{1,0:T(8,128)(2,1)}, u32[]{:S(2)}, u32[]{:S(2)}) collective-permute-start(bf16[512,1536]{1,0:T(8,128)(2,1)} %get-tuple-element.95), channel_id=1, source_target_pairs={{0,1},{1,0},{2,3},{3,2},{4,5},{5,4},{6,7},{7,6},{8,9},{9,8},{10,11... | collective-permute-start | bytes 4718600 | tf_op jit(solution)/shard_map/ppermute | solution.py:717
  85.9 75.2 %collective-permute-start.9 = (bf16[1,1536,1536]{2,1,0:T(8,128)(2,1)}, bf16[1,1536,1536]{2,1,0:T(8,128)(2,1)}, u32[]{:S(2)}, u32[]{:S(2)}) collective-permute-start(bf16[1,1536,1536]{2,1,0:T(8,128)(2,1)} %collective-permute-done.8.refs_8_.refs_7_), channel_id=1, source_target_pairs={{8,16},{16,24},{17,9},{9,1},{10,18},{18,26},{19,11},{11,3},{12,20}... | collective-permute-start | bytes 14155784 | tf_op jit(solution)/shard_map/ppermute | solution.py:795
  117.6 39.2 %copy-start = (bf16[512,1536]{1,0:T(8,128)(2,1)S(1)}, bf16[512,1536]{1,0:T(8,128)(2,1)}, u32[]{:S(2)}) copy-start(bf16[512,1536]{1,0:T(8,128)(2,1)} %param.15) | copy-start | bytes 4718596
  117.6 39.2 %copy-start.12 = (bf16[512,1536]{1,0:T(8,128)(2,1)S(1)}, bf16[512,1536]{1,0:T(8,128)(2,1)}, u32[]{:S(2)}) copy-start(bf16[512,1536]{1,0:T(8,128)(2,1)} %get-tuple-element.99) | copy-start | bytes 4718596
  117.6 6.0 collective-permute-start.3
  120.1 36.7 %collective-permute-start.5 = (bf16[512,1536]{1,0:T(8,128)(2,1)S(1)}, bf16[512,1536]{1,0:T(8,128)(2,1)S(1)}, u32[]{:S(2)}, u32[]{:S(2)}) collective-permute-start(bf16[512,1536]{1,0:T(8,128)(2,1)S(1)} %add_convert_fusion.4), channel_id=1, source_target_pairs={{0,2},{2,0},{1,3},{3,1},{4,6},{6,4},{5,7},{7,5},{8,10},{10,8},{9,1... | collective-permute-start | bytes 4718600 | tf_op jit(solution)/shard_map/ppermute | solution.py:718
  120.6 95.0 %collective-permute-start.11 = (bf16[1,1536,1536]{2,1,0:T(8,128)(2,1)}, bf16[1,1536,1536]{2,1,0:T(8,128)(2,1)}, u32[]{:S(2)}, u32[]{:S(2)}) collective-permute-start(bf16[1,1536,1536]{2,1,0:T(8,128)(2,1)} %bitcast.58), channel_id=1, source_target_pairs={{8,0},{17,25},{10,2},{19,27},{12,4},{21,29},{14,6},{23,31}} | collective-permute-start | bytes 14155784 | tf_op jit(solution)/shard_map/ppermute | solution.py:795
  122.0 36.0 %copy-start.11 = (bf16[512,1664]{1,0:T(8,128)(2,1)}, bf16[512,1664]{1,0:T(8,128)(2,1)S(1)}, u32[]{:S(2)}) copy-start(bf16[512,1664]{1,0:T(8,128)(2,1)S(1)} %pad_maximum_fusion.1.refs_3_.refs_4_) | copy-start | bytes 5111812
  122.0 42.1 %collective-permute-start.15 = (bf16[512,1664]{1,0:T(8,128)(2,1)S(1)}, bf16[512,1664]{1,0:T(8,128)(2,1)}, u32[]{:S(2)}, u32[]{:S(2)}) collective-permute-start(bf16[512,1664]{1,0:T(8,128)(2,1)S(1)} %pad_maximum_fusion.1.refs_3_.refs_4_), channel_id=1, source_target_pairs={{0,4},{4,0},{1,5},{5,1},{2,6},{6,2},{3,7},{7,3},{8,12},{12,8},{9,1... | collective-permute-start | bytes 5111816 | tf_op jit(solution)/shard_map/ppermute | solution.py:721
  159.6 36.3 %collective-permute-start.13 = (bf16[512,1536]{1,0:T(8,128)(2,1)S(1)}, bf16[512,1536]{1,0:T(8,128)(2,1)}, u32[]{:S(2)}, u32[]{:S(2)}) collective-permute-start(bf16[512,1536]{1,0:T(8,128)(2,1)S(1)} %multiply_convert_fusion.refs_1_.refs_0_), channel_id=1, source_target_pairs={{0,4},{4,0},{1,5},{5,1},{2,6},{6,2},{3,7},{7,3},{8,12},{12,8},{9,1... | collective-permute-start | bytes 4718600 | tf_op jit(solution)/shard_map/ppermute | solution.py:721
  161.2 73.2 %collective-permute-start.10 = (bf16[1,1536,1536]{2,1,0:T(8,128)(2,1)}, bf16[1,1536,1536]{2,1,0:T(8,128)(2,1)}, u32[]{:S(2)}, u32[]{:S(2)}) collective-permute-start(bf16[1,1536,1536]{2,1,0:T(8,128)(2,1)} %collective-permute-done.9.refs_9_.refs_8_), channel_id=1, source_target_pairs={{16,24},{9,1},{18,26},{11,3},{20,28},{13,5},{22,30},{15,7}} | collective-permute-start | bytes 14155784 | tf_op jit(solution)/shard_map/ppermute | solution.py:795
  164.1 37.2 %collective-permute-start.16 = (bf16[512,1664]{1,0:T(8,128)(2,1)}, bf16[512,1664]{1,0:T(8,128)(2,1)}, u32[]{:S(2)}, u32[]{:S(2)}) collective-permute-start(bf16[512,1664]{1,0:T(8,128)(2,1)} %collective-permute-done.15.refs_3_.refs_6_), channel_id=1, source_target_pairs={{0,1},{1,0},{2,3},{3,2},{4,5},{5,4},{6,7},{7,6},{8,9},{9,8},{10,11... | collective-permute-start | bytes 5111816 | tf_op jit(solution)/shard_map/ppermute | solution.py:717
  196.0 19.6 %collective-permute-start.14 = (bf16[512,1536]{1,0:T(8,128)(2,1)}, bf16[512,1536]{1,0:T(8,128)(2,1)}, u32[]{:S(2)}, u32[]{:S(2)}) collective-permute-start(bf16[512,1536]{1,0:T(8,128)(2,1)} %collective-permute-done.13.refs_1_.refs_2_), channel_id=1, source_target_pairs={{0,1},{1,0},{2,3},{3,2},{4,5},{5,4},{6,7},{7,6},{8,9},{9,8},{10,11... | collective-permute-start | bytes 4718600 | tf_op jit(solution)/shard_map/ppermute | solution.py:717
  200.9 63.4 %collective-permute-start.7 = (bf16[512,1664]{1,0:T(8,128)(2,1)}, bf16[512,1664]{1,0:T(8,128)(2,1)}, u32[]{:S(2)}, u32[]{:S(2)}) collective-permute-start(bf16[512,1664]{1,0:T(8,128)(2,1)} %copy-done.11), channel_id=1, source_target_pairs={{0,1},{1,0},{2,3},{3,2},{4,5},{5,4},{6,7},{7,6},{8,9},{9,8},{10,11... | collective-permute-start | bytes 5111816 | tf_op jit(solution)/shard_map/ppermute | solution.py:717
  201.4 62.9 %collective-permute-start.6 = (bf16[512,1536]{1,0:T(8,128)(2,1)}, bf16[512,1536]{1,0:T(8,128)(2,1)}, u32[]{:S(2)}, u32[]{:S(2)}) collective-permute-start(bf16[512,1536]{1,0:T(8,128)(2,1)} %copy-done.4), channel_id=1, source_target_pairs={{0,1},{1,0},{2,3},{3,2},{4,5},{5,4},{6,7},{7,6},{8,9},{9,8},{10,11... | collective-permute-start | bytes 4718600 | tf_op jit(solution)/shard_map/ppermute | solution.py:717
  256.2 49.1 %collective-permute-start.17 = (bf16[512,1664]{1,0:T(8,128)(2,1)}, bf16[512,1664]{1,0:T(8,128)(2,1)}, u32[]{:S(2)}, u32[]{:S(2)}) collective-permute-start(bf16[512,1664]{1,0:T(8,128)(2,1)} %get-tuple-element.124), channel_id=1, source_target_pairs={{0,1},{1,0},{2,3},{3,2},{4,5},{5,4},{6,7},{7,6},{8,9},{9,8},{10,11... | collective-permute-start | bytes 5111816 | tf_op jit(solution)/shard_map/ppermute | solution.py:717
  305.2 25.8 %collective-permute-start.12 = (bf16[512,1664]{1,0:T(8,128)(2,1)}, bf16[512,1664]{1,0:T(8,128)(2,1)}, u32[]{:S(2)}, u32[]{:S(2)}) collective-permute-start(bf16[512,1664]{1,0:T(8,128)(2,1)} %get-tuple-element.117), channel_id=1, source_target_pairs={{0,1},{1,0},{2,3},{3,2},{4,5},{5,4},{6,7},{7,6},{8,9},{9,8},{10,11... | collective-permute-start | bytes 5111816 | tf_op jit(solution)/shard_map/ppermute | solution.py:717
  309.0 39.8 %collective-permute-start.18 = (bf16[512,1664]{1,0:T(8,128)(2,1)}, bf16[512,1664]{1,0:T(8,128)(2,1)}, u32[]{:S(2)}, u32[]{:S(2)}) collective-permute-start(bf16[512,1664]{1,0:T(8,128)(2,1)} %add_convert_fusion), channel_id=1, source_target_pairs={{0,4},{4,0},{1,5},{5,1},{2,6},{6,2},{3,7},{7,3},{8,12},{12,8},{9,1... | collective-permute-start | bytes 5111816 | tf_op jit(solution)/shard_map/ppermute | solution.py:721
  328.1 77.4 %collective-permute-start.34 = (bf16[1536,1536]{1,0:T(8,128)(2,1)}, bf16[1536,1536]{1,0:T(8,128)(2,1)}, u32[]{:S(2)}, u32[]{:S(2)}) collective-permute-start(bf16[1536,1536]{1,0:T(8,128)(2,1)} %bitcast.55), channel_id=1, source_target_pairs={{24,16},{1,9},{26,18},{3,11},{28,20},{5,13},{30,22},{7,15}} | collective-permute-start | bytes 14155784 | tf_op jit(solution)/shard_map/ppermute | solution.py:795
  357.2 11.4 %collective-permute-start.19 = (bf16[512,1536]{1,0:T(8,128)(2,1)}, bf16[512,1536]{1,0:T(8,128)(2,1)}, u32[]{:S(2)}, u32[]{:S(2)}) collective-permute-start(bf16[512,1536]{1,0:T(8,128)(2,1)} %get-tuple-element.133.refs_10_.refs_0_), channel_id=1, source_target_pairs={{0,1},{1,0},{2,3},{3,2},{4,5},{5,4},{6,7},{7,6},{8,9},{9,8},{10,11... | collective-permute-start | bytes 4718600 | tf_op jit(solution)/shard_map/ppermute | solution.py:717
  358.0 46.9 %copy-start.20 = (bf16[384,1024]{1,0:T(8,128)(2,1)}, bf16[384,1024]{1,0:T(8,128)(2,1)S(1)}, u32[]{:S(2)}) copy-start(bf16[384,1024]{1,0:T(8,128)(2,1)S(1)} %constant_dynamic-update-slice_fusion.refs_2_) | copy-start | bytes 2359300
  358.0 47.2 %collective-permute-start.23 = (bf16[512,1536]{1,0:T(8,128)(2,1)}, bf16[512,1536]{1,0:T(8,128)(2,1)}, u32[]{:S(2)}, u32[]{:S(2)}) collective-permute-start(bf16[512,1536]{1,0:T(8,128)(2,1)} %get-tuple-element.133.refs_10_.refs_0_), channel_id=1, source_target_pairs={{0,2},{2,0},{1,3},{3,1},{4,6},{6,4},{5,7},{7,5},{8,10},{10,8},{9,1... | collective-permute-start | bytes 4718600 | tf_op jit(solution)/shard_map/ppermute | solution.py:718
  404.9 35.0 %collective-permute-start.21 = (bf16[512,1536]{1,0:T(8,128)(2,1)}, bf16[512,1536]{1,0:T(8,128)(2,1)}, u32[]{:S(2)}, u32[]{:S(2)}) collective-permute-start(bf16[512,1536]{1,0:T(8,128)(2,1)} %get-tuple-element.130), channel_id=1, source_target_pairs={{0,1},{1,0},{2,3},{3,2},{4,5},{5,4},{6,7},{7,6},{8,9},{9,8},{10,11... | collective-permute-start | bytes 4718600 | tf_op jit(solution)/shard_map/ppermute | solution.py:717
  405.2 39.8 %collective-permute-start.24 = (bf16[512,1536]{1,0:T(8,128)(2,1)}, bf16[512,1536]{1,0:T(8,128)(2,1)}, u32[]{:S(2)}, u32[]{:S(2)}) collective-permute-start(bf16[512,1536]{1,0:T(8,128)(2,1)} %collective-permute-done.23.refs_0_.refs_10_), channel_id=1, source_target_pairs={{0,1},{1,0},{2,3},{3,2},{4,5},{5,4},{6,7},{7,6},{8,9},{9,8},{10,11... | collective-permute-start | bytes 4718600 | tf_op jit(solution)/shard_map/ppermute | solution.py:717
  412.7 67.0 %collective-permute-start.35 = (bf16[1536,1536]{1,0:T(8,128)(2,1)}, bf16[1536,1536]{1,0:T(8,128)(2,1)}, u32[]{:S(2)}, u32[]{:S(2)}) collective-permute-start(bf16[1536,1536]{1,0:T(8,128)(2,1)} %fusion.4), channel_id=1, source_target_pairs={{16,8},{9,17},{18,10},{11,19},{20,12},{13,21},{22,14},{15,23}} | collective-permute-start | bytes 14155784 | tf_op jit(solution)/shard_map/ppermute | solution.py:795
  437.0 51.6 %collective-permute-start.37 = (bf16[1536,1536]{1,0:T(8,128)(2,1)}, bf16[1536,1536]{1,0:T(8,128)(2,1)}, u32[]{:S(2)}, u32[]{:S(2)}) collective-permute-start(bf16[1536,1536]{1,0:T(8,128)(2,1)} %bitcast.23), channel_id=1, source_target_pairs={{24,16},{1,9},{26,18},{3,11},{28,20},{5,13},{30,22},{7,15}} | collective-permute-start | bytes 14155784 | tf_op jit(solution)/shard_map/ppermute | solution.py:795
  443.4 36.3 %collective-permute-start.22 = (bf16[512,1536]{1,0:T(8,128)(2,1)}, bf16[512,1536]{1,0:T(8,128)(2,1)}, u32[]{:S(2)}, u32[]{:S(2)}) collective-permute-start(bf16[512,1536]{1,0:T(8,128)(2,1)} %add_convert_fusion.3), channel_id=1, source_target_pairs={{0,4},{4,0},{1,5},{5,1},{2,6},{6,2},{3,7},{7,3},{8,12},{12,8},{9,1... | collective-permute-start | bytes 4718600 | tf_op jit(solution)/shard_map/ppermute | solution.py:721
  486.9 57.8 %collective-permute-start.36 = (bf16[1536,1536]{1,0:T(8,128)(2,1)}, bf16[1536,1536]{1,0:T(8,128)(2,1)}, u32[]{:S(2)}, u32[]{:S(2)}) collective-permute-start(bf16[1536,1536]{1,0:T(8,128)(2,1)} %fusion.5), channel_id=1, source_target_pairs={{8,0},{17,25},{10,2},{19,27},{12,4},{21,29},{14,6},{23,31}} | collective-permute-start | bytes 14155784 | tf_op jit(solution)/shard_map/ppermute | solution.py:795
  495.8 60.5 %collective-permute-start.38 = (bf16[1536,1536]{1,0:T(8,128)(2,1)}, bf16[1536,1536]{1,0:T(8,128)(2,1)}, u32[]{:S(2)}, u32[]{:S(2)}) collective-permute-start(bf16[1536,1536]{1,0:T(8,128)(2,1)} %fusion), channel_id=1, source_target_pairs={{16,8},{9,17},{18,10},{11,19},{20,12},{13,21},{22,14},{15,23}} | collective-permute-start | bytes 14155784 | tf_op jit(solution)/shard_map/ppermute | solution.py:795
  498.6 66.4 %collective-permute-start.39 = (bf16[1536,1536]{1,0:T(8,128)(2,1)}, bf16[1536,1536]{1,0:T(8,128)(2,1)}, u32[]{:S(2)}, u32[]{:S(2)}) collective-permute-start(bf16[1536,1536]{1,0:T(8,128)(2,1)} %bitcast.23), channel_id=1, source_target_pairs={{0,8},{25,17},{2,10},{27,19},{4,12},{29,21},{6,14},{31,23}} | collective-permute-start | bytes 14155784 | tf_op jit(solution)/shard_map/ppermute | solution.py:795
  511.6 3.6 collective-permute-start.26
  528.7 1.4 collective-permute-start.28
  528.9 58.8 %collective-permute-start.20 = (bf16[512,1536]{1,0:T(8,128)(2,1)}, bf16[512,1536]{1,0:T(8,128)(2,1)}, u32[]{:S(2)}, u32[]{:S(2)}) collective-permute-start(bf16[512,1536]{1,0:T(8,128)(2,1)} %get-tuple-element.126), channel_id=1, source_target_pairs={{0,1},{1,0},{2,3},{3,2},{4,5},{5,4},{6,7},{7,6},{8,9},{9,8},{10,11... | collective-permute-start | bytes 4718600 | tf_op jit(solution)/shard_map/ppermute | solution.py:717
  529.3 109.2 %reduce-scatter.3.cloned.1.call-start = ((), (), s32[]{:S(2)}) async-start(), calls=%async_computation.2 | async-start | bytes 1228800 | tf_op jit(solution)/shard_map/reduce_scatter | solution.py:902
  530.8 13.9 %collective-permute-start.29 = (f32[10,1536]{1,0:T(8,128)S(1)}, f32[10,1536]{1,0:T(8,128)S(1)}, u32[]{:S(2)}, u32[]{:S(2)}) collective-permute-start(f32[10,1536]{1,0:T(8,128)S(1)} %fusion.24), channel_id=1, source_target_pairs={{0,2},{2,0},{1,3},{3,1},{4,6},{6,4},{5,7},{7,5},{8,10},{10,8},{9,1... | collective-permute-start | bytes 184328 | tf_op jit(solution)/shard_map/ppermute | solution.py:718
  544.7 63.6 %collective-permute-start.25 = (bf16[512,1536]{1,0:T(8,128)(2,1)}, bf16[512,1536]{1,0:T(8,128)(2,1)}, u32[]{:S(2)}, u32[]{:S(2)}) collective-permute-start(bf16[512,1536]{1,0:T(8,128)(2,1)} %get-tuple-element.145), channel_id=1, source_target_pairs={{0,1},{1,0},{2,3},{3,2},{4,5},{5,4},{6,7},{7,6},{8,9},{9,8},{10,11... | collective-permute-start | bytes 4718600 | tf_op jit(solution)/shard_map/ppermute | solution.py:717
  544.7 63.6 %collective-permute-start.27 = (bf16[512,1536]{1,0:T(8,128)(2,1)}, bf16[512,1536]{1,0:T(8,128)(2,1)}, u32[]{:S(2)}, u32[]{:S(2)}) collective-permute-start(bf16[512,1536]{1,0:T(8,128)(2,1)} %add_convert_fusion.1), channel_id=1, source_target_pairs={{0,2},{2,0},{1,3},{3,1},{4,6},{6,4},{5,7},{7,5},{8,10},{10,8},{9,1... | collective-permute-start | bytes 4718600 | tf_op jit(solution)/shard_map/ppermute | solution.py:718
  556.3 31.0 %collective-permute-start.30 = (f32[10,1536]{1,0:T(8,128)S(1)}, f32[10,1536]{1,0:T(8,128)S(1)}, u32[]{:S(2)}, u32[]{:S(2)}) collective-permute-start(f32[10,1536]{1,0:T(8,128)S(1)} %add.200), channel_id=1, source_target_pairs={{0,4},{4,0},{1,5},{5,1},{2,6},{6,2},{3,7},{7,3},{8,12},{12,8},{9,1... | collective-permute-start | bytes 184328 | tf_op jit(solution)/shard_map/ppermute | solution.py:721
  575.7 37.7 %collective-permute-start.40 = (bf16[768,1536]{1,0:T(8,128)(2,1)}, bf16[768,1536]{1,0:T(8,128)(2,1)}, u32[]{:S(2)}, u32[]{:S(2)}) collective-permute-start(bf16[768,1536]{1,0:T(8,128)(2,1)} %constant_dynamic-slice_fusion), channel_id=1, source_target_pairs={{0,2},{2,0},{8,10},{10,8},{17,19},{19,17},{25,27},{27,25},{4,6},{6... | collective-permute-start | bytes 7077896 | tf_op jit(solution)/shard_map/ppermute | solution.py:924
  587.3 18.2 %collective-permute-start.33 = (bf16[4,192,640]{2,1,0:T(8,128)(2,1)}, bf16[4,192,640]{2,1,0:T(8,128)(2,1)}, u32[]{:S(2)}, u32[]{:S(2)}) collective-permute-start(bf16[4,192,640]{2,1,0:T(8,128)(2,1)} %dynamic-slice_bitcast_fusion), channel_id=1, source_target_pairs={{0,4},{4,0},{1,5},{5,1},{2,6},{6,2},{3,7},{7,3},{8,12},{12,8},{9,1... | collective-permute-start | bytes 2949128 | tf_op jit(solution)/shard_map/ppermute | solution.py:721
  587.7 7.3 %collective-permute-start.31 = (f32[10,1536]{1,0:T(8,128)S(1)}, f32[10,1536]{1,0:T(8,128)S(1)}, u32[]{:S(2)}, u32[]{:S(2)}) collective-permute-start(f32[10,1536]{1,0:T(8,128)S(1)} %add.201), channel_id=1, source_target_pairs={{0,8},{8,0},{16,24},{24,16},{1,9},{9,1},{17,25},{25,17},{2,10},{10... | collective-permute-start | bytes 184328 | tf_op jit(solution)/shard_map/ppermute | solution.py:754
  595.0 9.3 %collective-permute-start.32 = (f32[10,1536]{1,0:T(8,128)S(1)}, f32[10,1536]{1,0:T(8,128)S(1)}, u32[]{:S(2)}, u32[]{:S(2)}) collective-permute-start(f32[10,1536]{1,0:T(8,128)S(1)} %add.202), channel_id=1, source_target_pairs={{0,16},{8,24},{16,0},{24,8},{1,17},{9,25},{17,1},{25,9},{2,18},{10... | collective-permute-start | bytes 184328 | tf_op jit(solution)/shard_map/ppermute | solution.py:754
  620.0 21.7 %collective-permute-start.41 = (bf16[384,1536]{1,0:T(8,128)(2,1)}, bf16[384,1536]{1,0:T(8,128)(2,1)}, u32[]{:S(2)}, u32[]{:S(2)}) collective-permute-start(bf16[384,1536]{1,0:T(8,128)(2,1)} %dynamic-slice_convert_fusion), channel_id=1, source_target_pairs={{0,1},{1,0},{2,3},{3,2},{4,5},{5,4},{6,7},{7,6},{8,9},{9,8},{10,11... | collective-permute-start | bytes 3538952 | tf_op jit(solution)/shard_map/ppermute | solution.py:717
  (27 other events, 202.1 us)
Sparse Core Ops, SparseCore 0:
  529.4 73.2 reduce-scatter.4
Sparse Core Ops, SparseCore 1:
  608.4 30.1 reduce-scatter.2

commit v3 on v2

--- a/solution.py
+++ b/solution.py
@@ -30,7 +30,7 @@
 
 def cost(micros):
     return pl.CostEstimate(
-        flops=int(micros * 1e9), transcendentals=0, bytes_accessed=int(micros * 3e6)
+        flops=int(micros * 1e+09), transcendentals=0, bytes_accessed=int(micros * 3e+06)
     )
 
 
@@ -101,7 +101,7 @@
         out_shape=[jax.ShapeDtypeStruct((q_cols, size), BF16)] + kv_shapes,
         input_output_aliases={parts + 3 + i: 1 + i for i in range(len(previous))},
         compiler_params=params(),
-        cost_estimate=cost(6),
+        cost_estimate=cost(0.5),
         name="qkv",
     )(*h_parts, w_all, cos, sin, *previous)
 
@@ -211,7 +211,7 @@
         ]
         + [jax.ShapeDtypeStruct((rows, width), BF16)] * count,
         compiler_params=params(),
-        cost_estimate=cost(9 * count),
+        cost_estimate=cost(3 * count),
         name="attend",
     )(scalars, q, k, vt, w_out)
 
@@ -434,7 +434,7 @@
     )(*inputs)
 
 
-def expert_kernel(experts, adds, choices, *refs):
+def expert_kernel(experts, adds, choices, alone, *refs):
     s_ref, h0, h1, dy0, dy1, router_ref = refs[:6]
     w_choices = refs[6 : 6 + choices]
     old = refs[6 + choices : 6 + choices + (4 if adds else 0)]
@@ -479,20 +479,28 @@
     def _():
         fetch_weights(e + 1, 1 - slot)
 
-    for i in range(2):
+    def block(i, carry):
+        for n in range(2):
+
+            @pl.when((e == 0) & (i == n))
+            def _():
+                tokens_in[2 * n].wait()
+                tokens_in[2 * n + 1].wait()
+                for copy in old_in[n::2]:
+                    copy.wait()
 
         @pl.when(e == 0)
         def _():
-            tokens_in[2 * i].wait()
             logits = dot(h_s[i], router_ref[...])
             logits = jnp.where(lane < experts, logits, MASK_FILL)
             weights = jnp.exp(logits - jnp.max(logits, axis=1, keepdims=True))
             weights = weights / jnp.sum(weights, axis=1, keepdims=True)
-            tokens_in[2 * i + 1].wait()
             gates[i] = weights * dy_s[i, :, width:].astype(F32)
 
-        if i == 0:
+        @pl.when(i == 0)
+        def _():
             pltpu.make_async_copy(w_choices[0].at[0], w_s.at[slot], in_sem.at[4 + slot]).wait()
+
         mine = lane == s_ref[1 + e]
         gate = jnp.sum(jnp.where(mine, gates[i], 0.0), axis=1, keepdims=True)
         both = dot(h_s[i], w_s[slot, :, : 2 * hidden])
@@ -507,55 +515,71 @@
         dact = gate * dact
         dgp = (dact * up * sg * (1.0 + gp * (1.0 - sg))).astype(BF16)
         dup = (dact * silu).astype(BF16)
+        here = pl.ds(pl.multiple_of(i * rows, rows), rows)
+        act_copy = pltpu.make_async_copy(act_o.at[i], act_out.at[e, here, :], out_sem.at[i])
+        dgu_copy = pltpu.make_async_copy(dgu_o.at[i], dgu_out.at[e, here, :], out_sem.at[2 + i])
 
         @pl.when(e > 0)
         def _():
-            pltpu.make_async_copy(
-                act_o.at[i], act_out.at[0, pl.ds(0, rows), :], out_sem.at[i]
-            ).wait()
-            pltpu.make_async_copy(
-                dgu_o.at[i], dgu_out.at[0, pl.ds(0, rows), :], out_sem.at[2 + i]
-            ).wait()
+            act_copy.wait()
+            dgu_copy.wait()
 
         act_o[i] = scaled
         dgu_o[i, :, :hidden] = dgp
         dgu_o[i, :, hidden:] = dup
-        here = pl.ds(i * rows, rows)
-        pltpu.make_async_copy(act_o.at[i], act_out.at[e, here, :], out_sem.at[i]).start()
-        pltpu.make_async_copy(dgu_o.at[i], dgu_out.at[e, here, :], out_sem.at[2 + i]).start()
+        act_copy.start()
+        dgu_copy.start()
         mix = dot(scaled, w_s[slot, :, 2 * hidden :], 1, 1)
         dh = dot(dgu_o[i], w_s[slot, :, : 2 * hidden], 1, 1)
 
-        @pl.when(e == 0)
-        def _():
-            if adds:
-                old_in[i].wait()
-                old_in[2 + i].wait()
-                mix_s[i] = mix + mix_o[i].astype(F32)
-                dh_s[i] = dh + dh_o[i, :, :width].astype(F32)
-                kept = dh_o[i, :, width:].astype(F32)
-                kept = kept + pltpu.roll(kept, LANES // 2, 1)
-                dgate[i] = own_dgate + jnp.where(lane < LANES // 2, kept, 0.0)
-            else:
-                mix_s[i] = mix
-                dh_s[i] = dh
-                dgate[i] = own_dgate
-
-        @pl.when(e > 0)
-        def _():
-            mix_s[i] += mix
-            dh_s[i] += dh
-            dgate[i] += own_dgate
-
-        @pl.when(e == last)
-        def _():
-            mix_o[i] = mix_s[i].astype(BF16)
-            dh_o[i, :, :width] = dh_s[i].astype(BF16)
-            high = dgate[i].astype(BF16).astype(F32)
-            low = dgate[i] - high
+        def finish(mix, dh, own_dgate):
+            mix_o[i] = mix.astype(BF16)
+            dh_o[i, :, :width] = dh.astype(BF16)
+            high = own_dgate.astype(BF16).astype(F32)
+            low = own_dgate - high
             dh_o[i, :, width:] = (high + pltpu.roll(low, LANES // 2, 1)).astype(BF16)
-            pltpu.make_async_copy(mix_o.at[i], (mix0, mix1)[i], out_sem.at[4 + i]).start()
-            pltpu.make_async_copy(dh_o.at[i], (dh0, dh1)[i], out_sem.at[6 + i]).start()
+
+        if adds:
+            kept = dh_o[i, :, width:].astype(F32)
+            kept = kept + pltpu.roll(kept, LANES // 2, 1)
+            kept = jnp.where(lane < LANES // 2, kept, 0.0)
+        if adds and alone:
+            finish(mix + mix_o[i].astype(F32), dh + dh_o[i, :, :width].astype(F32), own_dgate + kept)
+        elif alone:
+            finish(mix, dh, own_dgate)
+        else:
+
+            @pl.when(e == 0)
+            def _():
+                if adds:
+                    mix_s[i] = mix + mix_o[i].astype(F32)
+                    dh_s[i] = dh + dh_o[i, :, :width].astype(F32)
+                    dgate[i] = own_dgate + kept
+                else:
+                    mix_s[i] = mix
+                    dh_s[i] = dh
+                    dgate[i] = own_dgate
+
+            @pl.when(e > 0)
+            def _():
+                mix_s[i] += mix
+                dh_s[i] += dh
+                dgate[i] += own_dgate
+
+            @pl.when(e == last)
+            def _():
+                finish(mix_s[i], dh_s[i], dgate[i])
+
+        for n in range(2):
+
+            @pl.when((e == last) & (i == n))
+            def _():
+                pltpu.make_async_copy(mix_o.at[n], (mix0, mix1)[n], out_sem.at[4 + n]).start()
+                pltpu.make_async_copy(dh_o.at[n], (dh0, dh1)[n], out_sem.at[6 + n]).start()
+
+        return carry
+
+    lax.fori_loop(0, 2, block, 0)
 
     @pl.when(e == last)
     def _():
@@ -574,7 +598,7 @@
     hidden = cols // 3
     anywhere = pl.BlockSpec(memory_space=pl.ANY)
     return pl.pallas_call(
-        functools.partial(expert_kernel, experts, bool(old), len(choices)),
+        functools.partial(expert_kernel, experts, bool(old), len(choices), mine == 1),
         grid_spec=pltpu.PrefetchScalarGridSpec(
             num_scalar_prefetch=1,
             grid=(mine,),
@@ -648,7 +672,15 @@
 
     for copy in per_expert[:2]:
         copy.wait()
-    out_ref[0, :, : 2 * hidden] = dot(h_s[...], dgu_s[...], 0, 0).astype(BF16)
+
+    def rows_of(c):
+        return pl.ds(pl.multiple_of(c * (width // 3), width // 3), width // 3)
+
+    def gate_up(c, carry):
+        out_ref[0, rows_of(c), : 2 * hidden] = dot(h_s[:, rows_of(c)], dgu_s[...], 0, 0).astype(BF16)
+        return carry
+
+    lax.fori_loop(0, 3, gate_up, 0)
 
     @pl.when(e == 0)
     def _():
@@ -657,7 +689,12 @@
 
     for copy in per_expert[2:]:
         copy.wait()
-    out_ref[0, :, 2 * hidden :] = dot(dy_s[...], act_s[...], 0, 0).astype(BF16)
+
+    def down(c, carry):
+        out_ref[0, rows_of(c), 2 * hidden :] = dot(dy_s[:, rows_of(c)], act_s[...], 0, 0).astype(BF16)
+        return carry
+
+    lax.fori_loop(0, 3, down, 0)
 
 
 def expert_grads(h_parts, dy_parts, acts, dgus):
@@ -678,7 +715,7 @@
             pltpu.SemaphoreType.DMA((12,)),
         ],
         compiler_params=params(),
-        cost_estimate=cost(15),
+        cost_estimate=cost(8),
         name="expert_grads",
     )(*h_parts, *dy_parts, *acts, *dgus)
 
@@ -722,37 +759,26 @@
 
     bits = blocks.bit_length() - 1
 
-    def tp_gather(value):
-        held = {0: value}
-        for bit in reversed(range(bits)):
-            for i in list(held):
-                held[i | (1 << bit)] = tp_swap(held[i], bit)
-        return [held[i] for i in range(blocks)]
-
-    def tp_scatter(parts):
+    def fold(parts, kind):
         parts = dict(enumerate(parts))
-        for bit in range(bits):
+        for bit in range(bits - 1):
             for i in sorted(parts, reverse=True):
                 if i & (1 << bit):
                     parts[i] = tp_swap(parts[i], bit)
             for i in sorted(parts, reverse=True):
                 if i & (1 << bit):
-                    other = parts.pop(i)
-                    base = parts[i ^ (1 << bit)].astype(F32) + other.astype(F32)
-                    last = i == 1 << bit and bit == bits - 1
-                    parts[i ^ (1 << bit)] = base if last else base.astype(BF16)
-            if bit == bits - 2:
-                side, own = parts[1 << (bits - 1)], parts[0]
-        return parts[0], side, own
+                    total = parts[i ^ (1 << bit)].astype(F32) + parts.pop(i).astype(F32)
+                    parts[i ^ (1 << bit)] = total.astype(BF16 if bit < bits - 2 else kind)
+        return parts[0]
 
     def sum_all(value):
-        for bit in range(bits):
-            value = value + tp_swap(value, bit)
-        value = value + y_swap(value)
         step = 1
         while step < nz:
             value = value + lax.ppermute(value, "z", [(i, i ^ step) for i in range(nz)])
             step *= 2
+        value = value + y_swap(value)
+        for bit in range(bits):
+            value = value + tp_swap(value, bit)
         return value
 
     def own_columns(value):
@@ -763,9 +789,14 @@
     x = tokens.astype(F32)
     r1 = lax.rsqrt(jnp.mean(x * x, axis=-1, keepdims=True) + EPSILON)
     h1 = (x * r1 * norm1_gain).astype(BF16)
-    h_parts = tp_gather(h1)
-
-    w_all_t = jnp.concatenate([w_query, key_weight, value_weight], axis=1).T
+    h_parts = {0: h1}
+    for bit in reversed(range(bits)):
+        for i in list(h_parts):
+            if i < half:
+                h_parts[i | (1 << bit)] = tp_swap(h_parts[i], bit)
+
+    w_all = jnp.concatenate([w_query, key_weight, value_weight], axis=1)
+    w_all_t = w_all.T
     order = me ^ jnp.arange(blocks, dtype=jnp.int32)
     position = (order[:, None] * rows + jnp.arange(rows, dtype=jnp.int32)[None, :]).reshape(-1)
     frequency = ROPE_BASE ** (-(jnp.arange(HALF, dtype=F32) * (2.0 / HEAD_SIZE)))
@@ -774,7 +805,14 @@
     scalars = jnp.concatenate(
         [me.astype(jnp.int32)[None], piece_first_position[0], piece_length[0]]
     )
-    q_near, *kv = project_qkv(h_parts[:half], w_all_t, cos, sin, q_cols, kv_cols, 0, None)
+    near_rows = [h_parts[i] for i in range(half)]
+    q_near, *kv = project_qkv(near_rows, w_all_t, cos, sin, q_cols, kv_cols, 0, None)
+    h_parts[half] = after(h_parts[half], q_near)
+    for bit in reversed(range(bits - 1)):
+        for i in list(h_parts):
+            if i >= half:
+                h_parts[i | (1 << bit)] = tp_swap(h_parts[i], bit)
+    h_parts = [h_parts[i] for i in range(blocks)]
 
     mask = jnp.zeros((rows, LANES), jnp.bool_)
     for j in range(routes.shape[1]):
@@ -784,7 +822,7 @@
 
     mine = nz // 2
     cut = mine // 2
-    weight = after(jnp.concatenate([w_gate[0], w_up[0], w_down[0].T], axis=1), q_near)[None]
+    weight = after(jnp.concatenate([w_gate[0], w_up[0], w_down[0].T], axis=1), h_parts[1])[None]
     if nz == 4:
         ids = jnp.where(ic == 0, jnp.arange(2), 3 - jnp.arange(2)) * 2 + iy
         along = jnp.where(ic == 0, iz, 3 - iz)
@@ -806,15 +844,22 @@
         scalars, q, at, count, k, vt, w_out, rows, zone, base
     )
     o_3, lse_3, *out_3 = run(q_far, quarter, quarter, half + quarter)
+    early = ()
     if nz == 4:
+        early = (from_outer,)
         second = shift(after(from_outer, out_3[0]), [(1, 2), (2, 3)])
-    o_2, lse_2, *out_2 = run(after(q_far, out_3[0]), 0, quarter, half)
-    o_near, lse_near, *out_near = run(after(q_near, out_2[0]), 0, half, 0)
+    o_2, lse_2, *out_2 = run(after(q_far, out_3[0], *early), 0, quarter, half)
+    side = fold([*out_2, *out_3], BF16)
+    if nz == 4:
+        o_near, lse_near, *out_near = run(after(q_near, side), 0, half, 0)
+    else:
+        o_near, lse_near, *out_near = run(after(q_near, side), 0, half, 0)
     o_far = jnp.concatenate([o_2, o_3], axis=1)
     lse_far = jnp.concatenate([lse_2, lse_3], axis=1)
     dy_parts = [dy_own, tp_swap(after(dy_own, out_3[0]), 0), dy_side]
     dy_parts.append(tp_swap(after(dy_side, out_2[0]), 0))
-    attended, _, near_sum = tp_scatter([*out_near, *out_2, *out_3])
+    near_sum = fold(out_near, F32)
+    attended = near_sum + after(tp_swap(side, bits - 1), out_near[0]).astype(F32)
     if nz == 4:
         third = shift(after(second, near_sum), [(2, 3)])
         outer = (weight, from_outer, second, third)
@@ -823,29 +868,29 @@
         every = lax.all_gather(weight, "z", axis=0, tiled=True)
         every = lax.dynamic_slice_in_dim(every, ic * mine, mine, 0)
         outer, inner = (every[:cut],), (every[cut:],)
-    x1 = x + attended
+    x1 = (after(x, second, dy_side, from_inner) if nz == 4 else x) + attended
     r2 = lax.rsqrt(jnp.mean(x1 * x1, axis=-1, keepdims=True) + EPSILON)
     n2 = x1 * r2
     h2 = (n2 * norm2_gain).astype(BF16)
 
     router_wide = jnp.pad(w_router, ((0, 0), (0, LANES - experts)))
     h2_side = y_swap(h2)
-    h2_parts = [h2, tp_swap(h2, 0), h2_side, tp_swap(h2_side, 0)]
+    h2_parts = [h2, tp_swap(h2, 0), h2_side]
     head = along.astype(jnp.int32)[None]
     outer_ids = jnp.concatenate([head, ids[:cut].astype(jnp.int32)])
     inner_ids = jnp.concatenate([head, ids[cut:].astype(jnp.int32)])
     through = lambda s, at, w, old=(): run_experts(
-        s, h2_parts[at : at + 2], dy_parts[at : at + 2], router_wide, w, experts, 18 * cut, old
+        s, h2_parts[at : at + 2], dy_parts[at : at + 2], router_wide, w, experts, 8 * cut, old
     )
     first = through(inner_ids, 0, inner)
-    near = through(outer_ids, 0, outer, first[:4])
+    h2_parts.append(tp_swap(after(h2_side, first[4]), 0))
     third_pass = through(inner_ids, 2, inner)
-    far = through(outer_ids, 2, outer, third_pass[:4])
+    near = through(after(outer_ids, third_pass[4]), 0, outer, first[:4])
+    far = through(after(outer_ids, near[4]), 2, outer, third_pass[:4])
 
     join = lambda a, b: (a.astype(F32) + tp_swap(b, 0).astype(F32)).astype(BF16)
     dh_side = join(far[2], far[3])
     dh_own = near[2].astype(F32) + tp_swap(near[3], 0).astype(F32)
-    dh_sum = dh_own + y_swap(dh_side).astype(F32)
     grads_outer = expert_grads(
         [after(h2_parts[0], dh_side), *h2_parts[1:]], dy_parts, (near[4], far[4]), (near[5], far[5])
     )
@@ -855,7 +900,9 @@
         (first[4], third_pass[4]),
         (first[5], third_pass[5]),
     )
-
+    mixed_side = join(far[0], after(far[1], grads_outer))
+    mixed_core = tp_swap(after(near[1], grads_outer), 0)
+    dh_sum = after(dh_own, grads_inner, mixed_side, mixed_core) + after(y_swap(dh_side), grads_outer).astype(F32)
     probs = jax.nn.softmax(dot(h2, w_router), axis=-1)
     dprobs = dh_sum[:, width : width + experts]
     dprobs = dprobs + dh_sum[:, width + LANES // 2 : width + LANES // 2 + experts]
@@ -870,67 +917,100 @@
     router_part = dot(dlogits, h2, 0, 0)
     gain2 = jnp.sum(dh2 * n2, axis=0, keepdims=True)
 
-    da_parts = tp_gather(dx1.astype(BF16))
+    if nz == 4:
+        reduce = lambda g, axis: lax.psum_scatter(g, axis, scatter_dimension=0, tiled=True)
+        inner, outer = reduce(grads_inner[0], "z"), reduce(grads_outer[0], "z")
+    else:
+        inner, outer = grads_inner, grads_outer
+
+    da = dx1.astype(BF16)
+    da_parts = {0: da}
+    for bit in reversed(range(bits)):
+        for i in list(da_parts):
+            if i < half:
+                da_parts[i | (1 << bit)] = tp_swap(da_parts[i], bit)
     back = lambda q, o, lse, da, base, sums: attend_back(
         scalars, q, o, lse, k, kt, v, cos, sin, w_out, da, rows, zone, base, sums
     )
-    dq_near, *sums = back(q_near, o_near, lse_near, da_parts[:half], 0, None)
-    out_part = out_grads([after(da_parts[0], dq_near), *da_parts[1:half]], o_near, None)
+    near_parts = [da_parts[i] for i in range(half)]
+    dq_near, *sums = back(q_near, o_near, lse_near, near_parts, 0, None)
+    da_parts[half] = after(da_parts[half], dq_near)
+    for bit in reversed(range(bits - 1)):
+        for i in list(da_parts):
+            if i >= half:
+                da_parts[i | (1 << bit)] = tp_swap(da_parts[i], bit)
+    da_parts = [da_parts[i] for i in range(blocks)]
+    mixed_side = y_swap(after(mixed_side, da))
+    out_part = out_grads(
+        [after(da_parts[0], dq_near, mixed_side), *da_parts[1:half]], o_near, None
+    )
     out_part = out_grads(da_parts[half:], o_far, out_part)
-    mixed_side = join(after(far[0], dq_near), after(far[1], dq_near))
-    mixed_own = near[0].astype(F32) + tp_swap(after(near[1], dq_near), 0).astype(F32)
-    dq_far, dkv = back(after(q_far, out_part, mixed_side), o_far, lse_far, da_parts[half:], half, sums)
-    mixed_side = y_swap(mixed_side)
-    output = x1 + mixed_own + mixed_side.astype(F32)
-    dh1_far = input_grads(after(dq_far, mixed_side), dkv, w_all_t, rows, 1)
-    dh1_near = input_grads(dq_near, after(dkv, dh1_far[0]), w_all_t, rows, 0)
-    dh1, dh1_side, _ = tp_scatter([*dh1_near, *dh1_far])
+    each = width // (2 * nz)
+
+    def pick(grad, at):
+        grad = grad.reshape(nz, 2, each, grad.shape[1])
+        return lax.dynamic_index_in_dim(grad, at, 1, keepdims=False)
+
+    before = [out_part]
+    if nz == 4:
+
+        def x_reduce(g, cover):
+            pick_rows = lambda at: lax.dynamic_slice_in_dim(g, at * (width // 8), width // 8, 0)
+            other = after(tp_swap(pick_rows(1 - ix), 1), cover)
+            return (pick_rows(ix).astype(F32) + other.astype(F32)).astype(BF16)
+
+        before.append(outer)
+    dq_far, dkv = back(after(q_far, *before), o_far, lse_far, da_parts[half:], half, sums)
+    out_side = after(y_swap(pick(out_part, 1 - iy)), dkv)
+    qkv_grad, gain1 = qkv_grads(
+        h_parts, dq_near, dq_far, dkv, w_all_t, norm1_gain)
+    qkv_side = y_swap(pick(qkv_grad, 1 - iy))
+    dh1_far = input_grads(after(dq_far, qkv_grad), dkv, w_all_t, rows, 1)
+    qkv_side = after(qkv_side, dh1_far[0])
+    dh1_side = fold(dh1_far, BF16)
+    dh1_near = input_grads(
+        dq_near, after(dkv, dh1_side, qkv_side), w_all_t, rows, 0
+    )
+    dh1 = fold(dh1_near, F32) + after(tp_swap(dh1_side, bits - 1), dh1_near[0]).astype(F32)
+    output = after(x1, dh1_side) + near[0].astype(F32) + mixed_core.astype(F32) + mixed_side.astype(F32)
     n1 = x * r1
     scaled = dh1 * norm1_gain
     grad_input = dx1 + r1 * (scaled - n1 * jnp.mean(scaled * n1, axis=-1, keepdims=True))
 
-    grad_outproj = lax.psum_scatter(
-        out_part, ("z", "y"), scatter_dimension=0, tiled=True
-    ).astype(F32).T
-    qkv_grad, gain1 = qkv_grads(
-        [after(h_parts[0], dh1_side), *h_parts[1:]], dq_near, dq_far, dkv, w_all_t, norm1_gain
-    )
-    each = width // (2 * nz)
-    qkv_grad = qkv_grad.reshape(nz, 2, each, qkv_grad.shape[1])
-    pick = lambda at: lax.dynamic_index_in_dim(qkv_grad, at, 1, keepdims=False)
-    summed = pick(iy).astype(F32) + y_swap(pick(1 - iy)).astype(F32)
-    grad_qkv = lax.psum_scatter(
+    summed = jnp.concatenate(
+        [
+            after(pick(qkv_grad, iy), dh1_side).astype(F32) + qkv_side.astype(F32),
+            pick(out_part, iy).astype(F32) + out_side.astype(F32),
+        ],
+        axis=2,
+    )
+    summed = lax.psum_scatter(
         summed.astype(BF16).reshape(nz * each, -1), "z", scatter_dimension=0, tiled=True
     ).astype(F32)
-    small = own_columns(sum_all(jnp.concatenate([router_part, gain2, gain1], axis=0)))
-
+    grad_qkv, grad_outproj = summed[:, : q_cols + 2 * kv_cols], summed[:, q_cols + 2 * kv_cols :].T
+    small = jnp.concatenate([router_part, gain2, gain1], axis=0)
+    small = own_columns(sum_all(after(small, dh1_side)))
     if nz == 4:
-        outer, inner = grads_outer[0], grads_inner[0]
-        add = lambda a, b: (a.astype(F32) + b.astype(F32)).astype(BF16)
-        o1 = shift(outer, [(3, 2)])
-        i1 = shift(after(inner, o1), [(3, 2)])
-        o2 = shift(add(outer, o1), [(2, 1)])
-        i2 = shift(add(inner, i1), [(2, 1)])
-        o3 = shift(add(outer, o2), [(1, 0)])
-        i0 = shift(after(inner, i1), [(0, 1)])
-        whole = jnp.where(
-            along == 0,
-            outer.astype(F32) + o3.astype(F32),
-            inner.astype(F32) + i2.astype(F32) + i0.astype(F32),
-        ).astype(BF16)
-        side = width // 2
-        pairs = [(z, c) for z in range(4) for c in (z // 2,)]
-        other = lax.dynamic_slice_in_dim(whole, (1 - ix) * side, side, 0)
-        other = lax.ppermute(
-            other,
-            ("z", "x", "c"),
-            [((z * 2 + i) * 2 + c, (z * 2 + 1 - i) * 2 + c) for z, c in pairs for i in range(2)],
-        )
-        kept = lax.dynamic_slice_in_dim(whole, ix * side, side, 0)
-        kept = kept.astype(F32) + other.astype(F32)
-        own = lax.dynamic_slice_in_dim(kept, ic * (side // 2), side // 2, 0)
-        give = lax.dynamic_slice_in_dim(kept, (1 - ic) * (side // 2), side // 2, 0).astype(BF16)
-        part = jnp.where(ic == iz // 2, own, tp_swap(give, 0).astype(F32))
+        outer = x_reduce(outer, dkv)
+        inner = x_reduce(after(inner, dh1_side), dh1_near[0])
+        outer = after(outer, dh1_side)
+        home = lambda c, inside: (3 - inside if c else inside)
+        moves = [
+            [
+                ((z * 2 + x_) * 2 + c, home(c, int(x_ == first_)) * 4 + z)
+                for z in range(4)
+                for x_ in range(2)
+                for c in range(2)
+            ]
+            for first_ in range(2)
+        ]
+        zxc = ("z", "x", "c")
+        one = lax.ppermute(jnp.where(ix == 0, inner, outer), zxc, moves[0])
+        two = lax.ppermute(jnp.where(ix == 0, outer, inner), zxc, moves[1])
+        inside = (iz == 1) | (iz == 2)
+        part = jnp.concatenate(
+            [jnp.where(inside, one, two), jnp.where(inside, two, one)], axis=0
+        ).astype(F32)
     else:
         stacked = jnp.concatenate([grads_outer, grads_inner], axis=0)
         every = jnp.zeros((nz, width, 3 * hidden), BF16)

time: 665 us -> 607 us (0.913)
  waiting for transfers between devices: 161 us -> 112 us
  other arithmetic: 91.6 us -> 64.5 us
  Pallas kernels: 264 us -> 271 us
  local copies, waits for them, and re-layouts: 22.5 us -> 29.3 us
    convert_element_type x8 -> x7, other arithmetic: 42 us -> 11 us  [the longest x2 4.95 us: fold(): parts[i ^ 1 << bit] = total.astype(BF16 if bit < bits - 2 else kind)]
    ppermute x6 -> x7, waiting for transfers between devices: 57.2 us -> 26.2 us  [y_swap(): return lax.ppermute(value, 'y', [(0, 1), (1, 0)])]
    ppermute x10 -> x4, waiting for transfers between devices: 28.4 us -> 0.79 us  [shift(): return lax.ppermute(value, ('z', 'c'), perm)]
    ppermute x10 -> x4, starting transfers between devices: 34.1 us -> 12.9 us  [shift(): return lax.ppermute(value, ('z', 'c'), perm)]
    ppermute x1 -> x2, waiting for transfers between devices: 2.05 us -> 19.9 us  [the longest x1 11.3 us: body(): one = lax.ppermute(jnp.where(ix == 0, inner, outer), zxc, moves[0])]
    reduce_scatter x1, waiting for transfers between devices: 13.7 us -> 0.01 us  [body(): lax.psum_scatter(summed.astype(BF16).reshape(nz * each, -1), 'z', scatter...]
    ppermute x18 -> x17, starting transfers between devices: 10 us -> 23.4 us  [tp_swap(): return lax.ppermute(value, 'c', [(0, 1), (1, 0)])]
    ppermute x5 -> x7, waiting for transfers between devices: 47.2 us -> 55.3 us  [tp_swap(): return lax.ppermute(value, 'x', [(i, i ^ 1 << bit - 1) for i in range(nx)])]
  transfers between devices with their start and end apart: 44 -> 42, of which waited for: 14 -> 15; matrix products, arithmetic and copies ran while one was open for 16% -> 14% of each run, Pallas kernels for 40% -> 35%
where the time goes in v3:
time: 607 us; the launch traced here: 597 us
  Pallas kernels  271 us (45%)
  waiting for transfers between devices  112 us (18%)
  starting transfers between devices  100 us (16%)
  other arithmetic  64.5 us (11%)
  local copies, waits for them, and re-layouts  29.3 us (5%)
  between operations  14.8 us (2%)
    pallas_call x4, Pallas kernels, run_experts(): pl.pallas_call(functools.partial(expert_kernel, experts, bool(old), len(c...  84.8 us
    pallas_call x2, Pallas kernels, attend_back(): pl.pallas_call(functools.partial(attend_back_kernel, rows, zone, heads, g...  58.3 us
    ppermute x7, waiting for transfers between devices, tp_swap(): return lax.ppermute(value, 'x', [(i, i ^ 1 << bit - 1) for i in range(nx)])  55.3 us
    pallas_call x3, Pallas kernels, attend(): pl.pallas_call(functools.partial(attend_kernel, rows, zone, heads, groups...  48.1 us
    ppermute x7, starting transfers between devices, tp_swap(): return lax.ppermute(value, 'x', [(i, i ^ 1 << bit - 1) for i in range(nx)])  36.3 us
    pallas_call x2, Pallas kernels, expert_grads(): pl.pallas_call(expert_grad_kernel, grid=(mine,), in_specs=[anywhere] * 12...  35.9 us
    ppermute x7, waiting for transfers between devices, y_swap(): return lax.ppermute(value, 'y', [(0, 1), (1, 0)])  26.2 us
    ppermute x17, starting transfers between devices, tp_swap(): return lax.ppermute(value, 'c', [(0, 1), (1, 0)])  23.4 us
  transfers between devices with their start and end apart: 42, of which 15 were waited for; matrix products, arithmetic and copies ran while one was open for 14% of the time, Pallas kernels for 35%

profile of v3, /device:TPU:2, one launch (start us, length us, event | category | flops | bytes accessed | tf_op | source)
XLA Modules:
  0.0 597.2 jit_solution(17012963064644341376)
XLA Ops:
  13.2 3.7 pad_maximum_fusion
  16.9 5.8 collective-permute-start.1
  29.5 6.2 %qkv.2 = (bf16[384,1024]{1,0:T(8,128)(2,1)}, bf16[2,2048,64]{2,1,0:T(8,128)(2,1)}, bf16[128,2048]{1,0:T(8,128)(2,1)}, bf16[2,2048,64]{2,1,0:T(8,128)(2,1)}, bf16[128,2048]{1,0:T(8,128)(2,1)}) custom-call(bf16[512,1536]{1,0:T(8,128)(2,1)} %multiply_convert_fusion.1.refs_0_, bf16[512,1536]{1,0:T(8,128)(2,1)} %collective-permute-done.refs_1_, ...), custom_call_target="tpu_custom_call" | custom-call | flops 500000000 | bytes 1500000 | tf_op jit(solution)/shard_map/qkv/pallas_call | solution.py:90
  35.7 21.3 %collective-permute-done.2.refs_0_.refs_2_ = bf16[512,1536]{1,0:T(8,128)(2,1)} collective-permute-done((bf16[512,1536]{1,0:T(8,128)(2,1)}, bf16[512,1536]{1,0:T(8,128)(2,1)}, u32[]{:S(2)}, u32[]{:S(2)}) %collective-permute-start.2) | collective-permute-done | bytes 1572896 | tf_op jit(solution)/shard_map/ppermute | solution.py:755
  61.9 6.2 %qkv.3 = (bf16[384,1024]{1,0:T(8,128)(2,1)}, bf16[2,2048,64]{2,1,0:T(8,128)(2,1)}, bf16[128,2048]{1,0:T(8,128)(2,1)}, bf16[2,2048,64]{2,1,0:T(8,128)(2,1)}, bf16[128,2048]{1,0:T(8,128)(2,1)}) custom-call(bf16[512,1536]{1,0:T(8,128)(2,1)} %collective-permute-done.2.refs_0_.refs_2_, ...), custom_call_target="tpu_custom_call", output_to_operand_aliasing={{1}: (5, {}), {2}: (6, {}), {3}: (7, {}), {4}: (8, {})} | custom-call | flops 500000000 | bytes 1500000 | tf_op jit(solution)/shard_map/qkv/pallas_call | solution.py:90
  68.1 11.3 %attend.3 = (bf16[384,512]{1,0:T(8,128)(2,1)}, f32[6,512]{1,0:T(8,128)}, bf16[512,1536]{1,0:T(8,128)(2,1)}) custom-call(s32[9]{0:T(128)} %pad_add_fusion.s_ref.refs_0_, bf16[384,1024]{1,0:T(8,128)(2,1)} %get-tuple-element.168.q_ref.refs_1_, bf16[2,2048,64]{2,1,0:T(8,128)(2,1)} %get-tuple-element.111.k_ref.refs_4_, ...), custom_call_target="tpu_custom_call" | custom-call | flops 3000000000 | bytes 9000000 | tf_op jit(solution)/shard_map/attend/pallas_call | solution.py:186
  79.4 2.9 collective-permute-start.4
  85.5 8.4 %attend.4 = (bf16[384,512]{1,0:T(8,128)(2,1)}, f32[6,512]{1,0:T(8,128)}, bf16[512,1536]{1,0:T(8,128)(2,1)}) custom-call(s32[9]{0:T(128)} %pad_add_fusion.s_ref.refs_0_, bf16[384,1024]{1,0:T(8,128)(2,1)} %get-tuple-element.168.q_ref.refs_1_, bf16[2,2048,64]{2,1,0:T(8,128)(2,1)} %get-tuple-element.111.k_ref.refs_4_, ...), custom_call_target="tpu_custom_call" | custom-call | flops 3000000000 | bytes 9000000 | tf_op jit(solution)/shard_map/attend/pallas_call | solution.py:186
  93.9 3.4 add_convert_fusion.3
  97.3 12.7 %collective-permute-start.9 = (bf16[512,1536]{1,0:T(8,128)(2,1)}, bf16[512,1536]{1,0:T(8,128)(2,1)}, u32[]{:S(2)}, u32[]{:S(2)}) collective-permute-start(bf16[512,1536]{1,0:T(8,128)(2,1)} %add_convert_fusion.3), channel_id=1, source_target_pairs={{0,2},{2,0},{1,3},{3,1},{4,6},{6,4},{5,7},{7,5},{8,10},{10,8},{9,1... | collective-permute-start | bytes 4718600 | tf_op jit(solution)/shard_map/ppermute | solution.py:755
  110.0 28.4 %attend.5 = (bf16[384,1024]{1,0:T(8,128)(2,1)}, f32[6,1024]{1,0:T(8,128)}, bf16[512,1536]{1,0:T(8,128)(2,1)}, bf16[512,1536]{1,0:T(8,128)(2,1)}) custom-call(s32[9]{0:T(128)} %pad_add_fusion.s_ref.refs_0_, bf16[384,1024]{1,0:T(8,128)(2,1)} %get-tuple-element.119.q_ref.refs_1_, bf16[2,2048,64]{2,1,0:T(8,128)(2,1)} %get-tuple-element.111.k_ref.refs_4_, ...), custom_call_target="tpu_custom_call" | custom-call | flops 6000000000 | bytes 18000000 | tf_op jit(solution)/shard_map/attend/pallas_call | solution.py:186
  138.4 3.1 collective-permute-start.8
  149.3 3.0 collective-permute-start.15
  153.8 15.9 %collective-permute-start.11 = (bf16[512,1536]{1,0:T(8,128)(2,1)}, bf16[512,1536]{1,0:T(8,128)(2,1)}, u32[]{:S(2)}, u32[]{:S(2)}) collective-permute-start(bf16[512,1536]{1,0:T(8,128)(2,1)} %multiply_convert_fusion.refs_1_.refs_0_), channel_id=1, source_target_pairs={{0,1},{1,0},{2,3},{3,2},{4,5},{5,4},{6,7},{7,6},{8,9},{9,8},{10,11... | collective-permute-start | bytes 4718600 | tf_op jit(solution)/shard_map/ppermute | solution.py:754
  174.9 20.0 %experts.4 = (bf16[512,1536]{1,0:T(8,128)(2,1)}, bf16[512,1536]{1,0:T(8,128)(2,1)}, bf16[512,1664]{1,0:T(8,128)(2,1)}, bf16[512,1664]{1,0:T(8,128)(2,1)}, bf16[1...) custom-call(s32[2]{0:T(128)} %pad_add_fusion.2.refs_0_, bf16[512,1536]{1,0:T(8,128)(2,1)} %multiply_convert_fusion.refs_1_.refs_0_, ...), custom_call_target="tpu_custom_call" | custom-call | flops 8000000000 | bytes 24000000 | tf_op jit(solution)/shard_map/experts/pallas_call | solution.py:600
  194.9 11.4 %collective-permute-done.10.refs_1_.refs_2_ = bf16[512,1536]{1,0:T(8,128)(2,1)} collective-permute-done((bf16[512,1536]{1,0:T(8,128)(2,1)}, bf16[512,1536]{1,0:T(8,128)(2,1)}, u32[]{:S(2)}, u32[]{:S(2)}) %collective-permute-start.10) | collective-permute-done | bytes 1572896 | tf_op jit(solution)/shard_map/ppermute | solution.py:758
  210.1 20.1 %experts.5 = (bf16[512,1536]{1,0:T(8,128)(2,1)}, bf16[512,1536]{1,0:T(8,128)(2,1)}, bf16[512,1664]{1,0:T(8,128)(2,1)}, bf16[512,1664]{1,0:T(8,128)(2,1)}, bf16[1...) custom-call(s32[2]{0:T(128)} %pad_add_fusion.2.refs_0_, ...), custom_call_target="tpu_custom_call" | custom-call | flops 8000000000 | bytes 24000000 | tf_op jit(solution)/shard_map/experts/pallas_call | solution.py:600
  230.2 22.4 %experts.6 = (bf16[512,1536]{1,0:T(8,128)(2,1)}, bf16[512,1536]{1,0:T(8,128)(2,1)}, bf16[512,1664]{1,0:T(8,128)(2,1)}, bf16[512,1664]{1,0:T(8,128)(2,1)}, bf16[1...) custom-call(s32[2]{0:T(128)} %pad_add_fusion.1.refs_0_, bf16[512,1536]{1,0:T(8,128)(2,1)} %multiply_convert_fusion.refs_1_.refs_0_, ...), custom_call_target="tpu_custom_call" | custom-call | flops 8000000000 | bytes 24000000 | tf_op jit(solution)/shard_map/experts/pallas_call | solution.py:600
  252.6 22.4 %experts.7 = (bf16[512,1536]{1,0:T(8,128)(2,1)}, bf16[512,1536]{1,0:T(8,128)(2,1)}, bf16[512,1664]{1,0:T(8,128)(2,1)}, bf16[512,1664]{1,0:T(8,128)(2,1)}, bf16[1...) custom-call(s32[2]{0:T(128)} %pad_add_fusion.1.refs_0_, ...), custom_call_target="tpu_custom_call" | custom-call | flops 8000000000 | bytes 24000000 | tf_op jit(solution)/shard_map/experts/pallas_call | solution.py:600
  275.2 3.6 collective-permute-done.17
  278.8 3.1 add_convert_fusion
  282.0 17.7 %expert_grads.2 = bf16[1,1536,1536]{2,1,0:T(8,128)(2,1)} custom-call(bf16[512,1536]{1,0:T(8,128)(2,1)} %multiply_convert_fusion.refs_1_.refs_0_, bf16[512,1536]{1,0:T(8,128)(2,1)} %collective-permute-done.11.refs_2_.refs_1_, bf16[512,1536]{1,0:T(8,128)(2,1)} %collective-permute-done.10.refs_1_.refs_2_, ...), custom_call_target="tpu_custom_call" | custom-call | flops 8000000000 | bytes 24000000 | tf_op jit(solution)/shard_map/expert_grads/pallas_call | solution.py:704
  304.3 4.0 convert_add_fusion.1
  308.3 18.2 %expert_grads.3 = bf16[1,1536,1536]{2,1,0:T(8,128)(2,1)} custom-call(bf16[512,1536]{1,0:T(8,128)(2,1)} %multiply_convert_fusion.refs_1_.refs_0_, bf16[512,1536]{1,0:T(8,128)(2,1)} %collective-permute-done.11.refs_2_.refs_1_, bf16[512,1536]{1,0:T(8,128)(2,1)} %collective-permute-done.10.refs_1_.refs_2_, ...), custom_call_target="tpu_custom_call" | custom-call | flops 8000000000 | bytes 24000000 | tf_op jit(solution)/shard_map/expert_grads/pallas_call | solution.py:704
  326.5 3.6 add_convert_fusion.2
  330.1 12.3 %collective-permute-done.20 = bf16[512,1664]{1,0:T(8,128)(2,1)} collective-permute-done((bf16[512,1664]{1,0:T(8,128)(2,1)}, bf16[512,1664]{1,0:T(8,128)(2,1)}, u32[]{:S(2)}, u32[]{:S(2)}) %collective-permute-start.20) | collective-permute-done | bytes 1703968 | tf_op jit(solution)/shard_map/ppermute | solution.py:758
  346.3 3.3 fusion.9
  353.3 36.3 %attend_back.2 = (bf16[384,1024]{1,0:T(8,128)(2,1)}, f32[2,2048,64]{2,1,0:T(8,128)}, f32[2,2048,64]{2,1,0:T(8,128)}) custom-call(s32[9]{0:T(128)} %pad_add_fusion.s_ref.refs_0_, bf16[384,1024]{1,0:T(8,128)(2,1)} %get-tuple-element.119.q_ref.refs_1_, bf16[384,1024]{1,0:T(8,128)(2,1)} %get-tuple-element.158.refs_2_, f32[6,1024]{1,0:T(8,128)} %get-tuple-element.159.refs_3_, ...), custom_call_target="tpu_custom_call" | custom-call | flops 30000001024 | bytes 90000000 | tf_op jit(solution)/shard_map/attend_back/pallas_call | solution.py:329
  394.6 5.0 out_grads.2.refs_3_
  399.6 5.4 out_grads.3
  408.4 22.1 %attend_back.3 = (bf16[384,1024]{1,0:T(8,128)(2,1)}, bf16[256,2048]{1,0:T(8,128)(2,1)}) custom-call(s32[9]{0:T(128)} %pad_add_fusion.s_ref.refs_0_, bf16[384,1024]{1,0:T(8,128)(2,1)} %get-tuple-element.168.q_ref.refs_1_, bf16[384,1024]{1,0:T(8,128)(2,1)} %constant_dynamic-update-slice_fusion.refs_2_, f32[6,1024]{1,0:T(8,128)} %pad_maximum_fusion.4.refs_3_, ...), custom_call_target="tpu_custom_call" | custom-call | flops 30000001024 | bytes 90000000 | tf_op jit(solution)/shard_map/attend_back/pallas_call | solution.py:329
  430.5 9.9 %qkv_grads.1 = (bf16[1536,640]{1,0:T(8,128)(2,1)}, f32[1,1536]{1,0:T(1,128)}) custom-call(bf16[512,1536]{1,0:T(8,128)(2,1)} %multiply_convert_fusion.1.refs_0_, bf16[512,1536]{1,0:T(8,128)(2,1)} %collective-permute-done.refs_1_, bf16[512,1536]{1,0:T(8,128)(2,1)} %collective-permute-done.2.refs_0_.refs_2_, bf16[512,1536]{1,0:T(8,128)(2,1)} %copy-done.11, ...), custom_call_target="tpu_custom_call" | custom-call | flops 10000000000 | bytes 30000000 | tf_op jit(solution)/shard_map/qkv_grads/pallas_call | solution.py:396
  440.4 5.8 input_grads.2
  446.1 2.8 dynamic-slice_bitcast_fusion
  449.5 13.7 %collective-permute-start.36 = (bf16[192,1536]{1,0:T(8,128)(2,1)S(1)}, bf16[192,1536]{1,0:T(8,128)(2,1)S(1)}, u32[]{:S(2)}, u32[]{:S(2)}) collective-permute-start(bf16[192,1536]{1,0:T(8,128)(2,1)S(1)} %constant_dynamic-slice_fusion), channel_id=1, source_target_pairs={{0,2},{2,0},{1,3},{3,1},{4,6},{6,4},{5,7},{7,5},{8,10},{10,8},{9,1... | collective-permute-start | bytes 1769480 | tf_op jit(solution)/shard_map/ppermute | solution.py:755
  467.2 9.4 %collective-permute-done.36 = bf16[192,1536]{1,0:T(8,128)(2,1)S(1)} collective-permute-done((bf16[192,1536]{1,0:T(8,128)(2,1)S(1)}, bf16[192,1536]{1,0:T(8,128)(2,1)S(1)}, u32[]{:S(2)}, u32[]{:S(2)}) %collective-permute-start.36) | collective-permute-done | bytes 589856 | tf_op jit(solution)/shard_map/ppermute | solution.py:755
  480.0 8.9 %collective-permute-start.28 = (bf16[512,1536]{1,0:T(8,128)(2,1)}, bf16[512,1536]{1,0:T(8,128)(2,1)}, u32[]{:S(2)}, u32[]{:S(2)}) collective-permute-start(bf16[512,1536]{1,0:T(8,128)(2,1)} %add_convert_fusion.1), channel_id=1, source_target_pairs={{0,2},{2,0},{1,3},{3,1},{4,6},{6,4},{5,7},{7,5},{8,10},{10,8},{9,1... | collective-permute-start | bytes 4718600 | tf_op jit(solution)/shard_map/ppermute | solution.py:755
  488.9 4.0 collective-permute-start.29
  495.5 5.0 collective-permute-start.30
  500.5 5.8 input_grads.3
  513.2 23.6 %collective-permute-done.35 = bf16[192,1536]{1,0:T(8,128)(2,1)} collective-permute-done((bf16[192,1536]{1,0:T(8,128)(2,1)}, bf16[192,1536]{1,0:T(8,128)(2,1)}, u32[]{:S(2)}, u32[]{:S(2)}) %collective-permute-start.35) | collective-permute-done | bytes 589856 | tf_op jit(solution)/shard_map/ppermute | solution.py:755
  538.4 3.7 collective-permute-start.37
  542.1 5.9 collective-permute-start.38
  548.0 4.4 convert_add_fusion.2
  553.6 11.3 %collective-permute-done.37 = bf16[192,1536]{1,0:T(8,128)(2,1)S(1)} collective-permute-done((bf16[192,1536]{1,0:T(8,128)(2,1)S(1)}, bf16[192,1536]{1,0:T(8,128)(2,1)S(1)}, u32[]{:S(2)}, u32[]{:S(2)}) %collective-permute-start.37) | collective-permute-done | bytes 589856 | tf_op jit(solution)/shard_map/ppermute | solution.py:1008
  564.9 8.6 %collective-permute-done.38 = bf16[192,1536]{1,0:T(8,128)(2,1)S(1)} collective-permute-done((bf16[192,1536]{1,0:T(8,128)(2,1)S(1)}, bf16[192,1536]{1,0:T(8,128)(2,1)S(1)}, u32[]{:S(2)}, u32[]{:S(2)}) %collective-permute-start.38) | collective-permute-done | bytes 589856 | tf_op jit(solution)/shard_map/ppermute | solution.py:1009
  578.0 3.1 multiply_reduce_fusion.1
  581.1 4.8 multiply_add_fusion
  (194 shorter events, 88.9 us)
Async XLA Ops:
  7.2 401.2 %reduce-scatter.4.cloned.1.call-start = ((), (), s32[]{:S(2)}) async-start(), calls=%async_computation.3 | async-start | bytes 5898240 | tf_op jit(solution)/shard_map/reduce_scatter | solution.py:921
  11.4 5.5 collective-permute-start
  16.9 62.5 %collective-permute-start.1 = (bf16[1,1536,1536]{2,1,0:T(8,128)(2,1)}, bf16[1,1536,1536]{2,1,0:T(8,128)(2,1)}, u32[]{:S(2)}, u32[]{:S(2)}) collective-permute-start(bf16[1,1536,1536]{2,1,0:T(8,128)(2,1)} %bitcast.4.refs_7_.refs_6_), channel_id=1, source_target_pairs={{0,8},{8,16},{25,17},{17,9},{2,10},{10,18},{27,19},{19,11},{4,12},... | collective-permute-start | bytes 14155784 | tf_op jit(solution)/shard_map/ppermute | solution.py:833
  22.7 34.3 %collective-permute-start.2 = (bf16[512,1536]{1,0:T(8,128)(2,1)}, bf16[512,1536]{1,0:T(8,128)(2,1)}, u32[]{:S(2)}, u32[]{:S(2)}) collective-permute-start(bf16[512,1536]{1,0:T(8,128)(2,1)} %multiply_convert_fusion.1.refs_0_), channel_id=1, source_target_pairs={{0,2},{2,0},{1,3},{3,1},{4,6},{6,4},{5,7},{7,5},{8,10},{10,8},{9,1... | collective-permute-start | bytes 4718600 | tf_op jit(solution)/shard_map/ppermute | solution.py:755
  29.5 27.5 %copy-start.28 = (s32[1,4]{1,0:T(1,128)S(1)}, s32[1,4]{1,0:T(1,128)}, u32[]{:S(2)}) copy-start(s32[1,4]{1,0:T(1,128)} %param.28) | copy-start | bytes 52
  29.5 27.5 %copy-start.29 = (s32[1,4]{1,0:T(1,128)S(1)}, s32[1,4]{1,0:T(1,128)}, u32[]{:S(2)}) copy-start(s32[1,4]{1,0:T(1,128)} %param.27) | copy-start | bytes 52
  57.0 3.6 collective-permute-start.3
  57.7 88.8 %collective-permute-start.6 = (bf16[1,1536,1536]{2,1,0:T(8,128)(2,1)}, bf16[1,1536,1536]{2,1,0:T(8,128)(2,1)}, u32[]{:S(2)}, u32[]{:S(2)}) collective-permute-start(bf16[1,1536,1536]{2,1,0:T(8,128)(2,1)} %bitcast.4.refs_7_.refs_6_), channel_id=1, source_target_pairs={{8,0},{17,25},{10,2},{19,27},{12,4},{21,29},{14,6},{23,31}} | collective-permute-start | bytes 14155784 | tf_op jit(solution)/shard_map/ppermute | solution.py:833
  79.4 67.1 %collective-permute-start.4 = (bf16[1,1536,1536]{2,1,0:T(8,128)(2,1)}, bf16[1,1536,1536]{2,1,0:T(8,128)(2,1)}, u32[]{:S(2)}, u32[]{:S(2)}) collective-permute-start(bf16[1,1536,1536]{2,1,0:T(8,128)(2,1)} %collective-permute-done.1.refs_8_.refs_7_), channel_id=1, source_target_pairs={{8,16},{16,24},{17,9},{9,1},{10,18},{18,26},{19,11},{11,3},{12,20}... | collective-permute-start | bytes 14155784 | tf_op jit(solution)/shard_map/ppermute | solution.py:833
  82.3 11.6 %collective-permute-start.7 = (bf16[512,1536]{1,0:T(8,128)(2,1)}, bf16[512,1536]{1,0:T(8,128)(2,1)}, u32[]{:S(2)}, u32[]{:S(2)}) collective-permute-start(bf16[512,1536]{1,0:T(8,128)(2,1)} %get-tuple-element.113), channel_id=1, source_target_pairs={{0,1},{1,0},{2,3},{3,2},{4,5},{5,4},{6,7},{7,6},{8,9},{9,8},{10,11... | collective-permute-start | bytes 4718600 | tf_op jit(solution)/shard_map/ppermute | solution.py:754
  84.0 61.7 %collective-permute-start.5 = (bf16[512,1664]{1,0:T(8,128)(2,1)}, bf16[512,1664]{1,0:T(8,128)(2,1)S(1)}, u32[]{:S(2)}, u32[]{:S(2)}) collective-permute-start(bf16[512,1664]{1,0:T(8,128)(2,1)} %pad_maximum_fusion.1.refs_3_.refs_4_), channel_id=1, source_target_pairs={{0,4},{4,0},{1,5},{5,1},{2,6},{6,2},{3,7},{7,3},{8,12},{12,8},{9,1... | collective-permute-start | bytes 5111816 | tf_op jit(solution)/shard_map/ppermute | solution.py:758
  97.3 45.7 %collective-permute-start.9 = (bf16[512,1536]{1,0:T(8,128)(2,1)}, bf16[512,1536]{1,0:T(8,128)(2,1)}, u32[]{:S(2)}, u32[]{:S(2)}) collective-permute-start(bf16[512,1536]{1,0:T(8,128)(2,1)} %add_convert_fusion.3), channel_id=1, source_target_pairs={{0,2},{2,0},{1,3},{3,1},{4,6},{6,4},{5,7},{7,5},{8,10},{10,8},{9,1... | collective-permute-start | bytes 4718600 | tf_op jit(solution)/shard_map/ppermute | solution.py:755
  138.4 8.6 %collective-permute-start.8 = (bf16[512,1536]{1,0:T(8,128)(2,1)}, bf16[512,1536]{1,0:T(8,128)(2,1)S(1)}, u32[]{:S(2)}, u32[]{:S(2)}) collective-permute-start(bf16[512,1536]{1,0:T(8,128)(2,1)} %get-tuple-element.121), channel_id=1, source_target_pairs={{0,1},{1,0},{2,3},{3,2},{4,5},{5,4},{6,7},{7,6},{8,9},{9,8},{10,11... | collective-permute-start | bytes 4718600 | tf_op jit(solution)/shard_map/ppermute | solution.py:754
  142.9 31.9 %collective-permute-start.12 = (bf16[512,1664]{1,0:T(8,128)(2,1)}, bf16[512,1664]{1,0:T(8,128)(2,1)}, u32[]{:S(2)}, u32[]{:S(2)}) collective-permute-start(bf16[512,1664]{1,0:T(8,128)(2,1)} %pad_maximum_fusion.1.refs_3_.refs_4_), channel_id=1, source_target_pairs={{0,1},{1,0},{2,3},{3,2},{4,5},{5,4},{6,7},{7,6},{8,9},{9,8},{10,11... | collective-permute-start | bytes 5111816 | tf_op jit(solution)/shard_map/ppermute | solution.py:754
  149.3 80.9 %collective-permute-start.15 = (bf16[1,1536,1536]{2,1,0:T(8,128)(2,1)}, bf16[1,1536,1536]{2,1,0:T(8,128)(2,1)}, u32[]{:S(2)}, u32[]{:S(2)}) collective-permute-start(bf16[1,1536,1536]{2,1,0:T(8,128)(2,1)} %collective-permute-done.4.refs_9_.refs_8_), channel_id=1, source_target_pairs={{16,24},{9,1},{18,26},{11,3},{20,28},{13,5},{22,30},{15,7}} | collective-permute-start | bytes 14155784 | tf_op jit(solution)/shard_map/ppermute | solution.py:833
  153.8 21.1 %collective-permute-start.11 = (bf16[512,1536]{1,0:T(8,128)(2,1)}, bf16[512,1536]{1,0:T(8,128)(2,1)}, u32[]{:S(2)}, u32[]{:S(2)}) collective-permute-start(bf16[512,1536]{1,0:T(8,128)(2,1)} %multiply_convert_fusion.refs_1_.refs_0_), channel_id=1, source_target_pairs={{0,1},{1,0},{2,3},{3,2},{4,5},{5,4},{6,7},{7,6},{8,9},{9,8},{10,11... | collective-permute-start | bytes 4718600 | tf_op jit(solution)/shard_map/ppermute | solution.py:754
  169.7 36.6 %collective-permute-start.10 = (bf16[512,1536]{1,0:T(8,128)(2,1)}, bf16[512,1536]{1,0:T(8,128)(2,1)}, u32[]{:S(2)}, u32[]{:S(2)}) collective-permute-start(bf16[512,1536]{1,0:T(8,128)(2,1)} %multiply_convert_fusion.refs_1_.refs_0_), channel_id=1, source_target_pairs={{0,4},{4,0},{1,5},{5,1},{2,6},{6,2},{3,7},{7,3},{8,12},{12,8},{9,1... | collective-permute-start | bytes 4718600 | tf_op jit(solution)/shard_map/ppermute | solution.py:758
  174.9 32.7 %collective-permute-start.14 = (bf16[512,1664]{1,0:T(8,128)(2,1)}, bf16[512,1664]{1,0:T(8,128)(2,1)}, u32[]{:S(2)}, u32[]{:S(2)}) collective-permute-start(bf16[512,1664]{1,0:T(8,128)(2,1)} %copy-done.9), channel_id=1, source_target_pairs={{0,1},{1,0},{2,3},{3,2},{4,5},{5,4},{6,7},{7,6},{8,9},{9,8},{10,11... | collective-permute-start | bytes 5111816 | tf_op jit(solution)/shard_map/ppermute | solution.py:754
  206.4 3.8 collective-permute-start.13
  274.9 3.9 collective-permute-start.17
  299.7 189.2 %reduce-scatter.8.cloned.1.call-start = ((), (), s32[]{:S(2)}) async-start(), calls=%async_computation.5 | async-start | bytes 5898240 | tf_op jit(solution)/shard_map/reduce_scatter | solution.py:921
  299.8 4.6 collective-permute-start.16
  300.0 26.5 %collective-permute-start.18 = (bf16[512,1536]{1,0:T(8,128)(2,1)}, bf16[512,1536]{1,0:T(8,128)(2,1)}, u32[]{:S(2)}, u32[]{:S(2)}) collective-permute-start(bf16[512,1536]{1,0:T(8,128)(2,1)} %get-tuple-element.153), channel_id=1, source_target_pairs={{0,1},{1,0},{2,3},{3,2},{4,5},{5,4},{6,7},{7,6},{8,9},{9,8},{10,11... | collective-permute-start | bytes 4718600 | tf_op jit(solution)/shard_map/ppermute | solution.py:754
  302.7 39.7 %collective-permute-start.20 = (bf16[512,1664]{1,0:T(8,128)(2,1)}, bf16[512,1664]{1,0:T(8,128)(2,1)}, u32[]{:S(2)}, u32[]{:S(2)}) collective-permute-start(bf16[512,1664]{1,0:T(8,128)(2,1)} %add_convert_fusion), channel_id=1, source_target_pairs={{0,4},{4,0},{1,5},{5,1},{2,6},{6,2},{3,7},{7,3},{8,12},{12,8},{9,1... | collective-permute-start | bytes 5111816 | tf_op jit(solution)/shard_map/ppermute | solution.py:758
  304.3 25.8 %collective-permute-start.19 = (bf16[512,1536]{1,0:T(8,128)(2,1)}, bf16[512,1536]{1,0:T(8,128)(2,1)}, u32[]{:S(2)}, u32[]{:S(2)}) collective-permute-start(bf16[512,1536]{1,0:T(8,128)(2,1)} %get-tuple-element.155), channel_id=1, source_target_pairs={{0,1},{1,0},{2,3},{3,2},{4,5},{5,4},{6,7},{7,6},{8,9},{9,8},{10,11... | collective-permute-start | bytes 4718600 | tf_op jit(solution)/shard_map/ppermute | solution.py:754
  349.6 3.8 collective-permute-start.22
  349.6 236.3 %reduce-scatter.6.cloned.1.call-start = ((), (), s32[]{:S(2)}) async-start(), calls=%async_computation.4 | async-start | bytes 1966080 | tf_op jit(solution)/shard_map/reduce_scatter | solution.py:987
  349.6 40.0 %collective-permute-start.21 = (bf16[512,1536]{1,0:T(8,128)(2,1)}, bf16[512,1536]{1,0:T(8,128)(2,1)}, u32[]{:S(2)}, u32[]{:S(2)}) collective-permute-start(bf16[512,1536]{1,0:T(8,128)(2,1)} %get-tuple-element.167.refs_10_.refs_0_), channel_id=1, source_target_pairs={{0,2},{2,0},{1,3},{3,1},{4,6},{6,4},{5,7},{7,5},{8,10},{10,8},{9,1... | collective-permute-start | bytes 4718600 | tf_op jit(solution)/shard_map/ppermute | solution.py:755
  350.0 44.5 %collective-permute-start.24 = (bf16[512,1536]{1,0:T(8,128)(2,1)}, bf16[512,1536]{1,0:T(8,128)(2,1)}, u32[]{:S(2)}, u32[]{:S(2)}) collective-permute-start(bf16[512,1536]{1,0:T(8,128)(2,1)} %add_convert_fusion.2), channel_id=1, source_target_pairs={{0,4},{4,0},{1,5},{5,1},{2,6},{6,2},{3,7},{7,3},{8,12},{12,8},{9,1... | collective-permute-start | bytes 4718600 | tf_op jit(solution)/shard_map/ppermute | solution.py:758
  353.3 36.5 %copy-start.20 = (f32[1536]{0:T(1024)S(1)}, f32[1536]{0:T(1024)}, u32[]{:S(2)}) copy-start(f32[1536]{0:T(1024)} %param.16) | copy-start | bytes 18436
  353.3 37.1 %copy-start.24 = (f32[6,512]{1,0:T(8,128)S(1)}, f32[6,512]{1,0:T(8,128)}, u32[]{:S(2)}) copy-start(f32[6,512]{1,0:T(8,128)} %get-tuple-element.170) | copy-start | bytes 36868
  353.3 37.1 %copy-start.25 = (f32[6,512]{1,0:T(8,128)S(1)}, f32[6,512]{1,0:T(8,128)}, u32[]{:S(2)}) copy-start(f32[6,512]{1,0:T(8,128)} %get-tuple-element.169) | copy-start | bytes 36868
  389.6 10.0 %collective-permute-start.23 = (bf16[512,1536]{1,0:T(8,128)(2,1)}, bf16[512,1536]{1,0:T(8,128)(2,1)}, u32[]{:S(2)}, u32[]{:S(2)}) collective-permute-start(bf16[512,1536]{1,0:T(8,128)(2,1)} %collective-permute-done.21.refs_0_.refs_10_), channel_id=1, source_target_pairs={{0,1},{1,0},{2,3},{3,2},{4,5},{5,4},{6,7},{7,6},{8,9},{9,8},{10,11... | collective-permute-start | bytes 4718600 | tf_op jit(solution)/shard_map/ppermute | solution.py:754
  406.9 58.1 %collective-permute-start.34 = (bf16[4,192,384]{2,1,0:T(8,128)(2,1)}, bf16[4,192,384]{2,1,0:T(8,128)(2,1)}, u32[]{:S(2)}, u32[]{:S(2)}) collective-permute-start(bf16[4,192,384]{2,1,0:T(8,128)(2,1)} %dynamic-slice_bitcast_fusion.2), channel_id=1, source_target_pairs={{0,4},{4,0},{1,5},{5,1},{2,6},{6,2},{3,7},{7,3},{8,12},{12,8},{9,1... | collective-permute-start | bytes 1769480 | tf_op jit(solution)/shard_map/ppermute | solution.py:758
  446.1 32.4 %collective-permute-start.25 = (bf16[512,1536]{1,0:T(8,128)(2,1)}, bf16[512,1536]{1,0:T(8,128)(2,1)S(1)}, u32[]{:S(2)}, u32[]{:S(2)}) collective-permute-start(bf16[512,1536]{1,0:T(8,128)(2,1)} %get-tuple-element.178), channel_id=1, source_target_pairs={{0,1},{1,0},{2,3},{3,2},{4,5},{5,4},{6,7},{7,6},{8,9},{9,8},{10,11... | collective-permute-start | bytes 4718600 | tf_op jit(solution)/shard_map/ppermute | solution.py:754
  448.9 28.6 %collective-permute-start.26 = (bf16[4,192,640]{2,1,0:T(8,128)(2,1)S(1)}, bf16[4,192,640]{2,1,0:T(8,128)(2,1)S(1)}, u32[]{:S(2)}, u32[]{:S(2)}) collective-permute-start(bf16[4,192,640]{2,1,0:T(8,128)(2,1)S(1)} %get-tuple-element.230), channel_id=1, source_target_pairs={{0,4},{4,0},{1,5},{5,1},{2,6},{6,2},{3,7},{7,3},{8,12},{12,8},{9,1... | collective-permute-start | bytes 2949128 | tf_op jit(solution)/shard_map/ppermute | solution.py:758
  449.5 27.0 %collective-permute-start.36 = (bf16[192,1536]{1,0:T(8,128)(2,1)S(1)}, bf16[192,1536]{1,0:T(8,128)(2,1)S(1)}, u32[]{:S(2)}, u32[]{:S(2)}) collective-permute-start(bf16[192,1536]{1,0:T(8,128)(2,1)S(1)} %constant_dynamic-slice_fusion), channel_id=1, source_target_pairs={{0,2},{2,0},{1,3},{3,1},{4,6},{6,4},{5,7},{7,5},{8,10},{10,8},{9,1... | collective-permute-start | bytes 1769480 | tf_op jit(solution)/shard_map/ppermute | solution.py:755
  480.0 97.9 %collective-permute-start.28 = (bf16[512,1536]{1,0:T(8,128)(2,1)}, bf16[512,1536]{1,0:T(8,128)(2,1)}, u32[]{:S(2)}, u32[]{:S(2)}) collective-permute-start(bf16[512,1536]{1,0:T(8,128)(2,1)} %add_convert_fusion.1), channel_id=1, source_target_pairs={{0,2},{2,0},{1,3},{3,1},{4,6},{6,4},{5,7},{7,5},{8,10},{10,8},{9,1... | collective-permute-start | bytes 4718600 | tf_op jit(solution)/shard_map/ppermute | solution.py:755
  488.9 6.6 %collective-permute-start.29 = (f32[10,1536]{1,0:T(8,128)S(1)}, f32[10,1536]{1,0:T(8,128)S(1)}, u32[]{:S(2)}, u32[]{:S(2)}) collective-permute-start(f32[10,1536]{1,0:T(8,128)S(1)} %pad_maximum_fusion.3), channel_id=1, source_target_pairs={{0,8},{8,0},{16,24},{24,16},{1,9},{9,1},{17,25},{25,17},{2,10},{10... | collective-permute-start | bytes 184328 | tf_op jit(solution)/shard_map/ppermute | solution.py:777
  494.8 41.9 %collective-permute-start.35 = (bf16[192,1536]{1,0:T(8,128)(2,1)}, bf16[192,1536]{1,0:T(8,128)(2,1)}, u32[]{:S(2)}, u32[]{:S(2)}) collective-permute-start(bf16[192,1536]{1,0:T(8,128)(2,1)} %constant_dynamic-slice_fusion.1), channel_id=1, source_target_pairs={{0,2},{2,0},{1,3},{3,1},{4,6},{6,4},{5,7},{7,5},{8,10},{10,8},{9,1... | collective-permute-start | bytes 1769480 | tf_op jit(solution)/shard_map/ppermute | solution.py:755
  495.5 10.8 %collective-permute-start.30 = (f32[10,1536]{1,0:T(8,128)S(1)}, f32[10,1536]{1,0:T(8,128)S(1)}, u32[]{:S(2)}, u32[]{:S(2)}) collective-permute-start(f32[10,1536]{1,0:T(8,128)S(1)} %add.188), channel_id=1, source_target_pairs={{0,16},{8,24},{16,0},{24,8},{1,17},{9,25},{17,1},{25,9},{2,18},{10... | collective-permute-start | bytes 184328 | tf_op jit(solution)/shard_map/ppermute | solution.py:777
  506.3 4.7 collective-permute-start.31
  511.0 2.1 collective-permute-start.32
  512.5 35.5 %copy-start.12 = (bf16[512,1536]{1,0:T(8,128)(2,1)S(1)}, bf16[512,1536]{1,0:T(8,128)(2,1)}, u32[]{:S(2)}) copy-start(bf16[512,1536]{1,0:T(8,128)(2,1)} %get-tuple-element.180) | copy-start | bytes 4718596
  512.5 65.4 %collective-permute-start.27 = (bf16[512,1536]{1,0:T(8,128)(2,1)}, bf16[512,1536]{1,0:T(8,128)(2,1)}, u32[]{:S(2)}, u32[]{:S(2)}) collective-permute-start(bf16[512,1536]{1,0:T(8,128)(2,1)} %get-tuple-element.184), channel_id=1, source_target_pairs={{0,1},{1,0},{2,3},{3,2},{4,5},{5,4},{6,7},{7,6},{8,9},{9,8},{10,11... | collective-permute-start | bytes 4718600 | tf_op jit(solution)/shard_map/ppermute | solution.py:754
  513.1 39.3 %collective-permute-start.33 = (f32[10,1536]{1,0:T(8,128)S(1)}, f32[10,1536]{1,0:T(8,128)S(1)}, u32[]{:S(2)}, u32[]{:S(2)}) collective-permute-start(f32[10,1536]{1,0:T(8,128)S(1)} %add.191), channel_id=1, source_target_pairs={{0,2},{2,0},{1,3},{3,1},{4,6},{6,4},{5,7},{7,5},{8,10},{10,8},{9,1... | collective-permute-start | bytes 184328 | tf_op jit(solution)/shard_map/ppermute | solution.py:755
  538.4 26.4 %collective-permute-start.37 = (bf16[192,1536]{1,0:T(8,128)(2,1)S(1)}, bf16[192,1536]{1,0:T(8,128)(2,1)S(1)}, u32[]{:S(2)}, u32[]{:S(2)}) collective-permute-start(bf16[192,1536]{1,0:T(8,128)(2,1)S(1)} %get-tuple-element.227), channel_id=1, source_target_pairs={{0,8},{1,16},{2,0},{3,24},{8,9},{9,17},{10,1},{11,25},{16,10},{17,... | collective-permute-start | bytes 1769480 | tf_op jit(solution)/shard_map/ppermute | solution.py:1008
  542.1 31.3 %collective-permute-start.38 = (bf16[192,1536]{1,0:T(8,128)(2,1)S(1)}, bf16[192,1536]{1,0:T(8,128)(2,1)S(1)}, u32[]{:S(2)}, u32[]{:S(2)}) collective-permute-start(bf16[192,1536]{1,0:T(8,128)(2,1)S(1)} %get-tuple-element.228), channel_id=1, source_target_pairs={{0,0},{1,24},{2,8},{3,16},{8,1},{9,25},{10,9},{11,17},{16,2},{17,2... | collective-permute-start | bytes 1769480 | tf_op jit(solution)/shard_map/ppermute | solution.py:1009
  (24 other events, 165.4 us)
Sparse Core Ops, SparseCore 0:
  299.8 89.8 reduce-scatter.3
  392.1 85.7 reduce-scatter.7
  512.6 32.6 reduce-scatter.5

commit v4 on v3

--- a/solution.py
+++ b/solution.py
@@ -101,7 +101,7 @@
         out_shape=[jax.ShapeDtypeStruct((q_cols, size), BF16)] + kv_shapes,
         input_output_aliases={parts + 3 + i: 1 + i for i in range(len(previous))},
         compiler_params=params(),
-        cost_estimate=cost(0.5),
+        cost_estimate=cost(6),
         name="qkv",
     )(*h_parts, w_all, cos, sin, *previous)
 
@@ -176,7 +176,7 @@
             out_ref[...] = dot(o_ref[...], w_ref[...], 0, 0).astype(BF16)
 
 
-def attend(scalars, q, at, count, k, vt, w_out, rows, zone, base):
+def attend(scalars, q, at, count, k, vt, w_out, rows, zone, base, micros):
     q_cols = q.shape[0]
     size = count * rows
     groups = k.shape[0]
@@ -211,7 +211,7 @@
         ]
         + [jax.ShapeDtypeStruct((rows, width), BF16)] * count,
         compiler_params=params(),
-        cost_estimate=cost(3 * count),
+        cost_estimate=cost(micros),
         name="attend",
     )(scalars, q, k, vt, w_out)
 
@@ -715,7 +715,7 @@
             pltpu.SemaphoreType.DMA((12,)),
         ],
         compiler_params=params(),
-        cost_estimate=cost(8),
+        cost_estimate=cost(1),
         name="expert_grads",
     )(*h_parts, *dy_parts, *acts, *dgus)
 
@@ -786,6 +786,12 @@
         index = (iz * 2 + iy) * blocks + me
         return lax.dynamic_slice_in_dim(value, index * each, each, 1)
 
+    each = width // (2 * nz)
+
+    def pick(grad, at):
+        grad = grad.reshape(nz, 2, each, grad.shape[1])
+        return lax.dynamic_index_in_dim(grad, at, 1, keepdims=False)
+
     x = tokens.astype(F32)
     r1 = lax.rsqrt(jnp.mean(x * x, axis=-1, keepdims=True) + EPSILON)
     h1 = (x * r1 * norm1_gain).astype(BF16)
@@ -840,20 +846,20 @@
 
     q_far, k, kt, v, vt = project_qkv(h_parts[half:], w_all_t, cos, sin, q_cols, kv_cols, 1, kv)
     quarter = half // 2
-    run = lambda q, at, count, base: attend(
-        scalars, q, at, count, k, vt, w_out, rows, zone, base
-    )
-    o_3, lse_3, *out_3 = run(q_far, quarter, quarter, half + quarter)
+    run = lambda q, at, count, base, micros: attend(
+        scalars, q, at, count, k, vt, w_out, rows, zone, base, micros
+    )
+    o_3, lse_3, *out_3 = run(q_far, quarter, quarter, half + quarter, 9)
     early = ()
     if nz == 4:
         early = (from_outer,)
         second = shift(after(from_outer, out_3[0]), [(1, 2), (2, 3)])
-    o_2, lse_2, *out_2 = run(after(q_far, out_3[0], *early), 0, quarter, half)
+    o_2, lse_2, *out_2 = run(after(q_far, out_3[0], *early), 0, quarter, half, 2)
     side = fold([*out_2, *out_3], BF16)
     if nz == 4:
-        o_near, lse_near, *out_near = run(after(q_near, side), 0, half, 0)
+        o_near, lse_near, *out_near = run(after(q_near, side), 0, half, 0, 2)
     else:
-        o_near, lse_near, *out_near = run(after(q_near, side), 0, half, 0)
+        o_near, lse_near, *out_near = run(after(q_near, side), 0, half, 0, 2)
     o_far = jnp.concatenate([o_2, o_3], axis=1)
     lse_far = jnp.concatenate([lse_2, lse_3], axis=1)
     dy_parts = [dy_own, tp_swap(after(dy_own, out_3[0]), 0), dy_side]
@@ -891,18 +897,19 @@
     join = lambda a, b: (a.astype(F32) + tp_swap(b, 0).astype(F32)).astype(BF16)
     dh_side = join(far[2], far[3])
     dh_own = near[2].astype(F32) + tp_swap(near[3], 0).astype(F32)
-    grads_outer = expert_grads(
-        [after(h2_parts[0], dh_side), *h2_parts[1:]], dy_parts, (near[4], far[4]), (near[5], far[5])
-    )
     grads_inner = expert_grads(
-        [after(h2_parts[0], grads_outer), *h2_parts[1:]],
+        [after(h2_parts[0], dh_side), *h2_parts[1:]],
         dy_parts,
         (first[4], third_pass[4]),
         (first[5], third_pass[5]),
     )
-    mixed_side = join(far[0], after(far[1], grads_outer))
-    mixed_core = tp_swap(after(near[1], grads_outer), 0)
-    dh_sum = after(dh_own, grads_inner, mixed_side, mixed_core) + after(y_swap(dh_side), grads_outer).astype(F32)
+    grads_outer = expert_grads(
+        [after(h2_parts[0], grads_inner), *h2_parts[1:]],
+        dy_parts,
+        (near[4], far[4]),
+        (near[5], far[5]),
+    )
+    dh_sum = after(dh_own, grads_outer) + after(y_swap(dh_side), grads_outer).astype(F32)
     probs = jax.nn.softmax(dot(h2, w_router), axis=-1)
     dprobs = dh_sum[:, width : width + experts]
     dprobs = dprobs + dh_sum[:, width + LANES // 2 : width + LANES // 2 + experts]
@@ -918,8 +925,8 @@
     gain2 = jnp.sum(dh2 * n2, axis=0, keepdims=True)
 
     if nz == 4:
-        reduce = lambda g, axis: lax.psum_scatter(g, axis, scatter_dimension=0, tiled=True)
-        inner, outer = reduce(grads_inner[0], "z"), reduce(grads_outer[0], "z")
+        reduce = lambda g: lax.psum_scatter(g, "z", scatter_dimension=0, tiled=True)
+        inner, outer = reduce(grads_inner[0]), reduce(grads_outer[0])
     else:
         inner, outer = grads_inner, grads_outer
 
@@ -940,34 +947,27 @@
             if i >= half:
                 da_parts[i | (1 << bit)] = tp_swap(da_parts[i], bit)
     da_parts = [da_parts[i] for i in range(blocks)]
-    mixed_side = y_swap(after(mixed_side, da))
     out_part = out_grads(
-        [after(da_parts[0], dq_near, mixed_side), *da_parts[1:half]], o_near, None
+        [after(da_parts[0], dq_near), *da_parts[1:half]], o_near, None
     )
     out_part = out_grads(da_parts[half:], o_far, out_part)
-    each = width // (2 * nz)
-
-    def pick(grad, at):
-        grad = grad.reshape(nz, 2, each, grad.shape[1])
-        return lax.dynamic_index_in_dim(grad, at, 1, keepdims=False)
-
-    before = [out_part]
+    mixed_side = join(after(far[0], dq_near), after(far[1], dq_near))
+    mixed_core = tp_swap(after(near[1], dq_near), 0)
+    before = [out_part, mixed_side, mixed_core]
     if nz == 4:
 
-        def x_reduce(g, cover):
-            pick_rows = lambda at: lax.dynamic_slice_in_dim(g, at * (width // 8), width // 8, 0)
-            other = after(tp_swap(pick_rows(1 - ix), 1), cover)
-            return (pick_rows(ix).astype(F32) + other.astype(F32)).astype(BF16)
-
-        before.append(outer)
+        rows_of = lambda g, at: lax.dynamic_slice_in_dim(g, at * each, each, 0)
+        inner_side = tp_swap(rows_of(inner, 1 - ix), 1)
+        before.append(inner)
     dq_far, dkv = back(after(q_far, *before), o_far, lse_far, da_parts[half:], half, sums)
     out_side = after(y_swap(pick(out_part, 1 - iy)), dkv)
+    mixed_side = after(y_swap(mixed_side), dkv)
     qkv_grad, gain1 = qkv_grads(
         h_parts, dq_near, dq_far, dkv, w_all_t, norm1_gain)
     qkv_side = y_swap(pick(qkv_grad, 1 - iy))
     dh1_far = input_grads(after(dq_far, qkv_grad), dkv, w_all_t, rows, 1)
-    qkv_side = after(qkv_side, dh1_far[0])
     dh1_side = fold(dh1_far, BF16)
+    qkv_side = after(qkv_side, dh1_side)
     dh1_near = input_grads(
         dq_near, after(dkv, dh1_side, qkv_side), w_all_t, rows, 0
     )
@@ -991,9 +991,10 @@
     small = jnp.concatenate([router_part, gain2, gain1], axis=0)
     small = own_columns(sum_all(after(small, dh1_side)))
     if nz == 4:
-        outer = x_reduce(outer, dkv)
-        inner = x_reduce(after(inner, dh1_side), dh1_near[0])
-        outer = after(outer, dh1_side)
+        inner = rows_of(inner, ix).astype(F32) + after(inner_side, dh1_side).astype(F32)
+        outer_side = tp_swap(rows_of(after(outer, dh1_side), 1 - ix), 1)
+        outer = rows_of(outer, ix).astype(F32) + outer_side.astype(F32)
+        inner, outer = inner.astype(BF16), outer.astype(BF16)
         home = lambda c, inside: (3 - inside if c else inside)
         moves = [
             [

time: 607 us -> 591 us (0.974)
  waiting for transfers between devices: 112 us -> 93.2 us
  starting transfers between devices: 100 us -> 109 us
    ppermute x7, waiting for transfers between devices: 55.3 us -> 23.1 us  [tp_swap(): return lax.ppermute(value, 'x', [(i, i ^ 1 << bit - 1) for i in range(nx)])]
    ppermute x7, waiting for transfers between devices: 26.2 us -> 32.9 us  [y_swap(): return lax.ppermute(value, 'y', [(0, 1), (1, 0)])]
    unnamed x68 -> x70, local copies, waits for them, and re-layouts: 13 us -> 13.4 us
  transfers between devices with their start and end apart: 42 -> 42, of which waited for: 15 -> 15; matrix products, arithmetic and copies ran while one was open for 14% -> 14% of each run, Pallas kernels for 35% -> 36%
where the time goes in v4:
time: 591 us; the launch traced here: 582 us
  Pallas kernels  270 us (46%)
  starting transfers between devices  109 us (18%)
  waiting for transfers between devices  93.2 us (16%)
  other arithmetic  61.6 us (10%)
  local copies, waits for them, and re-layouts  27.9 us (5%)
  between operations  14.8 us (3%)
    pallas_call x4, Pallas kernels, run_experts(): pl.pallas_call(functools.partial(expert_kernel, experts, bool(old), len(c...  84.8 us
    pallas_call x2, Pallas kernels, attend_back(): pl.pallas_call(functools.partial(attend_back_kernel, rows, zone, heads, g...  58.4 us
    pallas_call x3, Pallas kernels, attend(): pl.pallas_call(functools.partial(attend_kernel, rows, zone, heads, groups...  48.1 us
    ppermute x7, starting transfers between devices, tp_swap(): return lax.ppermute(value, 'x', [(i, i ^ 1 << bit - 1) for i in range(nx)])  42 us
    pallas_call x2, Pallas kernels, expert_grads(): pl.pallas_call(expert_grad_kernel, grid=(mine,), in_specs=[anywhere] * 12...  34.9 us
    ppermute x7, waiting for transfers between devices, y_swap(): return lax.ppermute(value, 'y', [(0, 1), (1, 0)])  32.9 us
    ppermute x17, starting transfers between devices, tp_swap(): return lax.ppermute(value, 'c', [(0, 1), (1, 0)])  23.7 us
    ppermute x7, waiting for transfers between devices, tp_swap(): return lax.ppermute(value, 'x', [(i, i ^ 1 << bit - 1) for i in range(nx)])  23.1 us
  transfers between devices with their start and end apart: 42, of which 15 were waited for; matrix products, arithmetic and copies ran while one was open for 14% of the time, Pallas kernels for 36%

profile of v4, /device:TPU:2, one launch (start us, length us, event | category | flops | bytes accessed | tf_op | source)
XLA Modules:
  0.0 581.5 jit_solution(16979366025547656251)
XLA Ops:
  13.7 3.6 pad_maximum_fusion
  17.4 6.4 %collective-permute-start.1 = (bf16[1,1536,1536]{2,1,0:T(8,128)(2,1)}, bf16[1,1536,1536]{2,1,0:T(8,128)(2,1)}, u32[]{:S(2)}, u32[]{:S(2)}) collective-permute-start(bf16[1,1536,1536]{2,1,0:T(8,128)(2,1)} %bitcast.4.refs_7_.refs_6_), channel_id=1, source_target_pairs={{0,8},{8,16},{25,17},{17,9},{2,10},{10,18},{27,19},{19,11},{4,12},... | collective-permute-start | bytes 14155784 | tf_op jit(solution)/shard_map/ppermute | solution.py:839
  30.0 6.2 %qkv.2 = (bf16[384,1024]{1,0:T(8,128)(2,1)}, bf16[2,2048,64]{2,1,0:T(8,128)(2,1)}, bf16[128,2048]{1,0:T(8,128)(2,1)}, bf16[2,2048,64]{2,1,0:T(8,128)(2,1)}, bf16[128,2048]{1,0:T(8,128)(2,1)}) custom-call(bf16[512,1536]{1,0:T(8,128)(2,1)} %multiply_convert_fusion.1.refs_0_, bf16[512,1536]{1,0:T(8,128)(2,1)} %collective-permute-done.refs_1_, ...), custom_call_target="tpu_custom_call" | custom-call | flops 6000000000 | bytes 18000000 | tf_op jit(solution)/shard_map/qkv/pallas_call | solution.py:90
  36.2 12.9 %collective-permute-done.2.refs_0_.refs_2_ = bf16[512,1536]{1,0:T(8,128)(2,1)} collective-permute-done((bf16[512,1536]{1,0:T(8,128)(2,1)}, bf16[512,1536]{1,0:T(8,128)(2,1)}, u32[]{:S(2)}, u32[]{:S(2)}) %collective-permute-start.2) | collective-permute-done | bytes 1572896 | tf_op jit(solution)/shard_map/ppermute | solution.py:755
  54.0 6.2 %qkv.3 = (bf16[384,1024]{1,0:T(8,128)(2,1)}, bf16[2,2048,64]{2,1,0:T(8,128)(2,1)}, bf16[128,2048]{1,0:T(8,128)(2,1)}, bf16[2,2048,64]{2,1,0:T(8,128)(2,1)}, bf16[128,2048]{1,0:T(8,128)(2,1)}) custom-call(bf16[512,1536]{1,0:T(8,128)(2,1)} %collective-permute-done.2.refs_0_.refs_2_, ...), custom_call_target="tpu_custom_call", output_to_operand_aliasing={{1}: (5, {}), {2}: (6, {}), {3}: (7, {}), {4}: (8, {})} | custom-call | flops 6000000000 | bytes 18000000 | tf_op jit(solution)/shard_map/qkv/pallas_call | solution.py:90
  60.2 11.3 %attend.3 = (bf16[384,512]{1,0:T(8,128)(2,1)}, f32[6,512]{1,0:T(8,128)}, bf16[512,1536]{1,0:T(8,128)(2,1)}) custom-call(s32[9]{0:T(128)} %pad_add_fusion.s_ref.refs_0_, bf16[384,1024]{1,0:T(8,128)(2,1)} %get-tuple-element.167.q_ref.refs_1_, bf16[2,2048,64]{2,1,0:T(8,128)(2,1)} %get-tuple-element.110.k_ref.refs_4_, ...), custom_call_target="tpu_custom_call" | custom-call | flops 8999999488 | bytes 27000000 | tf_op jit(solution)/shard_map/attend/pallas_call | solution.py:186
  79.5 8.3 %attend.4 = (bf16[384,512]{1,0:T(8,128)(2,1)}, f32[6,512]{1,0:T(8,128)}, bf16[512,1536]{1,0:T(8,128)(2,1)}) custom-call(s32[9]{0:T(128)} %pad_add_fusion.s_ref.refs_0_, bf16[384,1024]{1,0:T(8,128)(2,1)} %get-tuple-element.167.q_ref.refs_1_, bf16[2,2048,64]{2,1,0:T(8,128)(2,1)} %get-tuple-element.110.k_ref.refs_4_, ...), custom_call_target="tpu_custom_call" | custom-call | flops 2000000000 | bytes 6000000 | tf_op jit(solution)/shard_map/attend/pallas_call | solution.py:186
  87.8 3.4 add_convert_fusion.3
  91.2 10.8 %collective-permute-start.9 = (bf16[512,1536]{1,0:T(8,128)(2,1)}, bf16[512,1536]{1,0:T(8,128)(2,1)}, u32[]{:S(2)}, u32[]{:S(2)}) collective-permute-start(bf16[512,1536]{1,0:T(8,128)(2,1)} %add_convert_fusion.3), channel_id=1, source_target_pairs={{0,2},{2,0},{1,3},{3,1},{4,6},{6,4},{5,7},{7,5},{8,10},{10,8},{9,1... | collective-permute-start | bytes 4718600 | tf_op jit(solution)/shard_map/ppermute | solution.py:755
  102.0 28.4 %attend.5 = (bf16[384,1024]{1,0:T(8,128)(2,1)}, f32[6,1024]{1,0:T(8,128)}, bf16[512,1536]{1,0:T(8,128)(2,1)}, bf16[512,1536]{1,0:T(8,128)(2,1)}) custom-call(s32[9]{0:T(128)} %pad_add_fusion.s_ref.refs_0_, bf16[384,1024]{1,0:T(8,128)(2,1)} %get-tuple-element.118.q_ref.refs_1_, bf16[2,2048,64]{2,1,0:T(8,128)(2,1)} %get-tuple-element.110.k_ref.refs_4_, ...), custom_call_target="tpu_custom_call" | custom-call | flops 2000000000 | bytes 6000000 | tf_op jit(solution)/shard_map/attend/pallas_call | solution.py:186
  130.5 3.1 collective-permute-start.8
  140.9 2.9 collective-permute-start.15
  145.3 16.3 %collective-permute-start.11 = (bf16[512,1536]{1,0:T(8,128)(2,1)}, bf16[512,1536]{1,0:T(8,128)(2,1)}, u32[]{:S(2)}, u32[]{:S(2)}) collective-permute-start(bf16[512,1536]{1,0:T(8,128)(2,1)} %multiply_convert_fusion.refs_1_.refs_0_), channel_id=1, source_target_pairs={{0,1},{1,0},{2,3},{3,2},{4,5},{5,4},{6,7},{7,6},{8,9},{9,8},{10,11... | collective-permute-start | bytes 4718600 | tf_op jit(solution)/shard_map/ppermute | solution.py:754
  166.9 20.0 %experts.4 = (bf16[512,1536]{1,0:T(8,128)(2,1)}, bf16[512,1536]{1,0:T(8,128)(2,1)}, bf16[512,1664]{1,0:T(8,128)(2,1)}, bf16[512,1664]{1,0:T(8,128)(2,1)}, bf16[1...) custom-call(s32[2]{0:T(128)} %pad_add_fusion.2.refs_0_, bf16[512,1536]{1,0:T(8,128)(2,1)} %multiply_convert_fusion.refs_1_.refs_0_, ...), custom_call_target="tpu_custom_call" | custom-call | flops 8000000000 | bytes 24000000 | tf_op jit(solution)/shard_map/experts/pallas_call | solution.py:600
  186.9 11.4 %collective-permute-done.10.refs_1_.refs_2_ = bf16[512,1536]{1,0:T(8,128)(2,1)} collective-permute-done((bf16[512,1536]{1,0:T(8,128)(2,1)}, bf16[512,1536]{1,0:T(8,128)(2,1)}, u32[]{:S(2)}, u32[]{:S(2)}) %collective-permute-start.10) | collective-permute-done | bytes 1572896 | tf_op jit(solution)/shard_map/ppermute | solution.py:758
  202.1 20.0 %experts.5 = (bf16[512,1536]{1,0:T(8,128)(2,1)}, bf16[512,1536]{1,0:T(8,128)(2,1)}, bf16[512,1664]{1,0:T(8,128)(2,1)}, bf16[512,1664]{1,0:T(8,128)(2,1)}, bf16[1...) custom-call(s32[2]{0:T(128)} %pad_add_fusion.2.refs_0_, ...), custom_call_target="tpu_custom_call" | custom-call | flops 8000000000 | bytes 24000000 | tf_op jit(solution)/shard_map/experts/pallas_call | solution.py:600
  222.1 22.4 %experts.6 = (bf16[512,1536]{1,0:T(8,128)(2,1)}, bf16[512,1536]{1,0:T(8,128)(2,1)}, bf16[512,1664]{1,0:T(8,128)(2,1)}, bf16[512,1664]{1,0:T(8,128)(2,1)}, bf16[1...) custom-call(s32[2]{0:T(128)} %pad_add_fusion.1.refs_0_, bf16[512,1536]{1,0:T(8,128)(2,1)} %multiply_convert_fusion.refs_1_.refs_0_, ...), custom_call_target="tpu_custom_call" | custom-call | flops 8000000000 | bytes 24000000 | tf_op jit(solution)/shard_map/experts/pallas_call | solution.py:600
  244.5 22.4 %experts.7 = (bf16[512,1536]{1,0:T(8,128)(2,1)}, bf16[512,1536]{1,0:T(8,128)(2,1)}, bf16[512,1664]{1,0:T(8,128)(2,1)}, bf16[512,1664]{1,0:T(8,128)(2,1)}, bf16[1...) custom-call(s32[2]{0:T(128)} %pad_add_fusion.1.refs_0_, ...), custom_call_target="tpu_custom_call" | custom-call | flops 8000000000 | bytes 24000000 | tf_op jit(solution)/shard_map/experts/pallas_call | solution.py:600
  267.1 3.7 collective-permute-done.17
  270.8 3.1 add_convert_fusion
  273.9 17.6 %expert_grads.2 = bf16[1,1536,1536]{2,1,0:T(8,128)(2,1)} custom-call(bf16[512,1536]{1,0:T(8,128)(2,1)} %multiply_convert_fusion.refs_1_.refs_0_, bf16[512,1536]{1,0:T(8,128)(2,1)} %collective-permute-done.11.refs_2_.refs_1_, bf16[512,1536]{1,0:T(8,128)(2,1)} %collective-permute-done.10.refs_1_.refs_2_, ...), custom_call_target="tpu_custom_call" | custom-call | flops 1000000000 | bytes 3000000 | tf_op jit(solution)/shard_map/expert_grads/pallas_call | solution.py:704
  295.6 17.4 %expert_grads.3 = bf16[1,1536,1536]{2,1,0:T(8,128)(2,1)} custom-call(bf16[512,1536]{1,0:T(8,128)(2,1)} %multiply_convert_fusion.refs_1_.refs_0_, bf16[512,1536]{1,0:T(8,128)(2,1)} %collective-permute-done.11.refs_2_.refs_1_, bf16[512,1536]{1,0:T(8,128)(2,1)} %collective-permute-done.10.refs_1_.refs_2_, ...), custom_call_target="tpu_custom_call" | custom-call | flops 1000000000 | bytes 3000000 | tf_op jit(solution)/shard_map/expert_grads/pallas_call | solution.py:704
  315.3 16.2 %collective-permute-done.18 = bf16[512,1664]{1,0:T(8,128)(2,1)} collective-permute-done((bf16[512,1664]{1,0:T(8,128)(2,1)}, bf16[512,1664]{1,0:T(8,128)(2,1)}, u32[]{:S(2)}, u32[]{:S(2)}) %collective-permute-start.18) | collective-permute-done | bytes 1703968 | tf_op jit(solution)/shard_map/ppermute | solution.py:758
  335.5 3.3 fusion.9
  339.2 3.3 collective-permute-done.20.refs_11_.refs_1_
  342.5 36.2 %attend_back.2 = (bf16[384,1024]{1,0:T(8,128)(2,1)}, f32[2,2048,64]{2,1,0:T(8,128)}, f32[2,2048,64]{2,1,0:T(8,128)}) custom-call(s32[9]{0:T(128)} %pad_add_fusion.s_ref.refs_0_, bf16[384,1024]{1,0:T(8,128)(2,1)} %get-tuple-element.118.q_ref.refs_1_, bf16[384,1024]{1,0:T(8,128)(2,1)} %get-tuple-element.152.refs_2_, f32[6,1024]{1,0:T(8,128)} %get-tuple-element.153.refs_3_, ...), custom_call_target="tpu_custom_call" | custom-call | flops 30000001024 | bytes 90000000 | tf_op jit(solution)/shard_map/attend_back/pallas_call | solution.py:329
  382.5 4.9 out_grads.2.refs_3_
  387.4 3.4 add_convert_fusion.2
  392.4 5.4 out_grads.3
  397.7 22.2 %attend_back.3 = (bf16[384,1024]{1,0:T(8,128)(2,1)}, bf16[256,2048]{1,0:T(8,128)(2,1)}) custom-call(s32[9]{0:T(128)} %pad_add_fusion.s_ref.refs_0_, bf16[384,1024]{1,0:T(8,128)(2,1)} %get-tuple-element.167.q_ref.refs_1_, bf16[384,1024]{1,0:T(8,128)(2,1)} %copy-done.19, f32[6,1024]{1,0:T(8,128)} %pad_maximum_fusion.4.refs_3_, ...), custom_call_target="tpu_custom_call" | custom-call | flops 30000001024 | bytes 90000000 | tf_op jit(solution)/shard_map/attend_back/pallas_call | solution.py:329
  420.0 9.9 %qkv_grads.1 = (bf16[1536,640]{1,0:T(8,128)(2,1)}, f32[1,1536]{1,0:T(1,128)}) custom-call(bf16[512,1536]{1,0:T(8,128)(2,1)} %multiply_convert_fusion.1.refs_0_, bf16[512,1536]{1,0:T(8,128)(2,1)} %collective-permute-done.refs_1_, bf16[512,1536]{1,0:T(8,128)(2,1)} %collective-permute-done.2.refs_0_.refs_2_, bf16[512,1536]{1,0:T(8,128)(2,1)} %copy-done.30, ...), custom_call_target="tpu_custom_call" | custom-call | flops 10000000000 | bytes 30000000 | tf_op jit(solution)/shard_map/qkv_grads/pallas_call | solution.py:396
  429.8 5.8 input_grads.2
  441.3 13.4 %collective-permute-start.35 = (bf16[192,1536]{1,0:T(8,128)(2,1)}, bf16[192,1536]{1,0:T(8,128)(2,1)}, u32[]{:S(2)}, u32[]{:S(2)}) collective-permute-start(bf16[192,1536]{1,0:T(8,128)(2,1)} %constant_dynamic-slice_fusion.1), channel_id=1, source_target_pairs={{0,2},{2,0},{1,3},{3,1},{4,6},{6,4},{5,7},{7,5},{8,10},{10,8},{9,1... | collective-permute-start | bytes 1769480 | tf_op jit(solution)/shard_map/ppermute | solution.py:755
  459.2 2.9 add_convert_fusion.1
  462.1 8.9 %collective-permute-start.28 = (bf16[512,1536]{1,0:T(8,128)(2,1)}, bf16[512,1536]{1,0:T(8,128)(2,1)}, u32[]{:S(2)}, u32[]{:S(2)}) collective-permute-start(bf16[512,1536]{1,0:T(8,128)(2,1)} %add_convert_fusion.1), channel_id=1, source_target_pairs={{0,2},{2,0},{1,3},{3,1},{4,6},{6,4},{5,7},{7,5},{8,10},{10,8},{9,1... | collective-permute-start | bytes 4718600 | tf_op jit(solution)/shard_map/ppermute | solution.py:755
  471.0 3.6 collective-permute-start.29
  476.7 3.7 collective-permute-done.26
  480.4 6.8 %collective-permute-start.30 = (f32[10,1536]{1,0:T(8,128)S(1)}, f32[10,1536]{1,0:T(8,128)S(1)}, u32[]{:S(2)}, u32[]{:S(2)}) collective-permute-start(f32[10,1536]{1,0:T(8,128)S(1)} %add.188), channel_id=1, source_target_pairs={{0,16},{8,24},{16,0},{24,8},{1,17},{9,25},{17,1},{25,9},{2,18},{10... | collective-permute-start | bytes 184328 | tf_op jit(solution)/shard_map/ppermute | solution.py:777
  495.2 5.8 input_grads.3
  501.5 8.4 %collective-permute-start.33 = (f32[10,1536]{1,0:T(8,128)S(1)}, f32[10,1536]{1,0:T(8,128)S(1)}, u32[]{:S(2)}, u32[]{:S(2)}) collective-permute-start(f32[10,1536]{1,0:T(8,128)S(1)} %add.191), channel_id=1, source_target_pairs={{0,2},{2,0},{1,3},{3,1},{4,6},{6,4},{5,7},{7,5},{8,10},{10,8},{9,1... | collective-permute-start | bytes 184328 | tf_op jit(solution)/shard_map/ppermute | solution.py:755
  509.9 9.2 %collective-permute-done.36 = bf16[192,1536]{1,0:T(8,128)(2,1)} collective-permute-done((bf16[192,1536]{1,0:T(8,128)(2,1)}, bf16[192,1536]{1,0:T(8,128)(2,1)}, u32[]{:S(2)}, u32[]{:S(2)}) %collective-permute-start.36) | collective-permute-done | bytes 589856 | tf_op jit(solution)/shard_map/ppermute | solution.py:755
  521.0 3.7 collective-permute-start.37
  524.7 5.2 collective-permute-start.38
  530.0 4.4 convert_add_fusion.2
  535.6 9.7 %collective-permute-done.37 = bf16[192,1536]{1,0:T(8,128)(2,1)S(1)} collective-permute-done((bf16[192,1536]{1,0:T(8,128)(2,1)S(1)}, bf16[192,1536]{1,0:T(8,128)(2,1)S(1)}, u32[]{:S(2)}, u32[]{:S(2)}) %collective-permute-start.37) | collective-permute-done | bytes 589856 | tf_op jit(solution)/shard_map/ppermute | solution.py:1009
  545.2 12.5 %collective-permute-done.38 = bf16[192,1536]{1,0:T(8,128)(2,1)S(1)} collective-permute-done((bf16[192,1536]{1,0:T(8,128)(2,1)S(1)}, bf16[192,1536]{1,0:T(8,128)(2,1)S(1)}, u32[]{:S(2)}, u32[]{:S(2)}) %collective-permute-start.38) | collective-permute-done | bytes 589856 | tf_op jit(solution)/shard_map/ppermute | solution.py:1010
  562.3 3.1 multiply_reduce_fusion.1
  565.4 4.8 multiply_add_fusion
  (195 shorter events, 92.0 us)
Async XLA Ops:
  7.2 390.6 %reduce-scatter.4.cloned.1.call-start = ((), (), s32[]{:S(2)}) async-start(), calls=%async_computation.3 | async-start | bytes 5898240 | tf_op jit(solution)/shard_map/reduce_scatter | solution.py:928
  12.0 5.4 collective-permute-start
  12.0 37.1 %collective-permute-start.2 = (bf16[512,1536]{1,0:T(8,128)(2,1)}, bf16[512,1536]{1,0:T(8,128)(2,1)}, u32[]{:S(2)}, u32[]{:S(2)}) collective-permute-start(bf16[512,1536]{1,0:T(8,128)(2,1)} %multiply_convert_fusion.1.refs_0_), channel_id=1, source_target_pairs={{0,2},{2,0},{1,3},{3,1},{4,6},{6,4},{5,7},{7,5},{8,10},{10,8},{9,1... | collective-permute-start | bytes 4718600 | tf_op jit(solution)/shard_map/ppermute | solution.py:755
  17.4 56.1 %collective-permute-start.1 = (bf16[1,1536,1536]{2,1,0:T(8,128)(2,1)}, bf16[1,1536,1536]{2,1,0:T(8,128)(2,1)}, u32[]{:S(2)}, u32[]{:S(2)}) collective-permute-start(bf16[1,1536,1536]{2,1,0:T(8,128)(2,1)} %bitcast.4.refs_7_.refs_6_), channel_id=1, source_target_pairs={{0,8},{8,16},{25,17},{17,9},{2,10},{10,18},{27,19},{19,11},{4,12},... | collective-permute-start | bytes 14155784 | tf_op jit(solution)/shard_map/ppermute | solution.py:839
  49.1 3.6 collective-permute-start.3
  49.7 87.7 %collective-permute-start.6 = (bf16[1,1536,1536]{2,1,0:T(8,128)(2,1)}, bf16[1,1536,1536]{2,1,0:T(8,128)(2,1)}, u32[]{:S(2)}, u32[]{:S(2)}) collective-permute-start(bf16[1,1536,1536]{2,1,0:T(8,128)(2,1)} %bitcast.4.refs_7_.refs_6_), channel_id=1, source_target_pairs={{8,0},{17,25},{10,2},{19,27},{12,4},{21,29},{14,6},{23,31}} | collective-permute-start | bytes 14155784 | tf_op jit(solution)/shard_map/ppermute | solution.py:839
  73.4 64.0 %collective-permute-start.4 = (bf16[1,1536,1536]{2,1,0:T(8,128)(2,1)}, bf16[1,1536,1536]{2,1,0:T(8,128)(2,1)}, u32[]{:S(2)}, u32[]{:S(2)}) collective-permute-start(bf16[1,1536,1536]{2,1,0:T(8,128)(2,1)} %collective-permute-done.1.refs_8_.refs_7_), channel_id=1, source_target_pairs={{8,16},{16,24},{17,9},{9,1},{10,18},{18,26},{19,11},{11,3},{12,20}... | collective-permute-start | bytes 14155784 | tf_op jit(solution)/shard_map/ppermute | solution.py:839
  76.2 11.6 %collective-permute-start.7 = (bf16[512,1536]{1,0:T(8,128)(2,1)}, bf16[512,1536]{1,0:T(8,128)(2,1)}, u32[]{:S(2)}, u32[]{:S(2)}) collective-permute-start(bf16[512,1536]{1,0:T(8,128)(2,1)} %get-tuple-element.112), channel_id=1, source_target_pairs={{0,1},{1,0},{2,3},{3,2},{4,5},{5,4},{6,7},{7,6},{8,9},{9,8},{10,11... | collective-permute-start | bytes 4718600 | tf_op jit(solution)/shard_map/ppermute | solution.py:754
  77.9 59.5 %collective-permute-start.5 = (bf16[512,1664]{1,0:T(8,128)(2,1)}, bf16[512,1664]{1,0:T(8,128)(2,1)S(1)}, u32[]{:S(2)}, u32[]{:S(2)}) collective-permute-start(bf16[512,1664]{1,0:T(8,128)(2,1)} %pad_maximum_fusion.1.refs_3_.refs_4_), channel_id=1, source_target_pairs={{0,4},{4,0},{1,5},{5,1},{2,6},{6,2},{3,7},{7,3},{8,12},{12,8},{9,1... | collective-permute-start | bytes 5111816 | tf_op jit(solution)/shard_map/ppermute | solution.py:758
  91.2 43.7 %collective-permute-start.9 = (bf16[512,1536]{1,0:T(8,128)(2,1)}, bf16[512,1536]{1,0:T(8,128)(2,1)}, u32[]{:S(2)}, u32[]{:S(2)}) collective-permute-start(bf16[512,1536]{1,0:T(8,128)(2,1)} %add_convert_fusion.3), channel_id=1, source_target_pairs={{0,2},{2,0},{1,3},{3,1},{4,6},{6,4},{5,7},{7,5},{8,10},{10,8},{9,1... | collective-permute-start | bytes 4718600 | tf_op jit(solution)/shard_map/ppermute | solution.py:755
  130.5 8.1 %collective-permute-start.8 = (bf16[512,1536]{1,0:T(8,128)(2,1)}, bf16[512,1536]{1,0:T(8,128)(2,1)S(1)}, u32[]{:S(2)}, u32[]{:S(2)}) collective-permute-start(bf16[512,1536]{1,0:T(8,128)(2,1)} %get-tuple-element.120), channel_id=1, source_target_pairs={{0,1},{1,0},{2,3},{3,2},{4,5},{5,4},{6,7},{7,6},{8,9},{9,8},{10,11... | collective-permute-start | bytes 4718600 | tf_op jit(solution)/shard_map/ppermute | solution.py:754
  134.9 31.9 %collective-permute-start.12 = (bf16[512,1664]{1,0:T(8,128)(2,1)}, bf16[512,1664]{1,0:T(8,128)(2,1)}, u32[]{:S(2)}, u32[]{:S(2)}) collective-permute-start(bf16[512,1664]{1,0:T(8,128)(2,1)} %pad_maximum_fusion.1.refs_3_.refs_4_), channel_id=1, source_target_pairs={{0,1},{1,0},{2,3},{3,2},{4,5},{5,4},{6,7},{7,6},{8,9},{9,8},{10,11... | collective-permute-start | bytes 5111816 | tf_op jit(solution)/shard_map/ppermute | solution.py:754
  140.9 81.1 %collective-permute-start.15 = (bf16[1,1536,1536]{2,1,0:T(8,128)(2,1)}, bf16[1,1536,1536]{2,1,0:T(8,128)(2,1)}, u32[]{:S(2)}, u32[]{:S(2)}) collective-permute-start(bf16[1,1536,1536]{2,1,0:T(8,128)(2,1)} %collective-permute-done.4.refs_9_.refs_8_), channel_id=1, source_target_pairs={{16,24},{9,1},{18,26},{11,3},{20,28},{13,5},{22,30},{15,7}} | collective-permute-start | bytes 14155784 | tf_op jit(solution)/shard_map/ppermute | solution.py:839
  145.3 21.5 %collective-permute-start.11 = (bf16[512,1536]{1,0:T(8,128)(2,1)}, bf16[512,1536]{1,0:T(8,128)(2,1)}, u32[]{:S(2)}, u32[]{:S(2)}) collective-permute-start(bf16[512,1536]{1,0:T(8,128)(2,1)} %multiply_convert_fusion.refs_1_.refs_0_), channel_id=1, source_target_pairs={{0,1},{1,0},{2,3},{3,2},{4,5},{5,4},{6,7},{7,6},{8,9},{9,8},{10,11... | collective-permute-start | bytes 4718600 | tf_op jit(solution)/shard_map/ppermute | solution.py:754
  161.7 36.6 %collective-permute-start.10 = (bf16[512,1536]{1,0:T(8,128)(2,1)}, bf16[512,1536]{1,0:T(8,128)(2,1)}, u32[]{:S(2)}, u32[]{:S(2)}) collective-permute-start(bf16[512,1536]{1,0:T(8,128)(2,1)} %multiply_convert_fusion.refs_1_.refs_0_), channel_id=1, source_target_pairs={{0,4},{4,0},{1,5},{5,1},{2,6},{6,2},{3,7},{7,3},{8,12},{12,8},{9,1... | collective-permute-start | bytes 4718600 | tf_op jit(solution)/shard_map/ppermute | solution.py:758
  166.8 32.7 %collective-permute-start.14 = (bf16[512,1664]{1,0:T(8,128)(2,1)}, bf16[512,1664]{1,0:T(8,128)(2,1)}, u32[]{:S(2)}, u32[]{:S(2)}) collective-permute-start(bf16[512,1664]{1,0:T(8,128)(2,1)} %copy-done.2), channel_id=1, source_target_pairs={{0,1},{1,0},{2,3},{3,2},{4,5},{5,4},{6,7},{7,6},{8,9},{9,8},{10,11... | collective-permute-start | bytes 5111816 | tf_op jit(solution)/shard_map/ppermute | solution.py:754
  198.3 3.8 collective-permute-start.13
  266.9 3.9 collective-permute-start.17
  291.5 179.5 %reduce-scatter.8.cloned.1.call-start = ((), (), s32[]{:S(2)}) async-start(), calls=%async_computation.5 | async-start | bytes 5898240 | tf_op jit(solution)/shard_map/reduce_scatter | solution.py:928
  291.6 21.4 %collective-permute-start.16 = (bf16[512,1664]{1,0:T(8,128)(2,1)}, bf16[512,1664]{1,0:T(8,128)(2,1)}, u32[]{:S(2)}, u32[]{:S(2)}) collective-permute-start(bf16[512,1664]{1,0:T(8,128)(2,1)} %get-tuple-element.134), channel_id=1, source_target_pairs={{0,1},{1,0},{2,3},{3,2},{4,5},{5,4},{6,7},{7,6},{8,9},{9,8},{10,11... | collective-permute-start | bytes 5111816 | tf_op jit(solution)/shard_map/ppermute | solution.py:754
  291.8 39.8 %collective-permute-start.18 = (bf16[512,1664]{1,0:T(8,128)(2,1)}, bf16[512,1664]{1,0:T(8,128)(2,1)}, u32[]{:S(2)}, u32[]{:S(2)}) collective-permute-start(bf16[512,1664]{1,0:T(8,128)(2,1)} %add_convert_fusion), channel_id=1, source_target_pairs={{0,4},{4,0},{1,5},{5,1},{2,6},{6,2},{3,7},{7,3},{8,12},{12,8},{9,1... | collective-permute-start | bytes 5111816 | tf_op jit(solution)/shard_map/ppermute | solution.py:758
  338.7 3.8 collective-permute-start.20
  338.7 231.5 %reduce-scatter.6.cloned.1.call-start = ((), (), s32[]{:S(2)}) async-start(), calls=%async_computation.4 | async-start | bytes 1966080 | tf_op jit(solution)/shard_map/reduce_scatter | solution.py:987
  338.8 40.0 %collective-permute-start.19 = (bf16[512,1536]{1,0:T(8,128)(2,1)}, bf16[512,1536]{1,0:T(8,128)(2,1)}, u32[]{:S(2)}, u32[]{:S(2)}) collective-permute-start(bf16[512,1536]{1,0:T(8,128)(2,1)} %get-tuple-element.160.refs_10_.refs_0_), channel_id=1, source_target_pairs={{0,2},{2,0},{1,3},{3,1},{4,6},{6,4},{5,7},{7,5},{8,10},{10,8},{9,1... | collective-permute-start | bytes 4718600 | tf_op jit(solution)/shard_map/ppermute | solution.py:755
  342.5 36.7 %copy-start.20 = (f32[1536]{0:T(1024)S(1)}, f32[1536]{0:T(1024)}, u32[]{:S(2)}) copy-start(f32[1536]{0:T(1024)} %param.16) | copy-start | bytes 18436
  342.5 38.5 %copy-start.24 = (f32[6,512]{1,0:T(8,128)S(1)}, f32[6,512]{1,0:T(8,128)}, u32[]{:S(2)}) copy-start(f32[6,512]{1,0:T(8,128)} %get-tuple-element.169) | copy-start | bytes 36868
  342.5 38.5 %copy-start.25 = (f32[6,512]{1,0:T(8,128)S(1)}, f32[6,512]{1,0:T(8,128)}, u32[]{:S(2)}) copy-start(f32[6,512]{1,0:T(8,128)} %get-tuple-element.168) | copy-start | bytes 36868
  342.5 39.1 %copy-start.16 = (bf16[384,512]{1,0:T(8,128)(2,1)S(1)}, bf16[384,512]{1,0:T(8,128)(2,1)}, u32[]{:S(2)}) copy-start(bf16[384,512]{1,0:T(8,128)(2,1)} %get-tuple-element.159) | copy-start | bytes 1179652
  378.6 8.8 %collective-permute-start.22 = (bf16[512,1536]{1,0:T(8,128)(2,1)}, bf16[512,1536]{1,0:T(8,128)(2,1)}, u32[]{:S(2)}, u32[]{:S(2)}) collective-permute-start(bf16[512,1536]{1,0:T(8,128)(2,1)} %get-tuple-element.164), channel_id=1, source_target_pairs={{0,1},{1,0},{2,3},{3,2},{4,5},{5,4},{6,7},{7,6},{8,9},{9,8},{10,11... | collective-permute-start | bytes 4718600 | tf_op jit(solution)/shard_map/ppermute | solution.py:754
  378.8 13.6 %collective-permute-start.21 = (bf16[512,1536]{1,0:T(8,128)(2,1)}, bf16[512,1536]{1,0:T(8,128)(2,1)}, u32[]{:S(2)}, u32[]{:S(2)}) collective-permute-start(bf16[512,1536]{1,0:T(8,128)(2,1)} %collective-permute-done.19.refs_0_.refs_10_), channel_id=1, source_target_pairs={{0,1},{1,0},{2,3},{3,2},{4,5},{5,4},{6,7},{7,6},{8,9},{9,8},{10,11... | collective-permute-start | bytes 4718600 | tf_op jit(solution)/shard_map/ppermute | solution.py:754
  380.8 16.9 %collective-permute-start.23 = (bf16[512,1536]{1,0:T(8,128)(2,1)}, bf16[512,1536]{1,0:T(8,128)(2,1)}, u32[]{:S(2)}, u32[]{:S(2)}) collective-permute-start(bf16[512,1536]{1,0:T(8,128)(2,1)} %get-tuple-element.166), channel_id=1, source_target_pairs={{0,1},{1,0},{2,3},{3,2},{4,5},{5,4},{6,7},{7,6},{8,9},{9,8},{10,11... | collective-permute-start | bytes 4718600 | tf_op jit(solution)/shard_map/ppermute | solution.py:754
  390.8 67.3 %collective-permute-start.25 = (bf16[512,1536]{1,0:T(8,128)(2,1)}, bf16[512,1536]{1,0:T(8,128)(2,1)}, u32[]{:S(2)}, u32[]{:S(2)}) collective-permute-start(bf16[512,1536]{1,0:T(8,128)(2,1)} %add_convert_fusion.2), channel_id=1, source_target_pairs={{0,4},{4,0},{1,5},{5,1},{2,6},{6,2},{3,7},{7,3},{8,12},{12,8},{9,1... | collective-permute-start | bytes 4718600 | tf_op jit(solution)/shard_map/ppermute | solution.py:758
  435.6 23.6 %collective-permute-start.24 = (bf16[512,1536]{1,0:T(8,128)(2,1)}, bf16[512,1536]{1,0:T(8,128)(2,1)}, u32[]{:S(2)}, u32[]{:S(2)}) collective-permute-start(bf16[512,1536]{1,0:T(8,128)(2,1)} %get-tuple-element.177), channel_id=1, source_target_pairs={{0,1},{1,0},{2,3},{3,2},{4,5},{5,4},{6,7},{7,6},{8,9},{9,8},{10,11... | collective-permute-start | bytes 4718600 | tf_op jit(solution)/shard_map/ppermute | solution.py:754
  437.0 21.1 %collective-permute-start.34 = (bf16[4,192,384]{2,1,0:T(8,128)(2,1)S(1)}, bf16[4,192,384]{2,1,0:T(8,128)(2,1)S(1)}, u32[]{:S(2)}, u32[]{:S(2)}) collective-permute-start(bf16[4,192,384]{2,1,0:T(8,128)(2,1)S(1)} %dynamic-slice_bitcast_fusion.2), channel_id=1, source_target_pairs={{0,4},{4,0},{1,5},{5,1},{2,6},{6,2},{3,7},{7,3},{8,12},{12,8},{9,1... | collective-permute-start | bytes 1769480 | tf_op jit(solution)/shard_map/ppermute | solution.py:758
  441.3 52.2 %collective-permute-start.35 = (bf16[192,1536]{1,0:T(8,128)(2,1)}, bf16[192,1536]{1,0:T(8,128)(2,1)}, u32[]{:S(2)}, u32[]{:S(2)}) collective-permute-start(bf16[192,1536]{1,0:T(8,128)(2,1)} %constant_dynamic-slice_fusion.1), channel_id=1, source_target_pairs={{0,2},{2,0},{1,3},{3,1},{4,6},{6,4},{5,7},{7,5},{8,10},{10,8},{9,1... | collective-permute-start | bytes 1769480 | tf_op jit(solution)/shard_map/ppermute | solution.py:755
  456.2 24.2 %collective-permute-start.26 = (bf16[4,192,640]{2,1,0:T(8,128)(2,1)}, bf16[4,192,640]{2,1,0:T(8,128)(2,1)}, u32[]{:S(2)}, u32[]{:S(2)}) collective-permute-start(bf16[4,192,640]{2,1,0:T(8,128)(2,1)} %get-tuple-element.228), channel_id=1, source_target_pairs={{0,4},{4,0},{1,5},{5,1},{2,6},{6,2},{3,7},{7,3},{8,12},{12,8},{9,1... | collective-permute-start | bytes 2949128 | tf_op jit(solution)/shard_map/ppermute | solution.py:758
  462.1 100.1 %collective-permute-start.28 = (bf16[512,1536]{1,0:T(8,128)(2,1)}, bf16[512,1536]{1,0:T(8,128)(2,1)}, u32[]{:S(2)}, u32[]{:S(2)}) collective-permute-start(bf16[512,1536]{1,0:T(8,128)(2,1)} %add_convert_fusion.1), channel_id=1, source_target_pairs={{0,2},{2,0},{1,3},{3,1},{4,6},{6,4},{5,7},{7,5},{8,10},{10,8},{9,1... | collective-permute-start | bytes 4718600 | tf_op jit(solution)/shard_map/ppermute | solution.py:755
  471.0 21.1 %copy-start.8 = (bf16[4,192,384]{2,1,0:T(8,128)(2,1)S(1)}, bf16[4,192,384]{2,1,0:T(8,128)(2,1)}, u32[]{:S(2)}) copy-start(bf16[4,192,384]{2,1,0:T(8,128)(2,1)} %fusion) | copy-start | bytes 1769476
  471.0 9.3 %collective-permute-start.29 = (f32[10,1536]{1,0:T(8,128)S(1)}, f32[10,1536]{1,0:T(8,128)S(1)}, u32[]{:S(2)}, u32[]{:S(2)}) collective-permute-start(f32[10,1536]{1,0:T(8,128)S(1)} %pad_maximum_fusion.3), channel_id=1, source_target_pairs={{0,8},{8,0},{16,24},{24,16},{1,9},{9,1},{17,25},{25,17},{2,10},{10... | collective-permute-start | bytes 184328 | tf_op jit(solution)/shard_map/ppermute | solution.py:777
  476.6 42.5 %collective-permute-start.36 = (bf16[192,1536]{1,0:T(8,128)(2,1)}, bf16[192,1536]{1,0:T(8,128)(2,1)}, u32[]{:S(2)}, u32[]{:S(2)}) collective-permute-start(bf16[192,1536]{1,0:T(8,128)(2,1)} %constant_dynamic-slice_fusion), channel_id=1, source_target_pairs={{0,2},{2,0},{1,3},{3,1},{4,6},{6,4},{5,7},{7,5},{8,10},{10,8},{9,1... | collective-permute-start | bytes 1769480 | tf_op jit(solution)/shard_map/ppermute | solution.py:755
  480.4 10.0 %collective-permute-start.30 = (f32[10,1536]{1,0:T(8,128)S(1)}, f32[10,1536]{1,0:T(8,128)S(1)}, u32[]{:S(2)}, u32[]{:S(2)}) collective-permute-start(f32[10,1536]{1,0:T(8,128)S(1)} %add.188), channel_id=1, source_target_pairs={{0,16},{8,24},{16,0},{24,8},{1,17},{9,25},{17,1},{25,9},{2,18},{10... | collective-permute-start | bytes 184328 | tf_op jit(solution)/shard_map/ppermute | solution.py:777
  490.4 4.7 collective-permute-start.31
  495.1 6.4 %collective-permute-start.32 = (f32[10,1536]{1,0:T(8,128)S(1)}, f32[10,1536]{1,0:T(8,128)S(1)}, u32[]{:S(2)}, u32[]{:S(2)}) collective-permute-start(f32[10,1536]{1,0:T(8,128)S(1)} %add.190), channel_id=1, source_target_pairs={{0,1},{1,0},{2,3},{3,2},{4,5},{5,4},{6,7},{7,6},{8,9},{9,8},{10,11... | collective-permute-start | bytes 184328 | tf_op jit(solution)/shard_map/ppermute | solution.py:754
  501.0 29.0 %copy-start.12 = (bf16[512,1536]{1,0:T(8,128)(2,1)S(1)}, bf16[512,1536]{1,0:T(8,128)(2,1)}, u32[]{:S(2)}) copy-start(bf16[512,1536]{1,0:T(8,128)(2,1)} %get-tuple-element.179) | copy-start | bytes 4718596
  501.0 61.3 %collective-permute-start.27 = (bf16[512,1536]{1,0:T(8,128)(2,1)}, bf16[512,1536]{1,0:T(8,128)(2,1)}, u32[]{:S(2)}, u32[]{:S(2)}) collective-permute-start(bf16[512,1536]{1,0:T(8,128)(2,1)} %get-tuple-element.184), channel_id=1, source_target_pairs={{0,1},{1,0},{2,3},{3,2},{4,5},{5,4},{6,7},{7,6},{8,9},{9,8},{10,11... | collective-permute-start | bytes 4718600 | tf_op jit(solution)/shard_map/ppermute | solution.py:754
  501.5 32.9 %collective-permute-start.33 = (f32[10,1536]{1,0:T(8,128)S(1)}, f32[10,1536]{1,0:T(8,128)S(1)}, u32[]{:S(2)}, u32[]{:S(2)}) collective-permute-start(f32[10,1536]{1,0:T(8,128)S(1)} %add.191), channel_id=1, source_target_pairs={{0,2},{2,0},{1,3},{3,1},{4,6},{6,4},{5,7},{7,5},{8,10},{10,8},{9,1... | collective-permute-start | bytes 184328 | tf_op jit(solution)/shard_map/ppermute | solution.py:755
  521.0 24.2 %collective-permute-start.37 = (bf16[192,1536]{1,0:T(8,128)(2,1)S(1)}, bf16[192,1536]{1,0:T(8,128)(2,1)S(1)}, u32[]{:S(2)}, u32[]{:S(2)}) collective-permute-start(bf16[192,1536]{1,0:T(8,128)(2,1)S(1)} %get-tuple-element.222), channel_id=1, source_target_pairs={{0,8},{1,16},{2,0},{3,24},{8,9},{9,17},{10,1},{11,25},{16,10},{17,... | collective-permute-start | bytes 1769480 | tf_op jit(solution)/shard_map/ppermute | solution.py:1009
  524.7 33.0 %collective-permute-start.38 = (bf16[192,1536]{1,0:T(8,128)(2,1)S(1)}, bf16[192,1536]{1,0:T(8,128)(2,1)S(1)}, u32[]{:S(2)}, u32[]{:S(2)}) collective-permute-start(bf16[192,1536]{1,0:T(8,128)(2,1)S(1)} %get-tuple-element.223), channel_id=1, source_target_pairs={{0,0},{1,24},{2,8},{3,16},{8,1},{9,25},{10,9},{11,17},{16,2},{17,2... | collective-permute-start | bytes 1769480 | tf_op jit(solution)/shard_map/ppermute | solution.py:1010
  (25 other events, 201.6 us)
Sparse Core Ops, SparseCore 0:
  291.6 89.9 reduce-scatter.3
  383.9 85.7 reduce-scatter.7
  493.7 43.0 reduce-scatter.5

commit v5 on v4

--- a/solution.py
+++ b/solution.py
@@ -715,7 +715,7 @@
             pltpu.SemaphoreType.DMA((12,)),
         ],
         compiler_params=params(),
-        cost_estimate=cost(1),
+        cost_estimate=cost(12),
         name="expert_grads",
     )(*h_parts, *dy_parts, *acts, *dgus)
 

time: 591 us -> 593 us (level)
    unnamed x70 -> x68, local copies, waits for them, and re-layouts: 13.4 us -> 9.92 us
where the time goes in v5:
time: 593 us; the launch traced here: 583 us
  Pallas kernels  271 us (46%)
  starting transfers between devices  113 us (19%)
  waiting for transfers between devices  91.8 us (15%)
  other arithmetic  64 us (11%)
  local copies, waits for them, and re-layouts  24.3 us (4%)
  between operations  14.8 us (2%)
    pallas_call x4, Pallas kernels, run_experts(): pl.pallas_call(functools.partial(expert_kernel, experts, bool(old), len(c...  84.8 us
    pallas_call x2, Pallas kernels, attend_back(): pl.pallas_call(functools.partial(attend_back_kernel, rows, zone, heads, g...  58.4 us
    pallas_call x3, Pallas kernels, attend(): pl.pallas_call(functools.partial(attend_kernel, rows, zone, heads, groups...  48 us
    ppermute x7, starting transfers between devices, tp_swap(): return lax.ppermute(value, 'x', [(i, i ^ 1 << bit - 1) for i in range(nx)])  40.1 us
    pallas_call x2, Pallas kernels, expert_grads(): pl.pallas_call(expert_grad_kernel, grid=(mine,), in_specs=[anywhere] * 12...  35.8 us
    ppermute x7, waiting for transfers between devices, y_swap(): return lax.ppermute(value, 'y', [(0, 1), (1, 0)])  31.4 us
    ppermute x17, starting transfers between devices, tp_swap(): return lax.ppermute(value, 'c', [(0, 1), (1, 0)])  27 us
    ppermute x7, waiting for transfers between devices, tp_swap(): return lax.ppermute(value, 'x', [(i, i ^ 1 << bit - 1) for i in range(nx)])  21.6 us
  transfers between devices with their start and end apart: 42, of which 15 were waited for; matrix products, arithmetic and copies ran while one was open for 14% of the time, Pallas kernels for 36%

profile of v5, /device:TPU:2, one launch (start us, length us, event | category | flops | bytes accessed | tf_op | source)
XLA Modules:
  0.0 583.5 jit_solution(17780128586038517232)
XLA Ops:
  13.2 3.7 pad_maximum_fusion
  16.9 6.4 %collective-permute-start.1 = (bf16[1,1536,1536]{2,1,0:T(8,128)(2,1)}, bf16[1,1536,1536]{2,1,0:T(8,128)(2,1)}, u32[]{:S(2)}, u32[]{:S(2)}) collective-permute-start(bf16[1,1536,1536]{2,1,0:T(8,128)(2,1)} %bitcast.4.refs_7_.refs_6_), channel_id=1, source_target_pairs={{0,8},{8,16},{25,17},{17,9},{2,10},{10,18},{27,19},{19,11},{4,12},... | collective-permute-start | bytes 14155784 | tf_op jit(solution)/shard_map/ppermute | solution.py:839
  29.5 6.2 %qkv.2 = (bf16[384,1024]{1,0:T(8,128)(2,1)}, bf16[2,2048,64]{2,1,0:T(8,128)(2,1)}, bf16[128,2048]{1,0:T(8,128)(2,1)}, bf16[2,2048,64]{2,1,0:T(8,128)(2,1)}, bf16[128,2048]{1,0:T(8,128)(2,1)}) custom-call(bf16[512,1536]{1,0:T(8,128)(2,1)} %multiply_convert_fusion.1.refs_0_, bf16[512,1536]{1,0:T(8,128)(2,1)} %collective-permute-done.refs_1_, ...), custom_call_target="tpu_custom_call" | custom-call | flops 6000000000 | bytes 18000000 | tf_op jit(solution)/shard_map/qkv/pallas_call | solution.py:90
  35.8 12.8 %collective-permute-done.2.refs_0_.refs_2_ = bf16[512,1536]{1,0:T(8,128)(2,1)} collective-permute-done((bf16[512,1536]{1,0:T(8,128)(2,1)}, bf16[512,1536]{1,0:T(8,128)(2,1)}, u32[]{:S(2)}, u32[]{:S(2)}) %collective-permute-start.2) | collective-permute-done | bytes 1572896 | tf_op jit(solution)/shard_map/ppermute | solution.py:755
  52.3 6.2 %qkv.3 = (bf16[384,1024]{1,0:T(8,128)(2,1)}, bf16[2,2048,64]{2,1,0:T(8,128)(2,1)}, bf16[128,2048]{1,0:T(8,128)(2,1)}, bf16[2,2048,64]{2,1,0:T(8,128)(2,1)}, bf16[128,2048]{1,0:T(8,128)(2,1)}) custom-call(bf16[512,1536]{1,0:T(8,128)(2,1)} %collective-permute-done.2.refs_0_.refs_2_, ...), custom_call_target="tpu_custom_call", output_to_operand_aliasing={{1}: (5, {}), {2}: (6, {}), {3}: (7, {}), {4}: (8, {})} | custom-call | flops 6000000000 | bytes 18000000 | tf_op jit(solution)/shard_map/qkv/pallas_call | solution.py:90
  58.5 11.3 %attend.3 = (bf16[384,512]{1,0:T(8,128)(2,1)}, f32[6,512]{1,0:T(8,128)}, bf16[512,1536]{1,0:T(8,128)(2,1)}) custom-call(s32[9]{0:T(128)} %pad_add_fusion.s_ref.refs_0_, bf16[384,1024]{1,0:T(8,128)(2,1)} %get-tuple-element.167.q_ref.refs_1_, bf16[2,2048,64]{2,1,0:T(8,128)(2,1)} %get-tuple-element.110.k_ref.refs_4_, ...), custom_call_target="tpu_custom_call" | custom-call | flops 8999999488 | bytes 27000000 | tf_op jit(solution)/shard_map/attend/pallas_call | solution.py:186
  69.9 3.1 collective-permute-done.1.refs_8_.refs_7_
  79.1 8.3 %attend.4 = (bf16[384,512]{1,0:T(8,128)(2,1)}, f32[6,512]{1,0:T(8,128)}, bf16[512,1536]{1,0:T(8,128)(2,1)}) custom-call(s32[9]{0:T(128)} %pad_add_fusion.s_ref.refs_0_, bf16[384,1024]{1,0:T(8,128)(2,1)} %get-tuple-element.167.q_ref.refs_1_, bf16[2,2048,64]{2,1,0:T(8,128)(2,1)} %get-tuple-element.110.k_ref.refs_4_, ...), custom_call_target="tpu_custom_call" | custom-call | flops 2000000000 | bytes 6000000 | tf_op jit(solution)/shard_map/attend/pallas_call | solution.py:186
  89.7 9.7 %collective-permute-start.9 = (bf16[512,1536]{1,0:T(8,128)(2,1)S(1)}, bf16[512,1536]{1,0:T(8,128)(2,1)}, u32[]{:S(2)}, u32[]{:S(2)}) collective-permute-start(bf16[512,1536]{1,0:T(8,128)(2,1)S(1)} %add_convert_fusion.3), channel_id=1, source_target_pairs={{0,2},{2,0},{1,3},{3,1},{4,6},{6,4},{5,7},{7,5},{8,10},{10,8},{9,1... | collective-permute-start | bytes 4718600 | tf_op jit(solution)/shard_map/ppermute | solution.py:755
  99.4 28.4 %attend.5 = (bf16[384,1024]{1,0:T(8,128)(2,1)}, f32[6,1024]{1,0:T(8,128)}, bf16[512,1536]{1,0:T(8,128)(2,1)}, bf16[512,1536]{1,0:T(8,128)(2,1)}) custom-call(s32[9]{0:T(128)} %pad_add_fusion.s_ref.refs_0_, bf16[384,1024]{1,0:T(8,128)(2,1)} %get-tuple-element.118.q_ref.refs_1_, bf16[2,2048,64]{2,1,0:T(8,128)(2,1)} %get-tuple-element.110.k_ref.refs_4_, ...), custom_call_target="tpu_custom_call" | custom-call | flops 2000000000 | bytes 6000000 | tf_op jit(solution)/shard_map/attend/pallas_call | solution.py:186
  127.8 3.1 collective-permute-start.8
  136.9 3.0 collective-permute-start.15
  141.4 19.8 %collective-permute-start.11 = (bf16[512,1536]{1,0:T(8,128)(2,1)}, bf16[512,1536]{1,0:T(8,128)(2,1)}, u32[]{:S(2)}, u32[]{:S(2)}) collective-permute-start(bf16[512,1536]{1,0:T(8,128)(2,1)} %multiply_convert_fusion.refs_1_.refs_0_), channel_id=1, source_target_pairs={{0,1},{1,0},{2,3},{3,2},{4,5},{5,4},{6,7},{7,6},{8,9},{9,8},{10,11... | collective-permute-start | bytes 4718600 | tf_op jit(solution)/shard_map/ppermute | solution.py:754
  166.4 20.0 %experts.4 = (bf16[512,1536]{1,0:T(8,128)(2,1)}, bf16[512,1536]{1,0:T(8,128)(2,1)}, bf16[512,1664]{1,0:T(8,128)(2,1)}, bf16[512,1664]{1,0:T(8,128)(2,1)}, bf16[1...) custom-call(s32[2]{0:T(128)} %pad_add_fusion.2.refs_0_, bf16[512,1536]{1,0:T(8,128)(2,1)} %multiply_convert_fusion.refs_1_.refs_0_, ...), custom_call_target="tpu_custom_call" | custom-call | flops 8000000000 | bytes 24000000 | tf_op jit(solution)/shard_map/experts/pallas_call | solution.py:600
  186.4 11.4 %collective-permute-done.10.refs_1_.refs_2_ = bf16[512,1536]{1,0:T(8,128)(2,1)} collective-permute-done((bf16[512,1536]{1,0:T(8,128)(2,1)}, bf16[512,1536]{1,0:T(8,128)(2,1)}, u32[]{:S(2)}, u32[]{:S(2)}) %collective-permute-start.10) | collective-permute-done | bytes 1572896 | tf_op jit(solution)/shard_map/ppermute | solution.py:758
  201.5 20.0 %experts.5 = (bf16[512,1536]{1,0:T(8,128)(2,1)}, bf16[512,1536]{1,0:T(8,128)(2,1)}, bf16[512,1664]{1,0:T(8,128)(2,1)}, bf16[512,1664]{1,0:T(8,128)(2,1)}, bf16[1...) custom-call(s32[2]{0:T(128)} %pad_add_fusion.2.refs_0_, ...), custom_call_target="tpu_custom_call" | custom-call | flops 8000000000 | bytes 24000000 | tf_op jit(solution)/shard_map/experts/pallas_call | solution.py:600
  221.5 22.3 %experts.6 = (bf16[512,1536]{1,0:T(8,128)(2,1)}, bf16[512,1536]{1,0:T(8,128)(2,1)}, bf16[512,1664]{1,0:T(8,128)(2,1)}, bf16[512,1664]{1,0:T(8,128)(2,1)}, bf16[1...) custom-call(s32[2]{0:T(128)} %pad_add_fusion.1.refs_0_, bf16[512,1536]{1,0:T(8,128)(2,1)} %multiply_convert_fusion.refs_1_.refs_0_, ...), custom_call_target="tpu_custom_call" | custom-call | flops 8000000000 | bytes 24000000 | tf_op jit(solution)/shard_map/experts/pallas_call | solution.py:600
  243.9 22.5 %experts.7 = (bf16[512,1536]{1,0:T(8,128)(2,1)}, bf16[512,1536]{1,0:T(8,128)(2,1)}, bf16[512,1664]{1,0:T(8,128)(2,1)}, bf16[512,1664]{1,0:T(8,128)(2,1)}, bf16[1...) custom-call(s32[2]{0:T(128)} %pad_add_fusion.1.refs_0_, ...), custom_call_target="tpu_custom_call" | custom-call | flops 8000000000 | bytes 24000000 | tf_op jit(solution)/shard_map/experts/pallas_call | solution.py:600
  266.5 3.7 collective-permute-done.17
  270.2 3.1 add_convert_fusion
  273.4 17.7 %expert_grads.2 = bf16[1,1536,1536]{2,1,0:T(8,128)(2,1)} custom-call(bf16[512,1536]{1,0:T(8,128)(2,1)} %multiply_convert_fusion.refs_1_.refs_0_, bf16[512,1536]{1,0:T(8,128)(2,1)} %collective-permute-done.11.refs_2_.refs_1_, bf16[512,1536]{1,0:T(8,128)(2,1)} %collective-permute-done.10.refs_1_.refs_2_, ...), custom_call_target="tpu_custom_call" | custom-call | flops 12000000000 | bytes 36000000 | tf_op jit(solution)/shard_map/expert_grads/pallas_call | solution.py:704
  295.7 4.1 convert_add_fusion.1
  299.8 18.1 %expert_grads.3 = bf16[1,1536,1536]{2,1,0:T(8,128)(2,1)} custom-call(bf16[512,1536]{1,0:T(8,128)(2,1)} %multiply_convert_fusion.refs_1_.refs_0_, bf16[512,1536]{1,0:T(8,128)(2,1)} %collective-permute-done.11.refs_2_.refs_1_, bf16[512,1536]{1,0:T(8,128)(2,1)} %collective-permute-done.10.refs_1_.refs_2_, ...), custom_call_target="tpu_custom_call" | custom-call | flops 12000000000 | bytes 36000000 | tf_op jit(solution)/shard_map/expert_grads/pallas_call | solution.py:704
  317.9 15.8 %collective-permute-done.18 = bf16[512,1664]{1,0:T(8,128)(2,1)} collective-permute-done((bf16[512,1664]{1,0:T(8,128)(2,1)}, bf16[512,1664]{1,0:T(8,128)(2,1)}, u32[]{:S(2)}, u32[]{:S(2)}) %collective-permute-start.18) | collective-permute-done | bytes 1703968 | tf_op jit(solution)/shard_map/ppermute | solution.py:758
  338.8 3.3 fusion.9
  342.5 3.3 collective-permute-done.20.refs_11_.refs_1_
  345.8 36.3 %attend_back.2 = (bf16[384,1024]{1,0:T(8,128)(2,1)}, f32[2,2048,64]{2,1,0:T(8,128)}, f32[2,2048,64]{2,1,0:T(8,128)}) custom-call(s32[9]{0:T(128)} %pad_add_fusion.s_ref.refs_0_, bf16[384,1024]{1,0:T(8,128)(2,1)} %get-tuple-element.118.q_ref.refs_1_, bf16[384,1024]{1,0:T(8,128)(2,1)} %get-tuple-element.152.refs_2_, f32[6,1024]{1,0:T(8,128)} %get-tuple-element.153.refs_3_, ...), custom_call_target="tpu_custom_call" | custom-call | flops 30000001024 | bytes 90000000 | tf_op jit(solution)/shard_map/attend_back/pallas_call | solution.py:329
  385.0 4.9 out_grads.2.refs_3_
  389.8 4.0 add_convert_fusion.2
  395.4 5.4 out_grads.3
  400.8 22.1 %attend_back.3 = (bf16[384,1024]{1,0:T(8,128)(2,1)}, bf16[256,2048]{1,0:T(8,128)(2,1)}) custom-call(s32[9]{0:T(128)} %pad_add_fusion.s_ref.refs_0_, bf16[384,1024]{1,0:T(8,128)(2,1)} %get-tuple-element.167.q_ref.refs_1_, bf16[384,1024]{1,0:T(8,128)(2,1)} %copy-done.19, f32[6,1024]{1,0:T(8,128)} %pad_maximum_fusion.4.refs_3_, ...), custom_call_target="tpu_custom_call" | custom-call | flops 30000001024 | bytes 90000000 | tf_op jit(solution)/shard_map/attend_back/pallas_call | solution.py:329
  422.9 9.8 %qkv_grads.1 = (bf16[1536,640]{1,0:T(8,128)(2,1)}, f32[1,1536]{1,0:T(1,128)}) custom-call(bf16[512,1536]{1,0:T(8,128)(2,1)} %multiply_convert_fusion.1.refs_0_, bf16[512,1536]{1,0:T(8,128)(2,1)} %collective-permute-done.refs_1_, bf16[512,1536]{1,0:T(8,128)(2,1)} %collective-permute-done.2.refs_0_.refs_2_, ...), custom_call_target="tpu_custom_call" | custom-call | flops 10000000000 | bytes 30000000 | tf_op jit(solution)/shard_map/qkv_grads/pallas_call | solution.py:396
  432.7 5.7 input_grads.2
  444.1 12.6 %collective-permute-start.35 = (bf16[192,1536]{1,0:T(8,128)(2,1)}, bf16[192,1536]{1,0:T(8,128)(2,1)}, u32[]{:S(2)}, u32[]{:S(2)}) collective-permute-start(bf16[192,1536]{1,0:T(8,128)(2,1)} %constant_dynamic-slice_fusion.1), channel_id=1, source_target_pairs={{0,2},{2,0},{1,3},{3,1},{4,6},{6,4},{5,7},{7,5},{8,10},{10,8},{9,1... | collective-permute-start | bytes 1769480 | tf_op jit(solution)/shard_map/ppermute | solution.py:755
  460.6 2.9 add_convert_fusion.1
  463.6 8.9 %collective-permute-start.28 = (bf16[512,1536]{1,0:T(8,128)(2,1)}, bf16[512,1536]{1,0:T(8,128)(2,1)}, u32[]{:S(2)}, u32[]{:S(2)}) collective-permute-start(bf16[512,1536]{1,0:T(8,128)(2,1)} %add_convert_fusion.1), channel_id=1, source_target_pairs={{0,2},{2,0},{1,3},{3,1},{4,6},{6,4},{5,7},{7,5},{8,10},{10,8},{9,1... | collective-permute-start | bytes 4718600 | tf_op jit(solution)/shard_map/ppermute | solution.py:755
  472.5 4.9 collective-permute-start.29
  482.1 6.9 %collective-permute-start.30 = (f32[10,1536]{1,0:T(8,128)S(1)}, f32[10,1536]{1,0:T(8,128)S(1)}, u32[]{:S(2)}, u32[]{:S(2)}) collective-permute-start(f32[10,1536]{1,0:T(8,128)S(1)} %add.188), channel_id=1, source_target_pairs={{0,16},{8,24},{16,0},{24,8},{1,17},{9,25},{17,1},{25,9},{2,18},{10... | collective-permute-start | bytes 184328 | tf_op jit(solution)/shard_map/ppermute | solution.py:777
  497.8 5.8 input_grads.3
  504.2 8.4 %collective-permute-start.33 = (f32[10,1536]{1,0:T(8,128)S(1)}, f32[10,1536]{1,0:T(8,128)S(1)}, u32[]{:S(2)}, u32[]{:S(2)}) collective-permute-start(f32[10,1536]{1,0:T(8,128)S(1)} %add.191), channel_id=1, source_target_pairs={{0,2},{2,0},{1,3},{3,1},{4,6},{6,4},{5,7},{7,5},{8,10},{10,8},{9,1... | collective-permute-start | bytes 184328 | tf_op jit(solution)/shard_map/ppermute | solution.py:755
  512.6 8.0 %collective-permute-done.36 = bf16[192,1536]{1,0:T(8,128)(2,1)} collective-permute-done((bf16[192,1536]{1,0:T(8,128)(2,1)}, bf16[192,1536]{1,0:T(8,128)(2,1)}, u32[]{:S(2)}, u32[]{:S(2)}) %collective-permute-start.36) | collective-permute-done | bytes 589856 | tf_op jit(solution)/shard_map/ppermute | solution.py:755
  522.5 3.6 collective-permute-start.37
  526.2 6.5 %collective-permute-start.38 = (bf16[192,1536]{1,0:T(8,128)(2,1)S(1)}, bf16[192,1536]{1,0:T(8,128)(2,1)S(1)}, u32[]{:S(2)}, u32[]{:S(2)}) collective-permute-start(bf16[192,1536]{1,0:T(8,128)(2,1)S(1)} %get-tuple-element.223), channel_id=1, source_target_pairs={{0,0},{1,24},{2,8},{3,16},{8,1},{9,25},{10,9},{11,17},{16,2},{17,2... | collective-permute-start | bytes 1769480 | tf_op jit(solution)/shard_map/ppermute | solution.py:1010
  532.6 4.4 convert_add_fusion.2
  538.2 9.1 %collective-permute-done.37 = bf16[192,1536]{1,0:T(8,128)(2,1)S(1)} collective-permute-done((bf16[192,1536]{1,0:T(8,128)(2,1)S(1)}, bf16[192,1536]{1,0:T(8,128)(2,1)S(1)}, u32[]{:S(2)}, u32[]{:S(2)}) %collective-permute-start.37) | collective-permute-done | bytes 589856 | tf_op jit(solution)/shard_map/ppermute | solution.py:1009
  547.3 12.4 %collective-permute-done.38 = bf16[192,1536]{1,0:T(8,128)(2,1)S(1)} collective-permute-done((bf16[192,1536]{1,0:T(8,128)(2,1)S(1)}, bf16[192,1536]{1,0:T(8,128)(2,1)S(1)}, u32[]{:S(2)}, u32[]{:S(2)}) %collective-permute-start.38) | collective-permute-done | bytes 589856 | tf_op jit(solution)/shard_map/ppermute | solution.py:1010
  564.3 3.1 multiply_reduce_fusion.1
  567.4 4.8 multiply_add_fusion
  (193 shorter events, 90.7 us)
Async XLA Ops:
  7.2 393.6 %reduce-scatter.4.cloned.1.call-start = ((), (), s32[]{:S(2)}) async-start(), calls=%async_computation.3 | async-start | bytes 5898240 | tf_op jit(solution)/shard_map/reduce_scatter | solution.py:928
  11.4 5.5 collective-permute-start
  11.4 37.1 %collective-permute-start.2 = (bf16[512,1536]{1,0:T(8,128)(2,1)}, bf16[512,1536]{1,0:T(8,128)(2,1)}, u32[]{:S(2)}, u32[]{:S(2)}) collective-permute-start(bf16[512,1536]{1,0:T(8,128)(2,1)} %multiply_convert_fusion.1.refs_0_), channel_id=1, source_target_pairs={{0,2},{2,0},{1,3},{3,1},{4,6},{6,4},{5,7},{7,5},{8,10},{10,8},{9,1... | collective-permute-start | bytes 4718600 | tf_op jit(solution)/shard_map/ppermute | solution.py:755
  16.9 56.1 %collective-permute-start.1 = (bf16[1,1536,1536]{2,1,0:T(8,128)(2,1)}, bf16[1,1536,1536]{2,1,0:T(8,128)(2,1)}, u32[]{:S(2)}, u32[]{:S(2)}) collective-permute-start(bf16[1,1536,1536]{2,1,0:T(8,128)(2,1)} %bitcast.4.refs_7_.refs_6_), channel_id=1, source_target_pairs={{0,8},{8,16},{25,17},{17,9},{2,10},{10,18},{27,19},{19,11},{4,12},... | collective-permute-start | bytes 14155784 | tf_op jit(solution)/shard_map/ppermute | solution.py:839
  48.6 3.8 collective-permute-start.3
  49.2 85.4 %collective-permute-start.6 = (bf16[1,1536,1536]{2,1,0:T(8,128)(2,1)}, bf16[1,1536,1536]{2,1,0:T(8,128)(2,1)}, u32[]{:S(2)}, u32[]{:S(2)}) collective-permute-start(bf16[1,1536,1536]{2,1,0:T(8,128)(2,1)} %bitcast.4.refs_7_.refs_6_), channel_id=1, source_target_pairs={{8,0},{17,25},{10,2},{19,27},{12,4},{21,29},{14,6},{23,31}} | collective-permute-start | bytes 14155784 | tf_op jit(solution)/shard_map/ppermute | solution.py:839
  73.0 61.6 %collective-permute-start.4 = (bf16[1,1536,1536]{2,1,0:T(8,128)(2,1)}, bf16[1,1536,1536]{2,1,0:T(8,128)(2,1)}, u32[]{:S(2)}, u32[]{:S(2)}) collective-permute-start(bf16[1,1536,1536]{2,1,0:T(8,128)(2,1)} %collective-permute-done.1.refs_8_.refs_7_), channel_id=1, source_target_pairs={{8,16},{16,24},{17,9},{9,1},{10,18},{18,26},{19,11},{11,3},{12,20}... | collective-permute-start | bytes 14155784 | tf_op jit(solution)/shard_map/ppermute | solution.py:839
  75.9 11.6 %collective-permute-start.7 = (bf16[512,1536]{1,0:T(8,128)(2,1)}, bf16[512,1536]{1,0:T(8,128)(2,1)}, u32[]{:S(2)}, u32[]{:S(2)}) collective-permute-start(bf16[512,1536]{1,0:T(8,128)(2,1)} %get-tuple-element.112), channel_id=1, source_target_pairs={{0,1},{1,0},{2,3},{3,2},{4,5},{5,4},{6,7},{7,6},{8,9},{9,8},{10,11... | collective-permute-start | bytes 4718600 | tf_op jit(solution)/shard_map/ppermute | solution.py:754
  77.6 57.0 %collective-permute-start.5 = (bf16[512,1664]{1,0:T(8,128)(2,1)}, bf16[512,1664]{1,0:T(8,128)(2,1)}, u32[]{:S(2)}, u32[]{:S(2)}) collective-permute-start(bf16[512,1664]{1,0:T(8,128)(2,1)} %pad_maximum_fusion.1.refs_3_.refs_4_), channel_id=1, source_target_pairs={{0,4},{4,0},{1,5},{5,1},{2,6},{6,2},{3,7},{7,3},{8,12},{12,8},{9,1... | collective-permute-start | bytes 5111816 | tf_op jit(solution)/shard_map/ppermute | solution.py:758
  89.7 42.4 %collective-permute-start.9 = (bf16[512,1536]{1,0:T(8,128)(2,1)S(1)}, bf16[512,1536]{1,0:T(8,128)(2,1)}, u32[]{:S(2)}, u32[]{:S(2)}) collective-permute-start(bf16[512,1536]{1,0:T(8,128)(2,1)S(1)} %add_convert_fusion.3), channel_id=1, source_target_pairs={{0,2},{2,0},{1,3},{3,1},{4,6},{6,4},{5,7},{7,5},{8,10},{10,8},{9,1... | collective-permute-start | bytes 4718600 | tf_op jit(solution)/shard_map/ppermute | solution.py:755
  127.8 6.8 %collective-permute-start.8 = (bf16[512,1536]{1,0:T(8,128)(2,1)}, bf16[512,1536]{1,0:T(8,128)(2,1)S(1)}, u32[]{:S(2)}, u32[]{:S(2)}) collective-permute-start(bf16[512,1536]{1,0:T(8,128)(2,1)} %get-tuple-element.120), channel_id=1, source_target_pairs={{0,1},{1,0},{2,3},{3,2},{4,5},{5,4},{6,7},{7,6},{8,9},{9,8},{10,11... | collective-permute-start | bytes 4718600 | tf_op jit(solution)/shard_map/ppermute | solution.py:754
  132.1 34.3 %collective-permute-start.12 = (bf16[512,1664]{1,0:T(8,128)(2,1)}, bf16[512,1664]{1,0:T(8,128)(2,1)}, u32[]{:S(2)}, u32[]{:S(2)}) collective-permute-start(bf16[512,1664]{1,0:T(8,128)(2,1)} %pad_maximum_fusion.1.refs_3_.refs_4_), channel_id=1, source_target_pairs={{0,1},{1,0},{2,3},{3,2},{4,5},{5,4},{6,7},{7,6},{8,9},{9,8},{10,11... | collective-permute-start | bytes 5111816 | tf_op jit(solution)/shard_map/ppermute | solution.py:754
  136.9 84.6 %collective-permute-start.15 = (bf16[1,1536,1536]{2,1,0:T(8,128)(2,1)}, bf16[1,1536,1536]{2,1,0:T(8,128)(2,1)}, u32[]{:S(2)}, u32[]{:S(2)}) collective-permute-start(bf16[1,1536,1536]{2,1,0:T(8,128)(2,1)} %collective-permute-done.4.refs_9_.refs_8_), channel_id=1, source_target_pairs={{16,24},{9,1},{18,26},{11,3},{20,28},{13,5},{22,30},{15,7}} | collective-permute-start | bytes 14155784 | tf_op jit(solution)/shard_map/ppermute | solution.py:839
  141.4 25.0 %collective-permute-start.11 = (bf16[512,1536]{1,0:T(8,128)(2,1)}, bf16[512,1536]{1,0:T(8,128)(2,1)}, u32[]{:S(2)}, u32[]{:S(2)}) collective-permute-start(bf16[512,1536]{1,0:T(8,128)(2,1)} %multiply_convert_fusion.refs_1_.refs_0_), channel_id=1, source_target_pairs={{0,1},{1,0},{2,3},{3,2},{4,5},{5,4},{6,7},{7,6},{8,9},{9,8},{10,11... | collective-permute-start | bytes 4718600 | tf_op jit(solution)/shard_map/ppermute | solution.py:754
  161.2 36.6 %collective-permute-start.10 = (bf16[512,1536]{1,0:T(8,128)(2,1)}, bf16[512,1536]{1,0:T(8,128)(2,1)}, u32[]{:S(2)}, u32[]{:S(2)}) collective-permute-start(bf16[512,1536]{1,0:T(8,128)(2,1)} %multiply_convert_fusion.refs_1_.refs_0_), channel_id=1, source_target_pairs={{0,4},{4,0},{1,5},{5,1},{2,6},{6,2},{3,7},{7,3},{8,12},{12,8},{9,1... | collective-permute-start | bytes 4718600 | tf_op jit(solution)/shard_map/ppermute | solution.py:758
  166.3 32.7 %collective-permute-start.14 = (bf16[512,1664]{1,0:T(8,128)(2,1)}, bf16[512,1664]{1,0:T(8,128)(2,1)}, u32[]{:S(2)}, u32[]{:S(2)}) collective-permute-start(bf16[512,1664]{1,0:T(8,128)(2,1)} %collective-permute-done.5.refs_3_.refs_6_), channel_id=1, source_target_pairs={{0,1},{1,0},{2,3},{3,2},{4,5},{5,4},{6,7},{7,6},{8,9},{9,8},{10,11... | collective-permute-start | bytes 5111816 | tf_op jit(solution)/shard_map/ppermute | solution.py:754
  197.8 3.8 collective-permute-start.13
  266.4 3.9 collective-permute-start.17
  291.1 181.4 %reduce-scatter.8.cloned.1.call-start = ((), (), s32[]{:S(2)}) async-start(), calls=%async_computation.5 | async-start | bytes 5898240 | tf_op jit(solution)/shard_map/reduce_scatter | solution.py:928
  291.2 4.5 collective-permute-start.16
  294.1 39.6 %collective-permute-start.18 = (bf16[512,1664]{1,0:T(8,128)(2,1)}, bf16[512,1664]{1,0:T(8,128)(2,1)}, u32[]{:S(2)}, u32[]{:S(2)}) collective-permute-start(bf16[512,1664]{1,0:T(8,128)(2,1)} %add_convert_fusion), channel_id=1, source_target_pairs={{0,4},{4,0},{1,5},{5,1},{2,6},{6,2},{3,7},{7,3},{8,12},{12,8},{9,1... | collective-permute-start | bytes 5111816 | tf_op jit(solution)/shard_map/ppermute | solution.py:758
  342.0 3.8 collective-permute-start.20
  342.1 230.2 %reduce-scatter.6.cloned.1.call-start = ((), (), s32[]{:S(2)}) async-start(), calls=%async_computation.4 | async-start | bytes 1966080 | tf_op jit(solution)/shard_map/reduce_scatter | solution.py:987
  342.1 40.1 %collective-permute-start.19 = (bf16[512,1536]{1,0:T(8,128)(2,1)}, bf16[512,1536]{1,0:T(8,128)(2,1)}, u32[]{:S(2)}, u32[]{:S(2)}) collective-permute-start(bf16[512,1536]{1,0:T(8,128)(2,1)} %get-tuple-element.160.refs_10_.refs_0_), channel_id=1, source_target_pairs={{0,2},{2,0},{1,3},{3,1},{4,6},{6,4},{5,7},{7,5},{8,10},{10,8},{9,1... | collective-permute-start | bytes 4718600 | tf_op jit(solution)/shard_map/ppermute | solution.py:755
  345.8 36.8 %copy-start.20 = (f32[1536]{0:T(1024)S(1)}, f32[1536]{0:T(1024)}, u32[]{:S(2)}) copy-start(f32[1536]{0:T(1024)} %param.16) | copy-start | bytes 18436
  345.8 37.4 %copy-start.16 = (bf16[384,512]{1,0:T(8,128)(2,1)S(1)}, bf16[384,512]{1,0:T(8,128)(2,1)}, u32[]{:S(2)}) copy-start(bf16[384,512]{1,0:T(8,128)(2,1)} %get-tuple-element.158) | copy-start | bytes 1179652
  345.8 37.6 %copy-start.24 = (f32[6,512]{1,0:T(8,128)S(1)}, f32[6,512]{1,0:T(8,128)}, u32[]{:S(2)}) copy-start(f32[6,512]{1,0:T(8,128)} %get-tuple-element.169) | copy-start | bytes 36868
  345.8 37.6 %copy-start.25 = (f32[6,512]{1,0:T(8,128)S(1)}, f32[6,512]{1,0:T(8,128)}, u32[]{:S(2)}) copy-start(f32[6,512]{1,0:T(8,128)} %get-tuple-element.168) | copy-start | bytes 36868
  345.8 38.2 %copy-start.15 = (bf16[384,512]{1,0:T(8,128)(2,1)S(1)}, bf16[384,512]{1,0:T(8,128)(2,1)}, u32[]{:S(2)}) copy-start(bf16[384,512]{1,0:T(8,128)(2,1)} %get-tuple-element.159) | copy-start | bytes 1179652
  382.1 7.7 %collective-permute-start.22 = (bf16[512,1536]{1,0:T(8,128)(2,1)}, bf16[512,1536]{1,0:T(8,128)(2,1)}, u32[]{:S(2)}, u32[]{:S(2)}) collective-permute-start(bf16[512,1536]{1,0:T(8,128)(2,1)} %get-tuple-element.164), channel_id=1, source_target_pairs={{0,1},{1,0},{2,3},{3,2},{4,5},{5,4},{6,7},{7,6},{8,9},{9,8},{10,11... | collective-permute-start | bytes 4718600 | tf_op jit(solution)/shard_map/ppermute | solution.py:754
  382.2 13.2 %collective-permute-start.21 = (bf16[512,1536]{1,0:T(8,128)(2,1)}, bf16[512,1536]{1,0:T(8,128)(2,1)}, u32[]{:S(2)}, u32[]{:S(2)}) collective-permute-start(bf16[512,1536]{1,0:T(8,128)(2,1)} %collective-permute-done.19.refs_0_.refs_10_), channel_id=1, source_target_pairs={{0,1},{1,0},{2,3},{3,2},{4,5},{5,4},{6,7},{7,6},{8,9},{9,8},{10,11... | collective-permute-start | bytes 4718600 | tf_op jit(solution)/shard_map/ppermute | solution.py:754
  383.3 17.5 %collective-permute-start.23 = (bf16[512,1536]{1,0:T(8,128)(2,1)}, bf16[512,1536]{1,0:T(8,128)(2,1)}, u32[]{:S(2)}, u32[]{:S(2)}) collective-permute-start(bf16[512,1536]{1,0:T(8,128)(2,1)} %get-tuple-element.166), channel_id=1, source_target_pairs={{0,1},{1,0},{2,3},{3,2},{4,5},{5,4},{6,7},{7,6},{8,9},{9,8},{10,11... | collective-permute-start | bytes 4718600 | tf_op jit(solution)/shard_map/ppermute | solution.py:754
  393.9 65.8 %collective-permute-start.25 = (bf16[512,1536]{1,0:T(8,128)(2,1)}, bf16[512,1536]{1,0:T(8,128)(2,1)}, u32[]{:S(2)}, u32[]{:S(2)}) collective-permute-start(bf16[512,1536]{1,0:T(8,128)(2,1)} %add_convert_fusion.2), channel_id=1, source_target_pairs={{0,4},{4,0},{1,5},{5,1},{2,6},{6,2},{3,7},{7,3},{8,12},{12,8},{9,1... | collective-permute-start | bytes 4718600 | tf_op jit(solution)/shard_map/ppermute | solution.py:758
  438.4 22.2 %collective-permute-start.24 = (bf16[512,1536]{1,0:T(8,128)(2,1)}, bf16[512,1536]{1,0:T(8,128)(2,1)}, u32[]{:S(2)}, u32[]{:S(2)}) collective-permute-start(bf16[512,1536]{1,0:T(8,128)(2,1)} %get-tuple-element.177), channel_id=1, source_target_pairs={{0,1},{1,0},{2,3},{3,2},{4,5},{5,4},{6,7},{7,6},{8,9},{9,8},{10,11... | collective-permute-start | bytes 4718600 | tf_op jit(solution)/shard_map/ppermute | solution.py:754
  439.8 19.8 %collective-permute-start.34 = (bf16[4,192,384]{2,1,0:T(8,128)(2,1)S(1)}, bf16[4,192,384]{2,1,0:T(8,128)(2,1)S(1)}, u32[]{:S(2)}, u32[]{:S(2)}) collective-permute-start(bf16[4,192,384]{2,1,0:T(8,128)(2,1)S(1)} %dynamic-slice_bitcast_fusion.2), channel_id=1, source_target_pairs={{0,4},{4,0},{1,5},{5,1},{2,6},{6,2},{3,7},{7,3},{8,12},{12,8},{9,1... | collective-permute-start | bytes 1769480 | tf_op jit(solution)/shard_map/ppermute | solution.py:758
  444.1 52.1 %collective-permute-start.35 = (bf16[192,1536]{1,0:T(8,128)(2,1)}, bf16[192,1536]{1,0:T(8,128)(2,1)}, u32[]{:S(2)}, u32[]{:S(2)}) collective-permute-start(bf16[192,1536]{1,0:T(8,128)(2,1)} %constant_dynamic-slice_fusion.1), channel_id=1, source_target_pairs={{0,2},{2,0},{1,3},{3,1},{4,6},{6,4},{5,7},{7,5},{8,10},{10,8},{9,1... | collective-permute-start | bytes 1769480 | tf_op jit(solution)/shard_map/ppermute | solution.py:755
  458.1 23.9 %collective-permute-start.26 = (bf16[4,192,640]{2,1,0:T(8,128)(2,1)}, bf16[4,192,640]{2,1,0:T(8,128)(2,1)}, u32[]{:S(2)}, u32[]{:S(2)}) collective-permute-start(bf16[4,192,640]{2,1,0:T(8,128)(2,1)} %get-tuple-element.228), channel_id=1, source_target_pairs={{0,4},{4,0},{1,5},{5,1},{2,6},{6,2},{3,7},{7,3},{8,12},{12,8},{9,1... | collective-permute-start | bytes 2949128 | tf_op jit(solution)/shard_map/ppermute | solution.py:758
  463.6 100.7 %collective-permute-start.28 = (bf16[512,1536]{1,0:T(8,128)(2,1)}, bf16[512,1536]{1,0:T(8,128)(2,1)}, u32[]{:S(2)}, u32[]{:S(2)}) collective-permute-start(bf16[512,1536]{1,0:T(8,128)(2,1)} %add_convert_fusion.1), channel_id=1, source_target_pairs={{0,2},{2,0},{1,3},{3,1},{4,6},{6,4},{5,7},{7,5},{8,10},{10,8},{9,1... | collective-permute-start | bytes 4718600 | tf_op jit(solution)/shard_map/ppermute | solution.py:755
  472.5 9.5 %collective-permute-start.29 = (f32[10,1536]{1,0:T(8,128)S(1)}, f32[10,1536]{1,0:T(8,128)S(1)}, u32[]{:S(2)}, u32[]{:S(2)}) collective-permute-start(f32[10,1536]{1,0:T(8,128)S(1)} %pad_maximum_fusion.3), channel_id=1, source_target_pairs={{0,8},{8,0},{16,24},{24,16},{1,9},{9,1},{17,25},{25,17},{2,10},{10... | collective-permute-start | bytes 184328 | tf_op jit(solution)/shard_map/ppermute | solution.py:777
  479.3 41.3 %collective-permute-start.36 = (bf16[192,1536]{1,0:T(8,128)(2,1)}, bf16[192,1536]{1,0:T(8,128)(2,1)}, u32[]{:S(2)}, u32[]{:S(2)}) collective-permute-start(bf16[192,1536]{1,0:T(8,128)(2,1)} %constant_dynamic-slice_fusion), channel_id=1, source_target_pairs={{0,2},{2,0},{1,3},{3,1},{4,6},{6,4},{5,7},{7,5},{8,10},{10,8},{9,1... | collective-permute-start | bytes 1769480 | tf_op jit(solution)/shard_map/ppermute | solution.py:755
  482.1 11.0 %collective-permute-start.30 = (f32[10,1536]{1,0:T(8,128)S(1)}, f32[10,1536]{1,0:T(8,128)S(1)}, u32[]{:S(2)}, u32[]{:S(2)}) collective-permute-start(f32[10,1536]{1,0:T(8,128)S(1)} %add.188), channel_id=1, source_target_pairs={{0,16},{8,24},{16,0},{24,8},{1,17},{9,25},{17,1},{25,9},{2,18},{10... | collective-permute-start | bytes 184328 | tf_op jit(solution)/shard_map/ppermute | solution.py:777
  493.1 4.7 collective-permute-start.31
  497.8 6.4 %collective-permute-start.32 = (f32[10,1536]{1,0:T(8,128)S(1)}, f32[10,1536]{1,0:T(8,128)S(1)}, u32[]{:S(2)}, u32[]{:S(2)}) collective-permute-start(f32[10,1536]{1,0:T(8,128)S(1)} %add.190), channel_id=1, source_target_pairs={{0,1},{1,0},{2,3},{3,2},{4,5},{5,4},{6,7},{7,6},{8,9},{9,8},{10,11... | collective-permute-start | bytes 184328 | tf_op jit(solution)/shard_map/ppermute | solution.py:754
  503.6 29.0 %copy-start.11 = (bf16[512,1536]{1,0:T(8,128)(2,1)S(1)}, bf16[512,1536]{1,0:T(8,128)(2,1)}, u32[]{:S(2)}) copy-start(bf16[512,1536]{1,0:T(8,128)(2,1)} %get-tuple-element.179) | copy-start | bytes 4718596
  503.6 60.6 %collective-permute-start.27 = (bf16[512,1536]{1,0:T(8,128)(2,1)}, bf16[512,1536]{1,0:T(8,128)(2,1)}, u32[]{:S(2)}, u32[]{:S(2)}) collective-permute-start(bf16[512,1536]{1,0:T(8,128)(2,1)} %get-tuple-element.184), channel_id=1, source_target_pairs={{0,1},{1,0},{2,3},{3,2},{4,5},{5,4},{6,7},{7,6},{8,9},{9,8},{10,11... | collective-permute-start | bytes 4718600 | tf_op jit(solution)/shard_map/ppermute | solution.py:754
  504.2 32.9 %collective-permute-start.33 = (f32[10,1536]{1,0:T(8,128)S(1)}, f32[10,1536]{1,0:T(8,128)S(1)}, u32[]{:S(2)}, u32[]{:S(2)}) collective-permute-start(f32[10,1536]{1,0:T(8,128)S(1)} %add.191), channel_id=1, source_target_pairs={{0,2},{2,0},{1,3},{3,1},{4,6},{6,4},{5,7},{7,5},{8,10},{10,8},{9,1... | collective-permute-start | bytes 184328 | tf_op jit(solution)/shard_map/ppermute | solution.py:755
  522.5 24.8 %collective-permute-start.37 = (bf16[192,1536]{1,0:T(8,128)(2,1)S(1)}, bf16[192,1536]{1,0:T(8,128)(2,1)S(1)}, u32[]{:S(2)}, u32[]{:S(2)}) collective-permute-start(bf16[192,1536]{1,0:T(8,128)(2,1)S(1)} %get-tuple-element.222), channel_id=1, source_target_pairs={{0,8},{1,16},{2,0},{3,24},{8,9},{9,17},{10,1},{11,25},{16,10},{17,... | collective-permute-start | bytes 1769480 | tf_op jit(solution)/shard_map/ppermute | solution.py:1009
  526.2 33.6 %collective-permute-start.38 = (bf16[192,1536]{1,0:T(8,128)(2,1)S(1)}, bf16[192,1536]{1,0:T(8,128)(2,1)S(1)}, u32[]{:S(2)}, u32[]{:S(2)}) collective-permute-start(bf16[192,1536]{1,0:T(8,128)(2,1)S(1)} %get-tuple-element.223), channel_id=1, source_target_pairs={{0,0},{1,24},{2,8},{3,16},{8,1},{9,25},{10,9},{11,17},{16,2},{17,2... | collective-permute-start | bytes 1769480 | tf_op jit(solution)/shard_map/ppermute | solution.py:1010
  (24 other events, 219.5 us)
Sparse Core Ops, SparseCore 0:
  291.2 89.8 reduce-scatter.3
  383.5 85.7 reduce-scatter.7
  496.3 42.7 reduce-scatter.5
